TPU v7x, 512 devices: a whole 4x8x8 slice. The times are simulated.
512 devices in a mesh: span: 4 (over x), seq: 32 (over z_hi, y, core), head: 4 (over z_lo).
Axes of the slice: x: 4, y: 8, z: 8 (z_hi: 2, z_lo: 4; z = z_hi * 4 + z_lo), core: 2. Of those that a mesh axis runs over, the one named last changes fastest.
Arguments:
- query_proj: bfloat16 [4, 1280, 3072], P('span', 'seq', 'head'), may hold values from -12 to 12
- key_proj: bfloat16 [4, 1280, 3072], P('span', 'seq', 'head'), may hold values from -12 to 12
- value_proj: bfloat16 [4, 1280, 3072], P('span', 'seq', 'head'), may hold values from -24 to 24
- block_order: int32 [4], replicated, may hold values from 0 to 3, each once
- valid_frames: int32 [4], replicated, may hold values from 1 to 8, as said below
- noise_steps: int32 [4], replicated, may hold values from 0 to 3
- gate_table: float32 [4, 6144], P(None, 'seq'), may hold values from 1 to 10
- out_weight: bfloat16 [3072, 6144], P('head', 'seq'), may hold values from -0.109375 to 0.109375
- residual: bfloat16 [4, 1280, 6144], P('span', 'head', 'seq'), may hold values from -3 to 3
Outputs:
- mixed: bfloat16 [4, 1280, 6144], P('span', 'head', 'seq')
Inputs may be any that keep to these rules, and one draw needn't show every extreme that they name: `valid_frames`: some block has all 8 frames open.
All inputs are finite; a program needn't handle non-finite values.
Results may differ from a plain program's by a relative error of at most 0.017.
Values may be sent and summed in bfloat16 or wider, within the bound.
No kernel may reach another device: no remote copies, remote signals or barrier semaphores. Data moves between devices by JAX's collectives and lax.ppermute only.
A program may use at most 128 MiB of HBM per device.

v0:
```python
import jax
import jax.numpy as jnp
from jax import lax
from jax.sharding import PartitionSpec as P

HD = 128
FRAMES = 8


floor_score = -1e30


def lookup(entries, picked):
    slots = jnp.arange(entries.shape[0], dtype=jnp.int32)
    return jnp.sum(jnp.where(slots[None, :] == picked[:, None], entries[None, :], 0), axis=1)


def attend(carry_state, queries, keys_piece, values_piece, visible):
    running_max, denominator, summed = carry_state
    score_scale = 1.0 / queries.shape[-1] ** 0.5
    scores = (
        jnp.einsum("qhe,khe->hqk", queries, keys_piece, preferred_element_type=jnp.float32)
        * score_scale
    )
    scores = jnp.where(visible[None, None, :], scores, floor_score)
    new_max = jnp.maximum(running_max, jnp.max(scores, axis=2))
    weights = jnp.where(visible[None, None, :], jnp.exp(scores - new_max[:, :, None]), 0.0)
    denominator = jnp.sum(weights, axis=2)
    summed = jnp.einsum(
        "hqk,khe->hqe",
        weights.astype(jnp.bfloat16),
        values_piece,
        preferred_element_type=jnp.float32,
    )
    return (new_max, denominator, summed)


def attend_some(carry_state, queries, keys_piece, values_piece, visible):
    return attend(carry_state, queries, keys_piece, values_piece, visible)


def shards(
    query_proj,
    key_proj,
    value_proj,
    block_order,
    valid_frames,
    noise_steps,
    gate_table,
    out_weight,
    residual,
):
    head_dim = HD
    tokens_here = query_proj.shape[1]
    block_len = tokens_here * lax.axis_size("seq")
    frame_len = block_len // FRAMES
    heads_here = query_proj.shape[2] // head_dim
    block_here = lax.axis_index("span")
    order_here = lookup(block_order, jnp.full((1,), block_here, jnp.int32))[0]
    queries = query_proj[0].reshape(tokens_here, heads_here, head_dim)
    start_state = (
        jnp.full((heads_here, tokens_here), floor_score, jnp.float32),
        jnp.zeros((heads_here, tokens_here), jnp.float32),
        jnp.zeros((heads_here, tokens_here, head_dim), jnp.float32),
    )
    keys_piece = lax.all_gather(key_proj, ("span", "seq"), axis=1, tiled=True)
    values_piece = lax.all_gather(value_proj, ("span", "seq"), axis=1, tiled=True)
    count_rows = keys_piece.shape[1]
    positions = jnp.arange(count_rows, dtype=jnp.int32)
    owners = positions // block_len
    frame_index = positions % block_len // frame_len
    visible = (lookup(block_order, owners) <= order_here) & (
        frame_index < lookup(valid_frames, owners)
    )
    final_state = attend_some(
        start_state,
        queries,
        keys_piece[0].reshape(count_rows, heads_here, head_dim),
        values_piece[0].reshape(count_rows, heads_here, head_dim),
        visible,
    )
    running_max, denominator, summed = final_state
    attended = (
        (summed / denominator[:, :, None])
        .transpose(1, 0, 2)
        .reshape(tokens_here, heads_here * head_dim)
        .astype(jnp.bfloat16)
    )
    partial_sums = jnp.dot(
        lax.all_gather(attended, "seq", axis=0, tiled=True),
        out_weight,
        preferred_element_type=jnp.float32,
    )
    head_total = lax.psum_scatter(
        partial_sums.astype(jnp.bfloat16), "head", scatter_dimension=0, tiled=True
    ).astype(jnp.float32)
    step_here = lookup(noise_steps, jnp.full((1,), block_here, jnp.int32))[0]
    step_slots = jnp.arange(gate_table.shape[0], dtype=jnp.int32)
    gate_row = jnp.sum(jnp.where((step_slots == step_here)[:, None], gate_table, 0.0), axis=0)
    mixed = (residual[0].astype(jnp.float32) + gate_row[None, :] * head_total).astype(jnp.bfloat16)
    return mixed[None]


def solution(mesh):
    placed = (
        P("span", "seq", "head"),
        P("span", "seq", "head"),
        P("span", "seq", "head"),
        P(),
        P(),
        P(),
        P(None, "seq"),
        P("head", "seq"),
        P("span", "head", "seq"),
    )
    return jax.shard_map(
        shards, mesh=mesh, in_specs=placed, out_specs=P("span", "head", "seq"), check_vma=False
    )
```

profile of v0, /device:TPU:1, one launch (start us, length us, event | category | flops | bytes accessed | tf_op | source)
XLA Modules:
  0.0 467.0 jit_solution(13273609546740067536)
XLA Ops:
  6.5 0.0 copy-start
  6.5 0.0 all-gather.4.cloned.1.call-start
  6.5 0.7 all-gather.4.cloned.1.call-update
  7.3 0.0 all-gather.6.cloned.1.call-start
  7.3 0.7 all-gather.6.cloned.1.call-update
  8.0 0.0 all-gather.8.cloned.1.call-start
  8.1 0.9 reshape_squeeze.9
  9.0 1.3 fusion.38
  10.3 0.8 select_reduce_fusion
  11.1 0.7 compare_and_fusion
  11.8 161.9 %all-gather.4.cloned.1.call-done = bf16[1,5120,768]{2,1,0:T(8,128)(2,1)} async-done(((bf16[1,40,768]{2,1,0:T(8,128)(2,1)}), bf16[1,5120,768]{2,1,0:T(8,128)(2,1)}) %all-gather.4.cloned.1.call-update) | async-done | bytes 7864336 | tf_op jit(solution)/shard_map/all_gather | solution.py:66
  173.7 10.7 %copy.23 = bf16[1,5120,768]{1,2,0:T(8,128)(2,1)} copy(bf16[1,5120,768]{2,1,0:T(8,128)(2,1)} %all-gather.4.cloned.1.call-done) | data formatting | bytes 15728640 | tf_op jit(solution)/shard_map/all_gather | solution.py:66
  184.5 4.8 %fusion.40 = (f32[6,40]{1,0:T(8,128)S(1)}, f32[6,40,5120]{2,1,0:T(8,128)S(1)}) fusion(bf16[5120,6,128]{0,2,1:T(8,128)(2,1)} %bitcast.27, bf16[40,6,128]{2,1,0:T(8,128)(2,1)S(1)} %reshape_squeeze.9, pred[5120]{0:T(1024)(128)(4,1)S(1)} %compare_and_fusion), kind=kOutput, calls=%fused_computation.50 | convolution fusion | flops 318258944 | bytes 12847040 | tf_op jit(solution)/shard_map/qhe,khe->hqk/dot_general | solution.py:22
  189.3 0.0 copy-start.1
  189.3 2.2 copy-done.1
  191.5 1.1 fusion.1
  192.5 135.4 %all-gather.6.cloned.1.call-done = bf16[1,5120,768]{2,1,0:T(8,128)(2,1)} async-done(((bf16[1,40,768]{2,1,0:T(8,128)(2,1)}), bf16[1,5120,768]{2,1,0:T(8,128)(2,1)}) %all-gather.6.cloned.1.call-update) | async-done | bytes 7864336 | tf_op jit(solution)/shard_map/all_gather | solution.py:67
  327.9 10.4 %copy.26 = bf16[1,5120,768]{1,2,0:T(8,128)(2,1)} copy(bf16[1,5120,768]{2,1,0:T(8,128)(2,1)} %all-gather.6.cloned.1.call-done) | data formatting | bytes 15728640 | tf_op jit(solution)/shard_map/all_gather | solution.py:67
  338.4 0.0 copy-start.4
  338.4 0.0 copy-start.3
  338.4 7.7 %fusion.17 = bf16[6,5,8,128]{3,2,1,0:T(8,128)(2,1)S(1)} fusion(bf16[5120,6,128]{0,2,1:T(8,128)(2,1)} %bitcast.26, f32[6,40,5120]{2,1,0:T(8,128)} %copy-done.1, f32[6,40]{1,0:T(8,128)S(1)} %broadcast_maximum_fusion, pred[5120]{0:T(1024)(128)(4,1)S(1)} %compare_and_fusion, f32[40,6]{0,1:T(8,128)S(1)} %bitcast.29), kind=kOutput, calls=%fused_computation.13 | convolution fusion | flops 318320640 | bytes 12848000 | tf_op jit(solution)/shard_map/hqk,khe->hqe/dot_general | solution.py:29
  346.0 0.0 copy-start.2
  346.0 0.6 copy.39
  346.7 0.0 all-gather.8.cloned.1.call-update
  346.7 0.0 reduce-scatter.4.cloned.1.call-start
  346.7 87.2 %all-gather.8.cloned.1.call-done = bf16[1280,768]{1,0:T(8,128)(2,1)} async-done(((bf16[40,768]{1,0:T(8,128)(2,1)}), bf16[1280,768]{1,0:T(8,128)(2,1)}) %all-gather.8.cloned.1.call-update) | async-done | bytes 1966096 | tf_op jit(solution)/shard_map/all_gather | solution.py:90
  434.0 0.0 copy-done
  434.0 2.3 convolution_convert_fusion
  436.3 1.1 copy.31
  437.4 0.0 reduce-scatter.4.cloned.1.call-update
  437.4 0.0 copy-done.4
  437.4 0.6 fusion.37
  438.1 0.6 iota_compare_fusion.1
  438.7 0.0 copy-done.3
  438.7 0.1 select_reduce_fusion.2
  438.8 19.8 %reduce-scatter.4.cloned.1.call-done = bf16[320,192]{1,0:T(8,128)(2,1)} async-done(((bf16[1280,192]{1,0:T(8,128)(2,1)}), bf16[320,192]{1,0:T(8,128)(2,1)}) %reduce-scatter.4.cloned.1.call-update) | async-done | bytes 122896
  458.6 1.1 copy.32
  459.6 0.0 copy-done.2
  459.6 0.8 fusion.21
  (2 shorter events, 0.0 us)
Async XLA Ops:
  6.5 427.4 %copy-start = (bf16[768,192]{0,1:T(8,128)(2,1)S(1)}, bf16[768,192]{0,1:T(8,128)(2,1)}, u32[]{:S(2)}) copy-start(bf16[768,192]{0,1:T(8,128)(2,1)} %param.16) | copy-start | bytes 884740
  6.5 167.2 %all-gather.4.cloned.1.call-start = ((), (), s32[]{:S(2)}) async-start(), calls=%async_computation.1 | async-start | bytes 7925760 | tf_op jit(solution)/shard_map/all_gather | solution.py:66
  7.3 320.7 %all-gather.6.cloned.1.call-start = ((), (), s32[]{:S(2)}) async-start(), calls=%async_computation.2 | async-start | bytes 7925760 | tf_op jit(solution)/shard_map/all_gather | solution.py:67
  8.0 425.9 %all-gather.8.cloned.1.call-start = ((), (), s32[]{:S(2)}) async-start(), calls=%async_computation.3 | async-start | bytes 2027520 | tf_op jit(solution)/shard_map/all_gather | solution.py:90
  189.3 2.2 copy-start.1
  338.4 99.1 %copy-start.4 = (s32[4]{0:T(128)S(1)}, s32[4]{0:T(128)}, u32[]{:S(2)}) copy-start(s32[4]{0:T(128)} %param.14) | copy-start | bytes 52
  338.4 100.4 %copy-start.3 = (f32[4,192]{1,0:T(4,128)S(1)}, f32[4,192]{1,0:T(4,128)}, u32[]{:S(2)}) copy-start(f32[4,192]{1,0:T(4,128)} %param.15) | copy-start | bytes 9220
  346.0 113.6 %copy-start.2 = (bf16[1,320,192]{1,2,0:T(8,128)(2,1)S(1)}, bf16[1,320,192]{1,2,0:T(8,128)(2,1)}, u32[]{:S(2)}) copy-start(bf16[1,320,192]{1,2,0:T(8,128)(2,1)} %param.17) | copy-start | bytes 368644
  346.7 111.9 %reduce-scatter.4.cloned.1.call-start = ((), (), s32[]{:S(2)}) async-start(), calls=%async_computation.4 | async-start | bytes 819200
Sparse Core Ops, SparseCore 0:
  12.0 161.7 all-gather.3
  178.4 149.5 all-gather.5
  346.8 87.0 all-gather.7
  437.5 20.9 reduce-scatter.3
where the time goes:
time: 469 us; the launch traced here: 467 us
  waiting for transfers between devices  406 us (87%)
  local copies, waits for them, and re-layouts  27 us (6%)
  matrix products  14.8 us (3%)
  between operations  13.2 us (3%)
  other arithmetic  6.04 us (1%)
    all_gather x1, waiting for transfers between devices, shards(): keys_piece = lax.all_gather(key_proj, ('span', 'seq'), axis=1, tiled=True)  162 us
    all_gather x1, waiting for transfers between devices, shards(): lax.all_gather(value_proj, ('span', 'seq'), axis=1, tiled=True)  135 us
    all_gather x1, waiting for transfers between devices, shards(): lax.all_gather(attended, 'seq', axis=0, tiled=True)  87.2 us
    unnamed x5, waiting for transfers between devices  21.2 us
    all_gather x1, local copies, waits for them, and re-layouts, shards(): keys_piece = lax.all_gather(key_proj, ('span', 'seq'), axis=1, tiled=True)  10.7 us
    all_gather x1, local copies, waits for them, and re-layouts, shards(): lax.all_gather(value_proj, ('span', 'seq'), axis=1, tiled=True)  10.4 us
  transfers between devices with their start and end apart: 4, of which 4 were waited for; matrix products, arithmetic and copies ran while one was open for 5% of the time, Pallas kernels for 0%

commit v1 on v0

v1 whole, which is shorter than its diff:
```python
import jax
import jax.numpy as jnp
from jax import lax
from jax.experimental import pallas as pl
from jax.experimental.pallas import tpu as pltpu
from jax.sharding import Mesh, PartitionSpec as P

HD = 128
FRAMES = 8
CLOSED = -1e30
LOWEST = -1e20
AXES = ("span", "zh", "y", "core", "head")


def attend_kernel(order_ref, valid_ref, q_ref, near_ref, far_ref, out_ref):
    spans = order_ref.shape[0]
    width = q_ref.shape[1]
    heads = width // HD
    rows = q_ref.shape[0]
    slab = near_ref.shape[0] // (2 * spans)
    part = slab // 2
    span = lax.axis_index("span")
    zh = lax.axis_index("zh")
    y = lax.axis_index("y")
    order_here = order_ref[span]
    keys = 2 * spans * slab
    place = lax.broadcasted_iota(jnp.int32, (1, keys), 1)
    place = jnp.where(place >= spans * slab, place - spans * slab, place)
    bias = jnp.zeros((1, keys), jnp.float32)
    frames_half = FRAMES // 2
    for block in range(spans):
        for turn in range(2):
            frame = (zh ^ turn) * frames_half + y // (8 // frames_half)
            is_open = (order_ref[block] <= order_here) & (frame < valid_ref[block])
            least = block * slab + turn * part
            inside = (place >= least) & (place < least + part)
            bias = jnp.where(inside & jnp.logical_not(is_open), CLOSED, bias)
    lane = lax.broadcasted_iota(jnp.int32, (rows, HD), 1)
    stats = jnp.zeros((rows, HD), jnp.float32)
    scale = 1.0 / HD**0.5
    for h in range(heads):
        cols = slice(h * HD, (h + 1) * HD)
        k = jnp.concatenate(
            [ref[2 * b * slab : (2 * b + 1) * slab, cols] for ref in (near_ref, far_ref) for b in range(spans)]
        )
        v = jnp.concatenate(
            [ref[(2 * b + 1) * slab : (2 * b + 2) * slab, cols] for ref in (near_ref, far_ref) for b in range(spans)]
        )
        s = lax.dot_general(q_ref[:, cols], k, (((1,), (1,)), ((), ())), preferred_element_type=jnp.float32)
        s = s * scale + bias
        top = jnp.maximum(jnp.max(s, axis=1, keepdims=True), LOWEST)
        top = top.astype(jnp.bfloat16).astype(jnp.float32)
        w = jnp.exp(s - top)
        total = jnp.sum(w, axis=1, keepdims=True)
        acc = jnp.dot(w.astype(jnp.bfloat16), v, preferred_element_type=jnp.float32)
        out_ref[:, cols] = acc.astype(jnp.bfloat16)
        coarse = total.astype(jnp.bfloat16).astype(jnp.float32)
        stats = jnp.where(lane == h, top, stats)
        stats = jnp.where(lane == heads + h, coarse, stats)
        stats = jnp.where(lane == 2 * heads + h, total - coarse, stats)
    out_ref[:, width:] = stats.astype(jnp.bfloat16)


def combine_kernel(parts_ref, out_ref):
    width = out_ref.shape[2]
    heads = width // HD
    stats = parts_ref[:, :, width:].astype(jnp.float32)
    for h in range(heads):
        cols = slice(h * HD, (h + 1) * HD)
        top = stats[:, :, h : h + 1]
        factor = jnp.exp(top - jnp.max(top, axis=0, keepdims=True))
        total = stats[:, :, heads + h : heads + h + 1] + stats[:, :, 2 * heads + h : 2 * heads + h + 1]
        denominator = jnp.sum(factor * total, axis=0)
        summed = jnp.sum(factor * parts_ref[:, :, cols].astype(jnp.float32), axis=0)
        done = (summed / denominator).astype(jnp.bfloat16)
        for i in range(out_ref.shape[0]):
            out_ref[i, :, cols] = done


def project_kernel(rows_ref, near_ref, far_ref, out_ref):
    zh = lax.axis_index("zh")
    head = lax.axis_index("head")
    half = rows_ref.shape[0] // 2
    for turn, weight in enumerate((near_ref, far_ref)):
        for r in range(2):
            piece = lax.dot_general(
                weight[...],
                rows_ref[r * half : (r + 1) * half, :],
                (((1,), (1,)), ((), ())),
                preferred_element_type=jnp.float32,
            )
            slot = (((zh ^ turn) * 2) + r) ^ head
            out_ref[slot] = piece.astype(jnp.bfloat16)


def shards(q, k, v, block_order, valid_frames, noise_steps, gate_table, out_weight, residual):
    tokens, width = q.shape[1:]
    ny = lax.axis_size("y")
    nx = lax.axis_size("span")
    swap = [(0, 1), (1, 0)]
    vmem = pl.BlockSpec(memory_space=pltpu.VMEM)
    smem = pl.BlockSpec(memory_space=pltpu.SMEM)
    bf16 = jnp.bfloat16
    params = pltpu.CompilerParams(vmem_limit_bytes=48 * 1024 * 1024)

    with jax.named_scope("fetch_kv_zh"):
        kv = jnp.concatenate([k, v])
        kv_far = lax.ppermute(kv, "zh", swap)
    with jax.named_scope("gather_q"):
        queries = lax.all_to_all(jnp.broadcast_to(q, (ny, tokens, width)), "y", 0, 0, tiled=True)
    with jax.named_scope("gather_kv"):
        kv = jnp.stack([kv[0], kv_far[0], kv[1], kv_far[1]])
        near = lax.all_gather(kv, "span", axis=0, tiled=True).reshape(nx * 4 * tokens, width)
        far = lax.ppermute(near, "core", swap)
    with jax.named_scope("fetch_weight"):
        weight = out_weight.T
        weight_far = lax.ppermute(weight, "zh", swap)
    parts = pl.pallas_call(
        attend_kernel,
        out_shape=jax.ShapeDtypeStruct((ny * tokens, width + HD), bf16),
        in_specs=[smem, smem, vmem, vmem, vmem],
        out_specs=vmem,
        compiler_params=params,
        name="attend",
    )(block_order, valid_frames, queries.reshape(ny * tokens, width), near, far)
    with jax.named_scope("return_parts"):
        parts = lax.all_to_all(parts.reshape(ny, tokens, width + HD), "y", 0, 0, tiled=True)
    attended = pl.pallas_call(
        combine_kernel,
        out_shape=jax.ShapeDtypeStruct((ny, tokens, width), bf16),
        in_specs=[vmem],
        out_specs=vmem,
        compiler_params=params,
        name="combine",
    )(parts)
    with jax.named_scope("gather_attended"):
        attended = lax.all_to_all(attended, "y", 0, 0, tiled=True)
        attended = lax.all_gather(attended, "core", axis=1, tiled=True).reshape(2 * ny * tokens, width)
    cols = weight.shape[0]
    pieces = pl.pallas_call(
        project_kernel,
        out_shape=jax.ShapeDtypeStruct((4, cols, ny * tokens), bf16),
        in_specs=[vmem, vmem, vmem],
        out_specs=vmem,
        compiler_params=params,
        name="project",
    )(attended, weight, weight_far)
    with jax.named_scope("sum_heads"):
        total = None
        for i in range(4):
            hops = []
            for zh in range(2):
                for head in range(4):
                    j = i ^ head
                    hops.append((zh * 4 + head, (j >> 1) * 4 + 2 * zh + (j & 1)))
            got = lax.ppermute(pieces[i], ("zh", "head"), hops).astype(jnp.float32)
            total = got if total is None else total + got
    with jax.named_scope("finish"):
        block = lax.axis_index("span")
        step = jnp.sum(jnp.where(jnp.arange(noise_steps.shape[0]) == block, noise_steps, 0))
        chosen = jnp.arange(gate_table.shape[0]) == step
        gate = jnp.sum(jnp.where(chosen[:, None], gate_table, 0.0), axis=0)
        mixed = (residual[0].T.astype(jnp.float32) + gate[:, None] * total).astype(bf16)
    return mixed.T[None]


def solution(mesh):
    fine = Mesh(mesh.devices.reshape(4, 2, 8, 2, 4), AXES)
    seq = ("zh", "y", "core")
    placed = (
        P("span", seq, "head"),
        P("span", seq, "head"),
        P("span", seq, "head"),
        P(),
        P(),
        P(),
        P(None, seq),
        P("head", seq),
        P("span", "head", seq),
    )
    return jax.shard_map(
        shards, mesh=fine, in_specs=placed, out_specs=P("span", "head", seq), check_vma=False
    )
```

time: 469 us -> 139 us (0.30)
  the two profiles are of different devices: /device:TPU:1 before, /device:TPU:73 now
where the time goes in v1:
time: 139 us
  blocking collectives  61.7 us (44%)
  starting transfers between devices  46.3 us (33%)
  waiting for transfers between devices  20.5 us (15%)
  Pallas kernels  5.68 us (4%)
  other arithmetic  3.05 us (2%)
  local copies, waits for them, and re-layouts  1.46 us (1%)
    all_to_all x1, blocking collectives, shards(): lax.all_to_all(jnp.broadcast_to(q, (ny, tokens, width)), 'y', 0, 0, tiled...  21.7 us
    all_to_all x1, blocking collectives, shards(): lax.all_to_all(parts.reshape(ny, tokens, width + HD), 'y', 0, 0, tiled=True)  21.5 us
    ppermute x4, starting transfers between devices, shards(): got = lax.ppermute(pieces[i], ('zh', 'head'), hops).astype(jnp.float32)  15.2 us
    all_gather x1, blocking collectives, shards(): lax.all_gather(kv, 'span', axis=0, tiled=True)  12.1 us
    ppermute x4, waiting for transfers between devices, shards(): got = lax.ppermute(pieces[i], ('zh', 'head'), hops).astype(jnp.float32)  11.2 us
    ppermute x1, starting transfers between devices, shards(): kv_far = lax.ppermute(kv, 'zh', swap)  9.87 us
    ppermute x1, starting transfers between devices, shards(): far = lax.ppermute(near, 'core', swap)  9.08 us
    ppermute x1, starting transfers between devices, shards(): weight_far = lax.ppermute(weight, 'zh', swap)  6.96 us
  transfers between devices with their start and end apart: 8, of which 5 were waited for; matrix products, arithmetic and copies ran while one was open for 1% of the time, Pallas kernels for 0%

profile of v1, /device:TPU:73, one launch (start us, length us, event | category | flops | bytes accessed | tf_op | source)
XLA Modules:
  0.0 138.9 jit_solution(6527194585280997130)
XLA Ops:
  0.0 0.9 pad_maximum_fusion.1
  0.9 0.0 copy-start.3
  0.9 0.0 copy-start.4
  0.9 9.9 %collective-permute-start = (bf16[2,40,768]{2,1,0:T(8,128)(2,1)S(1)}, bf16[2,40,768]{2,1,0:T(8,128)(2,1)S(1)}, u32[]{:S(2)}, u32[]{:S(2)}) collective-permute-start(bf16[2,40,768]{2,1,0:T(8,128)(2,1)S(1)} %pad_maximum_fusion.1), channel_id=1, source_target_pairs={{0,64},{64,0},{1,65},{65,1},{2,66},{66,2},{3,67},{67,3},{4,68},{68... | collective-permute-start | bytes 368648 | tf_op jit(solution)/shard_map/fetch_kv_zh/ppermute | solution.py:108
  10.8 3.0 %collective-permute-done = bf16[2,40,768]{2,1,0:T(8,128)(2,1)S(1)} collective-permute-done((bf16[2,40,768]{2,1,0:T(8,128)(2,1)S(1)}, bf16[2,40,768]{2,1,0:T(8,128)(2,1)S(1)}, u32[]{:S(2)}, u32[]{:S(2)}) %collective-permute-start) | collective-permute-done | bytes 122912 | tf_op jit(solution)/shard_map/fetch_kv_zh/ppermute | solution.py:108
  13.8 0.0 copy-done.3
  13.8 0.0 copy-done.4
  13.9 0.0 copy-start.6
  13.9 12.1 %all_gather.6 = bf16[16,40,768]{2,1,0:T(8,128)(2,1)S(1)} all-gather(bf16[4,40,768]{2,1,0:T(8,128)(2,1)S(1)} %pad_maximum_fusion), channel_id=1, replica_groups=mesh['span'=4,'zh'=2,'y'=8,'core'=2,'head'=4] {'span'}, dimensions={0}, use_global_device_ids=true | all-gather | bytes 1228800 | tf_op jit(solution)/shard_map/gather_kv/all_gather | solution.py:113
  26.0 9.1 %collective-permute-start.1 = (bf16[640,768]{1,0:T(8,128)(2,1)S(1)}, bf16[640,768]{1,0:T(8,128)(2,1)S(1)}, u32[]{:S(2)}, u32[]{:S(2)}) collective-permute-start(bf16[640,768]{1,0:T(8,128)(2,1)S(1)} %bitcast.30), channel_id=1, source_target_pairs={{0,4},{4,0},{1,5},{5,1},{2,6},{6,2},{3,7},{7,3},{8,12},{12,8},{9,1... | collective-permute-start | bytes 2949128 | tf_op jit(solution)/shard_map/gather_kv/ppermute | solution.py:114
  35.1 0.0 copy-done.6
  35.1 21.7 %all_to_all.15 = bf16[8,40,768]{2,1,0:T(8,128)(2,1)S(1)} all-to-all(bf16[8,40,768]{2,1,0:T(8,128)(2,1)S(1)} %broadcast_in_dim.32), channel_id=1, replica_groups=mesh['span'=4,'zh'=2,'y'=8,'core'=2,'head'=4] {'y'}, dimensions={0} | all-to-all | bytes 983040 | tf_op jit(solution)/shard_map/gather_q/all_to_all | solution.py:110
  56.8 0.0 copy-start.1
  56.8 0.0 copy-start.2
  56.8 0.0 collective-permute-done.1.far_ref
  56.8 0.6 copy-done.1
  57.5 0.0 copy-done.2
  57.5 3.5 %attend.1 = bf16[320,896]{1,0:T(8,128)(2,1)S(1)} custom-call(s32[4]{0:T(128)S(1)} %copy-done.1, s32[4]{0:T(128)S(1)} %copy-done.2, bf16[320,768]{1,0:T(8,128)(2,1)S(1)} %bitcast.33, bf16[640,768]{1,0:T(8,128)(2,1)S(1)} %bitcast.31, bf16[640,768]{1,0:T(8,128)(2,1)S(1)} %collective-permute-done.1.far_ref), custom_call_target="tpu_custom_call" | custom-call | tf_op jit(solution)/shard_map/attend/pallas_call | solution.py:118
  61.0 21.5 %all_to_all.16.parts_ref = bf16[8,40,896]{2,1,0:T(8,128)(2,1)S(1)} all-to-all(bf16[8,40,896]{2,1,0:T(8,128)(2,1)S(1)} %bitcast.32), channel_id=1, replica_groups=mesh['span'=4,'zh'=2,'y'=8,'core'=2,'head'=4] {'y'}, dimensions={0} | all-to-all | bytes 1146880 | tf_op jit(solution)/shard_map/return_parts/all_to_all | solution.py:127
  82.5 1.3 combine.1
  83.8 0.0 copy-start
  83.8 5.2 %all-to-all-start.2 = ((bf16[8,40,768]{2,1,0:T(8,128)(2,1)}), bf16[8,40,768]{2,1,0:T(8,128)(2,1)S(1)}, u32[]{:S(2)}, u32[]{:S(2)}) async-start(bf16[8,40,768]{2,1,0:T(8,128)(2,1)} %combine.1), calls=%async_computation.2 | async-start | bytes 983040 | tf_op jit(solution)/shard_map/gather_attended/all_to_all | solution.py:137
  89.0 0.0 copy-done
  89.0 7.0 %collective-permute-start.2 = (bf16[192,768]{1,0:T(8,128)(2,1)S(1)}, bf16[192,768]{1,0:T(8,128)(2,1)S(1)}, u32[]{:S(2)}, u32[]{:S(2)}) collective-permute-start(bf16[192,768]{1,0:T(8,128)(2,1)S(1)} %bitcast.34), channel_id=1, source_target_pairs={{0,64},{64,0},{1,65},{65,1},{2,66},{66,2},{3,67},{67,3},{4,68},{68... | collective-permute-start | bytes 884744 | tf_op jit(solution)/shard_map/fetch_weight/ppermute | solution.py:117
  96.0 0.0 copy-start.8
  96.0 0.6 copy-done.8
  96.6 0.6 fusion.3
  97.3 4.0 %all-to-all-done.2 = bf16[8,40,768]{2,1,0:T(8,128)(2,1)S(1)} async-done(((bf16[8,40,768]{2,1,0:T(8,128)(2,1)}), bf16[8,40,768]{2,1,0:T(8,128)(2,1)S(1)}, u32[]{:S(2)}, u32[]{:S(2)}) %all-to-all-start.2) | async-done | bytes 491552 | tf_op jit(solution)/shard_map/gather_attended/all_to_all | solution.py:137
  101.3 6.4 %all_gather.7 = bf16[8,80,768]{2,1,0:T(8,128)(2,1)S(1)} all-gather(bf16[8,40,768]{2,1,0:T(8,128)(2,1)S(1)} %all-to-all-done.2), channel_id=1, replica_groups=mesh['span'=4,'zh'=2,'y'=8,'core'=2,'head'=4] {'core'}, dimensions={1}, use_global_device_ids=true | all-gather | bytes 1474560 | tf_op jit(solution)/shard_map/gather_attended/all_gather | solution.py:138
  107.7 2.2 %collective-permute-done.2.far_ref = bf16[192,768]{1,0:T(8,128)(2,1)S(1)} collective-permute-done((bf16[192,768]{1,0:T(8,128)(2,1)S(1)}, bf16[192,768]{1,0:T(8,128)(2,1)S(1)}, u32[]{:S(2)}, u32[]{:S(2)}) %collective-permute-start.2) | collective-permute-done | bytes 294944 | tf_op jit(solution)/shard_map/fetch_weight/ppermute | solution.py:117
  109.9 0.9 project.1
  110.8 0.0 copy-start.5
  110.8 0.1 slice_bitcast_fusion.3
  110.9 0.0 copy-start.7
  110.9 0.7 collective-permute-start.3
  111.6 1.9 %collective-permute-start.4 = (bf16[192,320]{1,0:T(8,128)(2,1)S(1)}, bf16[192,320]{1,0:T(8,128)(2,1)S(1)}, u32[]{:S(2)}, u32[]{:S(2)}) collective-permute-start(bf16[192,320]{1,0:T(8,128)(2,1)S(1)} %get-tuple-element.8), channel_id=1, source_target_pairs={{0,1},{1,0},{2,65},{3,64},{64,3},{65,2},{66,67},{67,66},{4,5},{5,4... | collective-permute-start | bytes 368648 | tf_op jit(solution)/shard_map/sum_heads/ppermute | solution.py:156
  113.5 9.7 %collective-permute-start.5 = (bf16[192,320]{1,0:T(8,128)(2,1)S(1)}, bf16[192,320]{1,0:T(8,128)(2,1)S(1)}, u32[]{:S(2)}, u32[]{:S(2)}) collective-permute-start(bf16[192,320]{1,0:T(8,128)(2,1)S(1)} %get-tuple-element.7), channel_id=1, source_target_pairs={{0,64},{1,65},{2,0},{3,1},{64,66},{65,67},{66,2},{67,3},{4,68},{5,... | collective-permute-start | bytes 368648 | tf_op jit(solution)/shard_map/sum_heads/ppermute | solution.py:156
  123.2 2.9 %collective-permute-start.6 = (bf16[192,320]{1,0:T(8,128)(2,1)S(1)}, bf16[192,320]{1,0:T(8,128)(2,1)S(1)}, u32[]{:S(2)}, u32[]{:S(2)}) collective-permute-start(bf16[192,320]{1,0:T(8,128)(2,1)S(1)} %get-tuple-element.6), channel_id=1, source_target_pairs={{0,65},{1,64},{2,1},{3,0},{64,67},{65,66},{66,3},{67,2},{4,69},{5,... | collective-permute-start | bytes 368648 | tf_op jit(solution)/shard_map/sum_heads/ppermute | solution.py:156
  126.1 0.7 iota_compare_fusion
  126.8 0.0 copy-done.7
  126.8 0.1 select_reduce_fusion
  126.9 0.0 collective-permute-done.3
  126.9 0.0 collective-permute-done.4
  126.9 3.0 %collective-permute-done.5 = bf16[192,320]{1,0:T(8,128)(2,1)S(1)} collective-permute-done((bf16[192,320]{1,0:T(8,128)(2,1)S(1)}, bf16[192,320]{1,0:T(8,128)(2,1)S(1)}, u32[]{:S(2)}, u32[]{:S(2)}) %collective-permute-start.5) | collective-permute-done | bytes 122912 | tf_op jit(solution)/shard_map/sum_heads/ppermute | solution.py:156
  129.9 8.2 %collective-permute-done.6 = bf16[192,320]{1,0:T(8,128)(2,1)S(1)} collective-permute-done((bf16[192,320]{1,0:T(8,128)(2,1)S(1)}, bf16[192,320]{1,0:T(8,128)(2,1)S(1)}, u32[]{:S(2)}, u32[]{:S(2)}) %collective-permute-start.6) | collective-permute-done | bytes 122912 | tf_op jit(solution)/shard_map/sum_heads/ppermute | solution.py:156
  138.1 0.0 copy-done.5
  138.1 0.8 fusion.2
  (3 shorter events, 0.1 us)
Async XLA Ops:
  0.9 12.9 %copy-start.3 = (bf16[1,40,768]{2,1,0:T(8,128)(2,1)S(1)}, bf16[1,40,768]{2,1,0:T(8,128)(2,1)}, u32[]{:S(2)}) copy-start(bf16[1,40,768]{2,1,0:T(8,128)(2,1)} %param.11) | copy-start | bytes 184324
  0.9 12.9 %copy-start.4 = (bf16[1,40,768]{2,1,0:T(8,128)(2,1)S(1)}, bf16[1,40,768]{2,1,0:T(8,128)(2,1)}, u32[]{:S(2)}) copy-start(bf16[1,40,768]{2,1,0:T(8,128)(2,1)} %param.10) | copy-start | bytes 184324
  0.9 12.9 %collective-permute-start = (bf16[2,40,768]{2,1,0:T(8,128)(2,1)S(1)}, bf16[2,40,768]{2,1,0:T(8,128)(2,1)S(1)}, u32[]{:S(2)}, u32[]{:S(2)}) collective-permute-start(bf16[2,40,768]{2,1,0:T(8,128)(2,1)S(1)} %pad_maximum_fusion.1), channel_id=1, source_target_pairs={{0,64},{64,0},{1,65},{65,1},{2,66},{66,2},{3,67},{67,3},{4,68},{68... | collective-permute-start | bytes 368648 | tf_op jit(solution)/shard_map/fetch_kv_zh/ppermute | solution.py:108
  13.9 21.2 %copy-start.6 = (bf16[1,40,768]{2,1,0:T(8,128)(2,1)S(1)}, bf16[1,40,768]{2,1,0:T(8,128)(2,1)}, u32[]{:S(2)}) copy-start(bf16[1,40,768]{2,1,0:T(8,128)(2,1)} %param.9) | copy-start | bytes 184324
  26.0 30.8 %collective-permute-start.1 = (bf16[640,768]{1,0:T(8,128)(2,1)S(1)}, bf16[640,768]{1,0:T(8,128)(2,1)S(1)}, u32[]{:S(2)}, u32[]{:S(2)}) collective-permute-start(bf16[640,768]{1,0:T(8,128)(2,1)S(1)} %bitcast.30), channel_id=1, source_target_pairs={{0,4},{4,0},{1,5},{5,1},{2,6},{6,2},{3,7},{7,3},{8,12},{12,8},{9,1... | collective-permute-start | bytes 2949128 | tf_op jit(solution)/shard_map/gather_kv/ppermute | solution.py:114
  56.8 0.7 copy-start.1
  56.8 0.7 copy-start.2
  83.8 5.2 %copy-start = (bf16[768,192]{0,1:T(8,128)(2,1)S(1)}, bf16[768,192]{0,1:T(8,128)(2,1)}, u32[]{:S(2)}) copy-start(bf16[768,192]{0,1:T(8,128)(2,1)} %param.16) | copy-start | bytes 884740
  83.8 17.5 %all-to-all-start.2 = ((bf16[8,40,768]{2,1,0:T(8,128)(2,1)}), bf16[8,40,768]{2,1,0:T(8,128)(2,1)S(1)}, u32[]{:S(2)}, u32[]{:S(2)}) async-start(bf16[8,40,768]{2,1,0:T(8,128)(2,1)} %combine.1), calls=%async_computation.2 | async-start | bytes 983040 | tf_op jit(solution)/shard_map/gather_attended/all_to_all | solution.py:137
  89.0 20.9 %collective-permute-start.2 = (bf16[192,768]{1,0:T(8,128)(2,1)S(1)}, bf16[192,768]{1,0:T(8,128)(2,1)S(1)}, u32[]{:S(2)}, u32[]{:S(2)}) collective-permute-start(bf16[192,768]{1,0:T(8,128)(2,1)S(1)} %bitcast.34), channel_id=1, source_target_pairs={{0,64},{64,0},{1,65},{65,1},{2,66},{66,2},{3,67},{67,3},{4,68},{68... | collective-permute-start | bytes 884744 | tf_op jit(solution)/shard_map/fetch_weight/ppermute | solution.py:117
  96.0 0.7 copy-start.8
  110.8 27.3 %copy-start.5 = (bf16[1,320,192]{1,2,0:T(8,128)(2,1)S(1)}, bf16[1,320,192]{1,2,0:T(8,128)(2,1)}, u32[]{:S(2)}) copy-start(bf16[1,320,192]{1,2,0:T(8,128)(2,1)} %param.17) | copy-start | bytes 368644
  110.9 15.9 %copy-start.7 = (f32[4,192]{1,0:T(4,128)S(1)}, f32[4,192]{1,0:T(4,128)}, u32[]{:S(2)}) copy-start(f32[4,192]{1,0:T(4,128)} %param.15) | copy-start | bytes 9220
  110.9 16.0 %collective-permute-start.3 = (bf16[192,320]{1,0:T(8,128)(2,1)S(1)}, bf16[192,320]{1,0:T(8,128)(2,1)S(1)}, u32[]{:S(2)}, u32[]{:S(2)}) collective-permute-start(bf16[192,320]{1,0:T(8,128)(2,1)S(1)} %get-tuple-element.5), channel_id=1, source_target_pairs={{0,0},{1,1},{2,64},{3,65},{64,2},{65,3},{66,66},{67,67},{4,4},{5,5... | collective-permute-start | bytes 368648 | tf_op jit(solution)/shard_map/sum_heads/ppermute | solution.py:156
  111.6 15.3 %collective-permute-start.4 = (bf16[192,320]{1,0:T(8,128)(2,1)S(1)}, bf16[192,320]{1,0:T(8,128)(2,1)S(1)}, u32[]{:S(2)}, u32[]{:S(2)}) collective-permute-start(bf16[192,320]{1,0:T(8,128)(2,1)S(1)} %get-tuple-element.8), channel_id=1, source_target_pairs={{0,1},{1,0},{2,65},{3,64},{64,3},{65,2},{66,67},{67,66},{4,5},{5,4... | collective-permute-start | bytes 368648 | tf_op jit(solution)/shard_map/sum_heads/ppermute | solution.py:156
  113.5 16.4 %collective-permute-start.5 = (bf16[192,320]{1,0:T(8,128)(2,1)S(1)}, bf16[192,320]{1,0:T(8,128)(2,1)S(1)}, u32[]{:S(2)}, u32[]{:S(2)}) collective-permute-start(bf16[192,320]{1,0:T(8,128)(2,1)S(1)} %get-tuple-element.7), channel_id=1, source_target_pairs={{0,64},{1,65},{2,0},{3,1},{64,66},{65,67},{66,2},{67,3},{4,68},{5,... | collective-permute-start | bytes 368648 | tf_op jit(solution)/shard_map/sum_heads/ppermute | solution.py:156
  123.2 14.9 %collective-permute-start.6 = (bf16[192,320]{1,0:T(8,128)(2,1)S(1)}, bf16[192,320]{1,0:T(8,128)(2,1)S(1)}, u32[]{:S(2)}, u32[]{:S(2)}) collective-permute-start(bf16[192,320]{1,0:T(8,128)(2,1)S(1)} %get-tuple-element.6), channel_id=1, source_target_pairs={{0,65},{1,64},{2,1},{3,0},{64,67},{65,66},{66,3},{67,2},{4,69},{5,... | collective-permute-start | bytes 368648 | tf_op jit(solution)/shard_map/sum_heads/ppermute | solution.py:156

commit v2 on v1

v2 whole, which is shorter than its diff:
```python
import jax
import jax.numpy as jnp
from jax import lax
from jax.experimental import pallas as pl
from jax.experimental.pallas import tpu as pltpu
from jax.sharding import Mesh, PartitionSpec as P

HD = 128
CLOSED = -1e30
LOWEST = -1e20
AXES = ("span", "zh", "y2", "y1", "y0", "core", "head")
FRAME = ("zh", "y2", "y1")


def attend_kernel(order_ref, valid_ref, q_ref, near_ref, far_ref, out_ref):
    blocks = order_ref.shape[0]
    rows, width = q_ref.shape
    heads = width // HD
    slab = near_ref.shape[0] // (2 * blocks)
    frame = lax.axis_index("zh") * 4 + lax.axis_index("y2") * 2 + lax.axis_index("y1")
    order_here = order_ref[lax.axis_index("span")]
    place = lax.broadcasted_iota(jnp.int32, (1, 2 * blocks * slab), 1)
    place = jnp.where(place >= blocks * slab, place - blocks * slab, place)
    bias = jnp.zeros(place.shape, jnp.float32)
    for block in range(blocks):
        is_open = (order_ref[block] <= order_here) & (frame < valid_ref[block])
        inside = (place >= block * slab) & (place < (block + 1) * slab)
        bias = jnp.where(inside & jnp.logical_not(is_open), CLOSED, bias)
    lane = lax.broadcasted_iota(jnp.int32, (rows, HD), 1)
    stats = jnp.zeros((rows, HD), jnp.float32)
    scale = 1.0 / HD**0.5
    for h in range(heads):
        cols = slice(h * HD, (h + 1) * HD)
        k = jnp.concatenate(
            [ref[2 * b * slab : (2 * b + 1) * slab, cols] for ref in (near_ref, far_ref) for b in range(blocks)]
        )
        v = jnp.concatenate(
            [ref[(2 * b + 1) * slab : (2 * b + 2) * slab, cols] for ref in (near_ref, far_ref) for b in range(blocks)]
        )
        s = lax.dot_general(q_ref[:, cols], k, (((1,), (1,)), ((), ())), preferred_element_type=jnp.float32)
        s = s * scale + bias
        top = jnp.maximum(jnp.max(s, axis=1, keepdims=True), LOWEST)
        top = top.astype(jnp.bfloat16).astype(jnp.float32)
        w = jnp.exp(s - top)
        total = jnp.sum(w, axis=1, keepdims=True)
        acc = jnp.dot(w.astype(jnp.bfloat16), v, preferred_element_type=jnp.float32)
        out_ref[:, cols] = acc.astype(jnp.bfloat16)
        coarse = total.astype(jnp.bfloat16).astype(jnp.float32)
        stats = jnp.where(lane == h, top, stats)
        stats = jnp.where(lane == heads + h, coarse, stats)
        stats = jnp.where(lane == 2 * heads + h, total - coarse, stats)
    out_ref[:, width:] = stats.astype(jnp.bfloat16)


def combine_kernel(parts_ref, out_ref):
    width = out_ref.shape[2]
    heads = width // HD
    stats = parts_ref[:, :, width:].astype(jnp.float32)
    for h in range(heads):
        cols = slice(h * HD, (h + 1) * HD)
        top = stats[:, :, h : h + 1]
        factor = jnp.exp(top - jnp.max(top, axis=0, keepdims=True))
        total = stats[:, :, heads + h : heads + h + 1] + stats[:, :, 2 * heads + h : 2 * heads + h + 1]
        denominator = jnp.sum(factor * total, axis=0)
        summed = jnp.sum(factor * parts_ref[:, :, cols].astype(jnp.float32), axis=0)
        done = (summed / denominator).astype(jnp.bfloat16)
        for i in range(out_ref.shape[0]):
            out_ref[i, :, cols] = done


def project_kernel(rows_ref, near_ref, far_ref, out_ref):
    y0 = lax.axis_index("y0")
    chunks = out_ref.shape[0] // 2
    rows = rows_ref.shape[0] // chunks
    half = rows // 2
    for turn, weight in enumerate((near_ref, far_ref)):
        for chunk in range(chunks):
            piece = lax.dot_general(
                rows_ref[chunk * rows : (chunk + 1) * rows, :],
                weight[...],
                (((1,), (1,)), ((), ())),
                preferred_element_type=jnp.float32,
            )
            slot = chunk * 2 + (y0 ^ turn)
            out_ref[slot, :rows, :] = piece[:, :HD].astype(jnp.bfloat16)
            tail = jnp.concatenate([piece[:half, HD:], piece[half:, HD:]], axis=1)
            out_ref[slot, rows:, :] = tail.astype(jnp.bfloat16)


def finish_kernel(steps_ref, pieces_ref, gate_ref, residual_ref, out_ref):
    step = steps_ref[lax.axis_index("span")]
    gate = gate_ref[pl.ds(step, 1), :]
    rows = residual_ref.shape[1] // 2
    half = rows // 2
    sums = []
    for y0 in range(2):
        total = pieces_ref[y0].astype(jnp.float32)
        for head in range(1, 4):
            total = total + pieces_ref[2 * head + y0].astype(jnp.float32)
        sums.append(total)
    near, far = sums
    main = jnp.concatenate([near[:half], far[:half], near[half:rows], far[half:rows]])
    rest = HD // 2
    tail = jnp.concatenate([near[rows:, :rest], far[rows:, :rest], near[rows:, rest:], far[rows:, rest:]])
    main = (main * gate[:, :HD]).T
    tail = (tail * gate[:, HD:]).T
    out_ref[:HD, :] = (residual_ref[:HD, :].astype(jnp.float32) + main).astype(jnp.bfloat16)
    out_ref[HD:, :] = (residual_ref[HD:, :].astype(jnp.float32) + tail).astype(jnp.bfloat16)


def shards(q, k, v, block_order, valid_frames, noise_steps, gate_table, out_weight, residual):
    tokens, width = q.shape[1:]
    parts_n = 8
    nx = lax.axis_size("span")
    swap = [(0, 1), (1, 0)]
    vmem = pl.BlockSpec(memory_space=pltpu.VMEM)
    smem = pl.BlockSpec(memory_space=pltpu.SMEM)
    bf16 = jnp.bfloat16
    params = pltpu.CompilerParams(vmem_limit_bytes=48 * 1024 * 1024)

    with jax.named_scope("fetch_kv"):
        kv = jnp.concatenate([k, v])
        kv_far = lax.ppermute(kv, "y0", swap)
    with jax.named_scope("gather_q"):
        queries = lax.all_to_all(jnp.broadcast_to(q, (parts_n, tokens, width)), FRAME, 0, 0, tiled=True)
    with jax.named_scope("gather_kv"):
        kv = jnp.stack([kv[0], kv_far[0], kv[1], kv_far[1]])
        near = lax.all_gather(kv, "span", axis=0, tiled=True).reshape(nx * 4 * tokens, width)
        far = lax.ppermute(near, "core", swap)
    with jax.named_scope("fetch_weight"):
        weight = out_weight.T
        weight_far = lax.ppermute(weight, "y0", swap)
    parts = pl.pallas_call(
        attend_kernel,
        out_shape=jax.ShapeDtypeStruct((parts_n * tokens, width + HD), bf16),
        in_specs=[smem, smem, vmem, vmem, vmem],
        out_specs=vmem,
        compiler_params=params,
        name="attend",
    )(block_order, valid_frames, queries.reshape(parts_n * tokens, width), near, far)
    with jax.named_scope("return_parts"):
        parts = lax.all_to_all(parts.reshape(parts_n, tokens, width + HD), FRAME, 0, 0, tiled=True)
    attended = pl.pallas_call(
        combine_kernel,
        out_shape=jax.ShapeDtypeStruct((parts_n, tokens, width), bf16),
        in_specs=[vmem],
        out_specs=vmem,
        compiler_params=params,
        name="combine",
    )(parts)
    with jax.named_scope("gather_attended"):
        attended = lax.all_to_all(attended, FRAME, 0, 0, tiled=True)
        attended = lax.all_gather(attended, "core", axis=1, tiled=True).reshape(2 * parts_n * tokens, width)
    cols = weight.shape[0]
    slot_rows = 4 * tokens * cols // HD
    pieces = pl.pallas_call(
        project_kernel,
        out_shape=jax.ShapeDtypeStruct((8, slot_rows, HD), bf16),
        in_specs=[vmem, vmem, vmem],
        out_specs=vmem,
        compiler_params=params,
        name="project",
    )(attended, weight, weight_far)
    with jax.named_scope("sum_heads"):
        pieces = lax.all_to_all(pieces, ("head", "y0"), 0, 0, tiled=True)
    mixed = pl.pallas_call(
        finish_kernel,
        out_shape=jax.ShapeDtypeStruct(residual.shape[:0:-1], bf16),
        in_specs=[smem, vmem, vmem, vmem],
        out_specs=vmem,
        compiler_params=params,
        name="finish",
    )(noise_steps, pieces, gate_table, residual[0].T)
    return mixed.T[None]


def solution(mesh):
    fine = Mesh(mesh.devices.reshape(4, 2, 2, 2, 2, 2, 4), AXES)
    seq = ("zh", "y2", "y1", "y0", "core")
    placed = (
        P("span", seq, "head"),
        P("span", seq, "head"),
        P("span", seq, "head"),
        P(),
        P(),
        P(),
        P(None, seq),
        P("head", seq),
        P("span", "head", seq),
    )
    return jax.shard_map(
        shards, mesh=fine, in_specs=placed, out_specs=P("span", "head", seq), check_vma=False
    )
```

time: 139 us -> 142 us (1.022)
  the two profiles are of different devices: /device:TPU:73 before, /device:TPU:1 now
where the time goes in v2:
time: 142 us; the launch traced here: 141 us
  blocking collectives  91.6 us (65%)
  starting transfers between devices  20.6 us (15%)
  waiting for transfers between devices  19.1 us (13%)
  Pallas kernels  7.19 us (5%)
    all_to_all x1, blocking collectives, shards(): lax.all_to_all(jnp.broadcast_to(q, (parts_n, tokens, width)), FRAME, 0, 0...  31.2 us
    all_to_all x1, blocking collectives, shards(): lax.all_to_all(parts.reshape(parts_n, tokens, width + HD), FRAME, 0, 0, t...  27.8 us
    all_to_all x1, waiting for transfers between devices, shards(): attended = lax.all_to_all(attended, FRAME, 0, 0, tiled=True)  16.8 us
    all_to_all x1, blocking collectives, shards(): pieces = lax.all_to_all(pieces, ('head', 'y0'), 0, 0, tiled=True)  16.8 us
    all_gather x1, blocking collectives, shards(): lax.all_gather(kv, 'span', axis=0, tiled=True)  12.2 us
    ppermute x1, starting transfers between devices, shards(): far = lax.ppermute(near, 'core', swap)  10.9 us
    ppermute x1, starting transfers between devices, shards(): kv_far = lax.ppermute(kv, 'y0', swap)  4.17 us
    all_gather x1, blocking collectives, shards(): lax.all_gather(attended, 'core', axis=1, tiled=True)  3.67 us
  transfers between devices with their start and end apart: 4, of which 2 were waited for; matrix products, arithmetic and copies ran while one was open for 0% of the time, Pallas kernels for 0%

profile of v2, /device:TPU:1, one launch (start us, length us, event | category | flops | bytes accessed | tf_op | source)
XLA Modules:
  0.0 140.9 jit_solution(18319736019740757971)
XLA Ops:
  0.0 0.9 pad_maximum_fusion.1
  0.9 0.0 copy-start.6
  0.9 0.0 copy-start.7
  0.9 4.2 %collective-permute-start = (bf16[2,40,768]{2,1,0:T(8,128)(2,1)S(1)}, bf16[2,40,768]{2,1,0:T(8,128)(2,1)S(1)}, u32[]{:S(2)}, u32[]{:S(2)}) collective-permute-start(bf16[2,40,768]{2,1,0:T(8,128)(2,1)S(1)} %pad_maximum_fusion.1), channel_id=1, source_target_pairs={{0,8},{8,0},{1,9},{9,1},{2,10},{10,2},{3,11},{11,3},{4,12},{12,4},... | collective-permute-start | bytes 368648 | tf_op jit(solution)/shard_map/fetch_kv/ppermute | solution.py:123
  5.1 2.3 %collective-permute-done = bf16[2,40,768]{2,1,0:T(8,128)(2,1)S(1)} collective-permute-done((bf16[2,40,768]{2,1,0:T(8,128)(2,1)S(1)}, bf16[2,40,768]{2,1,0:T(8,128)(2,1)S(1)}, u32[]{:S(2)}, u32[]{:S(2)}) %collective-permute-start) | collective-permute-done | bytes 122912 | tf_op jit(solution)/shard_map/fetch_kv/ppermute | solution.py:123
  7.3 0.0 copy-done.6
  7.3 0.0 copy-done.7
  7.4 0.0 copy-start.8
  7.4 12.2 %all_gather.6 = bf16[16,40,768]{2,1,0:T(8,128)(2,1)S(1)} all-gather(bf16[4,40,768]{2,1,0:T(8,128)(2,1)S(1)} %pad_maximum_fusion), channel_id=1, replica_groups=mesh['span'=4,'zh'=2,'y2'=2,'y1'=2,'y0'=2,'core'=2,'head'=4] {'span'}, dimensions={0}, use_global_device_ids=true | all-gather | bytes 1228800 | tf_op jit(solution)/shard_map/gather_kv/all_gather | solution.py:128
  19.6 10.9 %collective-permute-start.1 = (bf16[640,768]{1,0:T(8,128)(2,1)S(1)}, bf16[640,768]{1,0:T(8,128)(2,1)S(1)}, u32[]{:S(2)}, u32[]{:S(2)}) collective-permute-start(bf16[640,768]{1,0:T(8,128)(2,1)S(1)} %bitcast.13), channel_id=1, source_target_pairs={{0,4},{4,0},{1,5},{5,1},{2,6},{6,2},{3,7},{7,3},{8,12},{12,8},{9,1... | collective-permute-start | bytes 2949128 | tf_op jit(solution)/shard_map/gather_kv/ppermute | solution.py:129
  30.5 0.0 copy-done.8
  30.6 31.2 %all_to_all.20 = bf16[8,40,768]{2,1,0:T(8,128)(2,1)S(1)} all-to-all(bf16[8,40,768]{2,1,0:T(8,128)(2,1)S(1)} %broadcast_in_dim.11), channel_id=1, replica_groups=mesh['span'=4,'zh'=2,'y2'=2,'y1'=2,'y0'=2,'core'=2,'head'=4] {'zh','y2',..., dimensions={0} | all-to-all | bytes 983040 | tf_op jit(solution)/shard_map/gather_q/all_to_all | solution.py:125
  61.8 0.0 copy-start.4
  61.8 0.0 copy-start.5
  61.8 0.0 collective-permute-done.1.far_ref
  61.8 0.6 copy-done.4
  62.4 0.0 copy-done.5
  62.4 3.5 %attend.1 = bf16[320,896]{1,0:T(8,128)(2,1)S(1)} custom-call(s32[4]{0:T(128)S(1)} %copy-done.4, s32[4]{0:T(128)S(1)} %copy-done.5, bf16[320,768]{1,0:T(8,128)(2,1)S(1)} %bitcast.16, bf16[640,768]{1,0:T(8,128)(2,1)S(1)} %bitcast.14, bf16[640,768]{1,0:T(8,128)(2,1)S(1)} %collective-permute-done.1.far_ref), custom_call_target="tpu_custom_call" | custom-call | tf_op jit(solution)/shard_map/attend/pallas_call | solution.py:133
  65.9 27.8 %all_to_all.21.parts_ref = bf16[8,40,896]{2,1,0:T(8,128)(2,1)S(1)} all-to-all(bf16[8,40,896]{2,1,0:T(8,128)(2,1)S(1)} %bitcast.15), channel_id=1, replica_groups=mesh['span'=4,'zh'=2,'y2'=2,'y1'=2,'y0'=2,'core'=2,'head'=4] {'zh','y2',..., dimensions={0} | all-to-all | bytes 1146880 | tf_op jit(solution)/shard_map/return_parts/all_to_all | solution.py:142
  93.7 1.3 combine.1
  95.1 0.0 copy-start
  95.1 3.6 %all-to-all-start.2 = ((bf16[8,40,768]{2,1,0:T(8,128)(2,1)}), bf16[8,40,768]{2,1,0:T(8,128)(2,1)S(1)}, u32[]{:S(2)}, u32[]{:S(2)}) async-start(bf16[8,40,768]{2,1,0:T(8,128)(2,1)} %combine.1), calls=%async_computation.2 | async-start | bytes 983040 | tf_op jit(solution)/shard_map/gather_attended/all_to_all | solution.py:152
  98.7 0.0 copy-done
  98.7 1.9 %collective-permute-start.2 = (bf16[192,768]{1,0:T(8,128)(2,1)S(1)}, bf16[192,768]{1,0:T(8,128)(2,1)S(1)}, u32[]{:S(2)}, u32[]{:S(2)}) collective-permute-start(bf16[192,768]{1,0:T(8,128)(2,1)S(1)} %bitcast.17), channel_id=1, source_target_pairs={{0,8},{8,0},{1,9},{9,1},{2,10},{10,2},{3,11},{11,3},{4,12},{12,4},... | collective-permute-start | bytes 884744 | tf_op jit(solution)/shard_map/fetch_weight/ppermute | solution.py:132
  100.6 16.8 %all-to-all-done.2 = bf16[8,40,768]{2,1,0:T(8,128)(2,1)S(1)} async-done(((bf16[8,40,768]{2,1,0:T(8,128)(2,1)}), bf16[8,40,768]{2,1,0:T(8,128)(2,1)S(1)}, u32[]{:S(2)}, u32[]{:S(2)}) %all-to-all-start.2) | async-done | bytes 491552 | tf_op jit(solution)/shard_map/gather_attended/all_to_all | solution.py:152
  117.4 3.7 %all_gather.7 = bf16[8,80,768]{2,1,0:T(8,128)(2,1)S(1)} all-gather(bf16[8,40,768]{2,1,0:T(8,128)(2,1)S(1)} %all-to-all-done.2), channel_id=1, replica_groups=mesh['span'=4,'zh'=2,'y2'=2,'y1'=2,'y0'=2,'core'=2,'head'=4] {'core'}, dimensions={1}, use_global_device_ids=true | all-gather | bytes 1474560 | tf_op jit(solution)/shard_map/gather_attended/all_gather | solution.py:153
  121.1 0.0 collective-permute-done.2.far_ref
  121.1 1.0 project.1
  122.1 0.0 copy-start.1
  122.1 0.0 copy-start.2
  122.1 16.8 %all_to_all.22.pieces_ref = bf16[8,240,128]{2,1,0:T(8,128)(2,1)S(1)} all-to-all(bf16[8,240,128]{2,1,0:T(8,128)(2,1)S(1)} %project.1), channel_id=1, replica_groups=mesh['span'=4,'zh'=2,'y2'=2,'y1'=2,'y0'=2,'core'=2,'head'=4] {'head','y0'}, dimensions={0} | all-to-all | bytes 983040 | tf_op jit(solution)/shard_map/sum_heads/all_to_all | solution.py:165
  138.9 0.0 copy-start.3
  138.9 0.0 copy-done.1
  138.9 0.0 copy-done.2
  138.9 0.6 copy-done.3
  139.5 1.4 finish.1
  (3 shorter events, 0.1 us)
Async XLA Ops:
  0.9 6.5 %copy-start.6 = (bf16[1,40,768]{2,1,0:T(8,128)(2,1)S(1)}, bf16[1,40,768]{2,1,0:T(8,128)(2,1)}, u32[]{:S(2)}) copy-start(bf16[1,40,768]{2,1,0:T(8,128)(2,1)} %param.11) | copy-start | bytes 184324
  0.9 6.5 %copy-start.7 = (bf16[1,40,768]{2,1,0:T(8,128)(2,1)S(1)}, bf16[1,40,768]{2,1,0:T(8,128)(2,1)}, u32[]{:S(2)}) copy-start(bf16[1,40,768]{2,1,0:T(8,128)(2,1)} %param.10) | copy-start | bytes 184324
  0.9 6.4 %collective-permute-start = (bf16[2,40,768]{2,1,0:T(8,128)(2,1)S(1)}, bf16[2,40,768]{2,1,0:T(8,128)(2,1)S(1)}, u32[]{:S(2)}, u32[]{:S(2)}) collective-permute-start(bf16[2,40,768]{2,1,0:T(8,128)(2,1)S(1)} %pad_maximum_fusion.1), channel_id=1, source_target_pairs={{0,8},{8,0},{1,9},{9,1},{2,10},{10,2},{3,11},{11,3},{4,12},{12,4},... | collective-permute-start | bytes 368648 | tf_op jit(solution)/shard_map/fetch_kv/ppermute | solution.py:123
  7.4 23.1 %copy-start.8 = (bf16[1,40,768]{2,1,0:T(8,128)(2,1)S(1)}, bf16[1,40,768]{2,1,0:T(8,128)(2,1)}, u32[]{:S(2)}) copy-start(bf16[1,40,768]{2,1,0:T(8,128)(2,1)} %param.9) | copy-start | bytes 184324
  19.6 42.2 %collective-permute-start.1 = (bf16[640,768]{1,0:T(8,128)(2,1)S(1)}, bf16[640,768]{1,0:T(8,128)(2,1)S(1)}, u32[]{:S(2)}, u32[]{:S(2)}) collective-permute-start(bf16[640,768]{1,0:T(8,128)(2,1)S(1)} %bitcast.13), channel_id=1, source_target_pairs={{0,4},{4,0},{1,5},{5,1},{2,6},{6,2},{3,7},{7,3},{8,12},{12,8},{9,1... | collective-permute-start | bytes 2949128 | tf_op jit(solution)/shard_map/gather_kv/ppermute | solution.py:129
  61.8 0.7 copy-start.4
  61.8 0.7 copy-start.5
  95.1 3.6 %copy-start = (bf16[768,192]{0,1:T(8,128)(2,1)S(1)}, bf16[768,192]{0,1:T(8,128)(2,1)}, u32[]{:S(2)}) copy-start(bf16[768,192]{0,1:T(8,128)(2,1)} %param.16) | copy-start | bytes 884740
  95.1 22.4 %all-to-all-start.2 = ((bf16[8,40,768]{2,1,0:T(8,128)(2,1)}), bf16[8,40,768]{2,1,0:T(8,128)(2,1)S(1)}, u32[]{:S(2)}, u32[]{:S(2)}) async-start(bf16[8,40,768]{2,1,0:T(8,128)(2,1)} %combine.1), calls=%async_computation.2 | async-start | bytes 983040 | tf_op jit(solution)/shard_map/gather_attended/all_to_all | solution.py:152
  98.7 22.4 %collective-permute-start.2 = (bf16[192,768]{1,0:T(8,128)(2,1)S(1)}, bf16[192,768]{1,0:T(8,128)(2,1)S(1)}, u32[]{:S(2)}, u32[]{:S(2)}) collective-permute-start(bf16[192,768]{1,0:T(8,128)(2,1)S(1)} %bitcast.17), channel_id=1, source_target_pairs={{0,8},{8,0},{1,9},{9,1},{2,10},{10,2},{3,11},{11,3},{4,12},{12,4},... | collective-permute-start | bytes 884744 | tf_op jit(solution)/shard_map/fetch_weight/ppermute | solution.py:132
  122.1 16.8 %copy-start.1 = (bf16[1,320,192]{1,2,0:T(8,128)(2,1)S(1)}, bf16[1,320,192]{1,2,0:T(8,128)(2,1)}, u32[]{:S(2)}) copy-start(bf16[1,320,192]{1,2,0:T(8,128)(2,1)} %param.17) | copy-start | bytes 368644
  122.1 16.8 %copy-start.2 = (f32[4,192]{1,0:T(4,128)S(1)}, f32[4,192]{1,0:T(4,128)}, u32[]{:S(2)}) copy-start(f32[4,192]{1,0:T(4,128)} %gate_ref.1) | copy-start | bytes 9220
  138.9 0.7 copy-start.3

commit v3 on v2

v3 whole, which is shorter than its diff:
```python
import jax
import jax.numpy as jnp
from jax import lax
from jax.experimental import pallas as pl
from jax.experimental.pallas import tpu as pltpu
from jax.sharding import Mesh, PartitionSpec as P

HD = 128
CLOSED = -1e30
LOWEST = -1e20
AXES = ("span", "zh", "y", "core", "head")
FRAMES = 8


def attend_kernel(order_ref, valid_ref, q_ref, keys_ref, values_ref, out_ref):
    blocks = order_ref.shape[0]
    rows, width = q_ref.shape
    heads = width // HD
    count = keys_ref.shape[0]
    slab = count // (2 * blocks)
    zh = lax.axis_index("zh")
    y = lax.axis_index("y")
    order_here = order_ref[lax.axis_index("span")]
    place = lax.broadcasted_iota(jnp.int32, (1, count), 1)
    place = jnp.where(place >= blocks * slab, place - blocks * slab, place)
    bias = jnp.zeros(place.shape, jnp.float32)
    for block in range(blocks):
        for turn in range(2):
            frame = (zh ^ turn) * (FRAMES // 2) + y // 2
            is_open = (order_ref[block] <= order_here) & (frame < valid_ref[block])
            least = block * slab + turn * (slab // 2)
            inside = (place >= least) & (place < least + slab // 2)
            bias = jnp.where(inside & jnp.logical_not(is_open), CLOSED, bias)
    lane = lax.broadcasted_iota(jnp.int32, (rows, HD), 1)
    stats = jnp.zeros((rows, HD), jnp.float32)
    scale = 1.0 / HD**0.5
    for h in range(heads):
        cols = slice(h * HD, (h + 1) * HD)
        s = lax.dot_general(
            q_ref[:, cols], keys_ref[:, cols], (((1,), (1,)), ((), ())), preferred_element_type=jnp.float32
        )
        s = s * scale + bias
        top = jnp.maximum(jnp.max(s, axis=1, keepdims=True), LOWEST)
        top = top.astype(jnp.bfloat16).astype(jnp.float32)
        w = jnp.exp(s - top)
        total = jnp.sum(w, axis=1, keepdims=True)
        acc = jnp.dot(w.astype(jnp.bfloat16), values_ref[:, cols], preferred_element_type=jnp.float32)
        out_ref[:, cols] = acc.astype(jnp.bfloat16)
        coarse = total.astype(jnp.bfloat16).astype(jnp.float32)
        stats = jnp.where(lane == h, top, stats)
        stats = jnp.where(lane == heads + h, coarse, stats)
        stats = jnp.where(lane == 2 * heads + h, total - coarse, stats)
    out_ref[:, width:] = stats.astype(jnp.bfloat16)


def combine_kernel(parts_ref, out_ref):
    width = out_ref.shape[2]
    heads = width // HD
    stats = parts_ref[:, :, width:].astype(jnp.float32)
    for h in range(heads):
        cols = slice(h * HD, (h + 1) * HD)
        top = stats[:, :, h : h + 1]
        factor = jnp.exp(top - jnp.max(top, axis=0, keepdims=True))
        total = stats[:, :, heads + h : heads + h + 1] + stats[:, :, 2 * heads + h : 2 * heads + h + 1]
        denominator = jnp.sum(factor * total, axis=0)
        summed = jnp.sum(factor * parts_ref[:, :, cols].astype(jnp.float32), axis=0)
        done = (summed / denominator).astype(jnp.bfloat16)
        for i in range(out_ref.shape[0]):
            out_ref[i, :, cols] = done


def project_kernel(rows_ref, near_ref, far_ref, out_ref):
    zh = lax.axis_index("zh")
    rows = rows_ref.shape[0] // 2
    half = rows // 2
    for turn, weight in enumerate((near_ref, far_ref)):
        for r in range(2):
            piece = lax.dot_general(
                rows_ref[r * rows : (r + 1) * rows, :],
                weight[...],
                (((1,), (1,)), ((), ())),
                preferred_element_type=jnp.float32,
            )
            slot = 4 * (zh ^ turn) + 2 * zh + r
            out_ref[slot, :rows, :] = piece[:, :HD].astype(jnp.bfloat16)
            tail = jnp.concatenate([piece[:half, HD:], piece[half:, HD:]], axis=1)
            out_ref[slot, rows:, :] = tail.astype(jnp.bfloat16)


def finish_kernel(steps_ref, pieces_ref, gate_ref, residual_ref, out_ref):
    step = steps_ref[lax.axis_index("span")]
    gate = gate_ref[pl.ds(step, 1), :]
    rows = residual_ref.shape[1]
    first = 4 * (lax.axis_index("head") // 2)
    total = pieces_ref[first].astype(jnp.float32)
    for head in range(1, 4):
        total = total + pieces_ref[first + head].astype(jnp.float32)
    main = total[:rows]
    tail = jnp.concatenate([total[rows:, : HD // 2], total[rows:, HD // 2 :]])
    main = (main * gate[:, :HD]).T
    tail = (tail * gate[:, HD:]).T
    out_ref[:HD, :] = (residual_ref[:HD, :].astype(jnp.float32) + main).astype(jnp.bfloat16)
    out_ref[HD:, :] = (residual_ref[HD:, :].astype(jnp.float32) + tail).astype(jnp.bfloat16)


def shards(q, k, v, block_order, valid_frames, noise_steps, gate_table, out_weight, residual):
    tokens, width = q.shape[1:]
    parts_n = lax.axis_size("y")
    nx = lax.axis_size("span")
    swap = [(0, 1), (1, 0)]
    vmem = pl.BlockSpec(memory_space=pltpu.VMEM)
    smem = pl.BlockSpec(memory_space=pltpu.SMEM)
    bf16 = jnp.bfloat16
    params = pltpu.CompilerParams(vmem_limit_bytes=48 * 1024 * 1024)

    with jax.named_scope("fetch_kv"):
        kv = jnp.concatenate([k, v])
        kv_far = lax.ppermute(kv, "zh", swap)
    with jax.named_scope("gather_q"):
        queries = lax.all_to_all(jnp.broadcast_to(q, (parts_n, tokens, width)), "y", 0, 0, tiled=True)
    with jax.named_scope("gather_kv"):
        kv = jnp.stack([kv[0], kv_far[0], kv[1], kv_far[1]])
        kv = kv.reshape(2, 2 * tokens, width)
        near = lax.all_gather(kv, "span", axis=1, tiled=True)
        keys = lax.all_gather(near[0], "core", axis=0, tiled=True)
        values = lax.all_gather(near[1], "core", axis=0, tiled=True)
    with jax.named_scope("fetch_weight"):
        weight = out_weight.T
        weight_far = lax.ppermute(weight, "zh", swap)
    parts = pl.pallas_call(
        attend_kernel,
        out_shape=jax.ShapeDtypeStruct((parts_n * tokens, width + HD), bf16),
        in_specs=[smem, smem, vmem, vmem, vmem],
        out_specs=vmem,
        compiler_params=params,
        name="attend",
    )(block_order, valid_frames, queries.reshape(parts_n * tokens, width), keys, values)
    with jax.named_scope("return_parts"):
        parts = lax.all_to_all(parts.reshape(parts_n, tokens, width + HD), "y", 0, 0, tiled=True)
    attended = pl.pallas_call(
        combine_kernel,
        out_shape=jax.ShapeDtypeStruct((parts_n, tokens, width), bf16),
        in_specs=[vmem],
        out_specs=vmem,
        compiler_params=params,
        name="combine",
    )(parts)
    with jax.named_scope("gather_attended"):
        attended = lax.all_to_all(attended, "y", 0, 0, tiled=True)
        attended = lax.all_gather(attended, "core", axis=1, tiled=True).reshape(2 * parts_n * tokens, width)
    cols = weight.shape[0]
    slot_rows = parts_n * tokens * cols // HD
    pieces = pl.pallas_call(
        project_kernel,
        out_shape=jax.ShapeDtypeStruct((8, slot_rows, HD), bf16),
        in_specs=[vmem, vmem, vmem],
        out_specs=vmem,
        compiler_params=params,
        name="project",
    )(attended, weight, weight_far)
    with jax.named_scope("sum_heads"):
        pieces = lax.all_to_all(pieces, ("zh", "head"), 0, 0, tiled=True)
    mixed = pl.pallas_call(
        finish_kernel,
        out_shape=jax.ShapeDtypeStruct(residual.shape[:0:-1], bf16),
        in_specs=[smem, vmem, vmem, vmem],
        out_specs=vmem,
        compiler_params=params,
        name="finish",
    )(noise_steps, pieces, gate_table, residual[0].T)
    return mixed.T[None]


def solution(mesh):
    fine = Mesh(mesh.devices.reshape(4, 2, 8, 2, 4), AXES)
    seq = ("zh", "y", "core")
    placed = (
        P("span", seq, "head"),
        P("span", seq, "head"),
        P("span", seq, "head"),
        P(),
        P(),
        P(),
        P(None, seq),
        P("head", seq),
        P("span", "head", seq),
    )
    return jax.shard_map(
        shards, mesh=fine, in_specs=placed, out_specs=P("span", "head", seq), check_vma=False
    )
```

time: 142 us -> 131 us (0.923)
  blocking collectives: 91.6 us -> 80.9 us
  waiting for transfers between devices: 19.1 us -> 10.6 us
  starting transfers between devices: 20.6 us -> 26.9 us
  local copies, waits for them, and re-layouts: 1.39 us -> 3.05 us
    all_to_all x3 -> x2, blocking collectives: 75.8 us -> 56.6 us  [the longest x1 31.8 us: shards(): pieces = lax.all_to_all(pieces, ('zh', 'head'), 0, 0, tiled=True)]
    all_gather x1 -> x3, blocking collectives: 12.2 us -> 20.2 us  [the longest x1 13.1 us: shards(): near = lax.all_gather(kv, 'span', axis=1, tiled=True)]
    all_to_all x1 -> x2, starting transfers between devices: 3.61 us -> 10.4 us  [the longest x1 6.82 us: shards(): lax.all_to_all(jnp.broadcast_to(q, (parts_n, tokens, width)), 'y', 0, 0,...]
    all_to_all x1 -> x2, waiting for transfers between devices: 16.8 us -> 10.6 us  [the longest x1 10.6 us: shards(): attended = lax.all_to_all(attended, 'y', 0, 0, tiled=True)]
    ppermute x3 -> x2, waiting for transfers between devices: 2.26 us -> 0.01 us  [the longest x1 0.01 us: shards(): kv_far = lax.ppermute(kv, 'zh', swap)]
    ppermute x3 -> x2, starting transfers between devices: 17 us -> 16.5 us  [the longest x1 11.5 us: shards(): kv_far = lax.ppermute(kv, 'zh', swap)]
  transfers between devices with their start and end apart: 4 -> 4, of which waited for: 2 -> 1; matrix products, arithmetic and copies ran while one was open for 0% -> 1% of each run, Pallas kernels for 0% -> 0%
where the time goes in v3:
time: 131 us; the launch traced here: 129 us
  blocking collectives  80.9 us (62%)
  starting transfers between devices  26.9 us (21%)
  waiting for transfers between devices  10.6 us (8%)
  Pallas kernels  6.94 us (5%)
  local copies, waits for them, and re-layouts  3.05 us (2%)
    all_to_all x1, blocking collectives, shards(): pieces = lax.all_to_all(pieces, ('zh', 'head'), 0, 0, tiled=True)  31.8 us
    all_to_all x1, blocking collectives, shards(): lax.all_to_all(parts.reshape(parts_n, tokens, width + HD), 'y', 0, 0, til...  24.8 us
    all_gather x1, blocking collectives, shards(): near = lax.all_gather(kv, 'span', axis=1, tiled=True)  13.1 us
    ppermute x1, starting transfers between devices, shards(): kv_far = lax.ppermute(kv, 'zh', swap)  11.5 us
    all_to_all x1, waiting for transfers between devices, shards(): attended = lax.all_to_all(attended, 'y', 0, 0, tiled=True)  10.6 us
    all_to_all x1, starting transfers between devices, shards(): lax.all_to_all(jnp.broadcast_to(q, (parts_n, tokens, width)), 'y', 0, 0,...  6.82 us
    ppermute x1, starting transfers between devices, shards(): weight_far = lax.ppermute(weight, 'zh', swap)  5.03 us
    all_gather x1, blocking collectives, shards(): keys = lax.all_gather(near[0], 'core', axis=0, tiled=True)  4.61 us
  transfers between devices with their start and end apart: 4, of which 1 were waited for; matrix products, arithmetic and copies ran while one was open for 1% of the time, Pallas kernels for 0%

profile of v3, /device:TPU:1, one launch (start us, length us, event | category | flops | bytes accessed | tf_op | source)
XLA Modules:
  0.0 129.4 jit_solution(4324723383499772989)
XLA Ops:
  0.0 0.0 copy-start.8
  0.0 0.9 pad_maximum_fusion.1
  0.9 11.5 %collective-permute-start = (bf16[2,40,768]{2,1,0:T(8,128)(2,1)S(1)}, bf16[2,40,768]{2,1,0:T(8,128)(2,1)S(1)}, u32[]{:S(2)}, u32[]{:S(2)}) collective-permute-start(bf16[2,40,768]{2,1,0:T(8,128)(2,1)S(1)} %pad_maximum_fusion.1), channel_id=1, source_target_pairs={{0,64},{64,0},{1,65},{65,1},{2,66},{66,2},{3,67},{67,3},{4,68},{68... | collective-permute-start | bytes 368648 | tf_op jit(solution)/shard_map/fetch_kv/ppermute | solution.py:118
  12.4 0.0 copy-done.8
  12.4 0.8 broadcast_in_dim.11
  13.2 6.8 %all-to-all-start = ((bf16[8,40,768]{2,1,0:T(8,128)(2,1)}), bf16[8,40,768]{2,1,0:T(8,128)(2,1)S(1)}, u32[]{:S(2)}, u32[]{:S(2)}) async-start(bf16[8,40,768]{2,1,0:T(8,128)(2,1)} %broadcast_in_dim.11), calls=%async_computation | async-start | bytes 983040 | tf_op jit(solution)/shard_map/gather_q/all_to_all | solution.py:120
  20.0 0.0 copy-start.6
  20.0 0.0 copy-start.7
  20.0 0.0 collective-permute-done
  20.0 0.8 copy-done.6
  20.8 0.0 copy-done.7
  20.9 13.1 %all_gather.12 = bf16[2,320,768]{2,1,0:T(8,128)(2,1)S(1)} all-gather(bf16[2,80,768]{2,1,0:T(8,128)(2,1)S(1)} %bitcast.22), channel_id=1, replica_groups=mesh['span'=4,'zh'=2,'y'=8,'core'=2,'head'=4] {'span'}, dimensions={1}, use_global_device_ids=true | all-gather | bytes 1228800 | tf_op jit(solution)/shard_map/gather_kv/all_gather | solution.py:124
  34.0 0.1 fusion
  34.0 4.6 %all-gather = bf16[1,640,768]{2,1,0:T(8,128)(2,1)S(1)} all-gather(bf16[1,320,768]{2,1,0:T(8,128)(2,1)S(1)} %get-tuple-element.6), channel_id=2, replica_groups=mesh['span'=4,'zh'=2,'y'=8,'core'=2,'head'=4] {'core'}, dimensions={1}, use_global_device_ids=true | all-gather | bytes 1474560 | tf_op jit(solution)/shard_map/gather_kv/all_gather | solution.py:125
  38.7 2.5 %all-gather.1 = bf16[1,640,768]{2,1,0:T(8,128)(2,1)S(1)} all-gather(bf16[1,320,768]{2,1,0:T(8,128)(2,1)S(1)} %get-tuple-element.5), channel_id=3, replica_groups=mesh['span'=4,'zh'=2,'y'=8,'core'=2,'head'=4] {'core'}, dimensions={1}, use_global_device_ids=true | all-gather | bytes 1474560 | tf_op jit(solution)/shard_map/gather_kv/all_gather | solution.py:126
  41.2 0.0 all-to-all-done
  41.2 0.0 copy-start.4
  41.2 0.0 copy-start.5
  41.2 0.7 copy-done.4
  41.8 0.0 copy-done.5
  41.8 3.4 %attend.1 = bf16[320,896]{1,0:T(8,128)(2,1)S(1)} custom-call(s32[4]{0:T(128)S(1)} %copy-done.4, s32[4]{0:T(128)S(1)} %copy-done.5, bf16[320,768]{1,0:T(8,128)(2,1)S(1)} %bitcast.18, bf16[640,768]{1,0:T(8,128)(2,1)S(1)} %bitcast.15, bf16[640,768]{1,0:T(8,128)(2,1)S(1)} %bitcast.16), custom_call_target="tpu_custom_call" | custom-call | tf_op jit(solution)/shard_map/attend/pallas_call | solution.py:130
  45.3 24.8 %all_to_all.20.parts_ref = bf16[8,40,896]{2,1,0:T(8,128)(2,1)S(1)} all-to-all(bf16[8,40,896]{2,1,0:T(8,128)(2,1)S(1)} %bitcast.17), channel_id=1, replica_groups=mesh['span'=4,'zh'=2,'y'=8,'core'=2,'head'=4] {'y'}, dimensions={0} | all-to-all | bytes 1146880 | tf_op jit(solution)/shard_map/return_parts/all_to_all | solution.py:139
  70.1 1.3 %combine.1 = bf16[8,40,768]{2,1,0:T(8,128)(2,1)} custom-call(bf16[8,40,896]{2,1,0:T(8,128)(2,1)S(1)} %all_to_all.20.parts_ref), custom_call_target="tpu_custom_call" | custom-call | tf_op jit(solution)/shard_map/combine/pallas_call | solution.py:140
  71.4 0.0 copy-start
  71.4 3.6 %all-to-all-start.2 = ((bf16[8,40,768]{2,1,0:T(8,128)(2,1)}), bf16[8,40,768]{2,1,0:T(8,128)(2,1)S(1)}, u32[]{:S(2)}, u32[]{:S(2)}) async-start(bf16[8,40,768]{2,1,0:T(8,128)(2,1)} %combine.1), calls=%async_computation.2 | async-start | bytes 983040 | tf_op jit(solution)/shard_map/gather_attended/all_to_all | solution.py:149
  75.0 0.0 copy-done
  75.0 5.0 %collective-permute-start.1 = (bf16[192,768]{1,0:T(8,128)(2,1)S(1)}, bf16[192,768]{1,0:T(8,128)(2,1)S(1)}, u32[]{:S(2)}, u32[]{:S(2)}) collective-permute-start(bf16[192,768]{1,0:T(8,128)(2,1)S(1)} %bitcast.19), channel_id=1, source_target_pairs={{0,64},{64,0},{1,65},{65,1},{2,66},{66,2},{3,67},{67,3},{4,68},{68... | collective-permute-start | bytes 884744 | tf_op jit(solution)/shard_map/fetch_weight/ppermute | solution.py:129
  80.0 10.6 %all-to-all-done.2 = bf16[8,40,768]{2,1,0:T(8,128)(2,1)S(1)} async-done(((bf16[8,40,768]{2,1,0:T(8,128)(2,1)}), bf16[8,40,768]{2,1,0:T(8,128)(2,1)S(1)}, u32[]{:S(2)}, u32[]{:S(2)}) %all-to-all-start.2) | async-done | bytes 491552 | tf_op jit(solution)/shard_map/gather_attended/all_to_all | solution.py:149
  90.7 4.1 %all_gather.15 = bf16[8,80,768]{2,1,0:T(8,128)(2,1)S(1)} all-gather(bf16[8,40,768]{2,1,0:T(8,128)(2,1)S(1)} %all-to-all-done.2), channel_id=1, replica_groups=mesh['span'=4,'zh'=2,'y'=8,'core'=2,'head'=4] {'core'}, dimensions={1}, use_global_device_ids=true | all-gather | bytes 1474560 | tf_op jit(solution)/shard_map/gather_attended/all_gather | solution.py:150
  94.8 0.0 collective-permute-done.1.far_ref
  94.8 0.8 project.1
  95.6 0.0 copy-start.1
  95.6 0.0 copy-start.2
  95.6 31.8 %all_to_all.21.pieces_ref = bf16[8,480,128]{2,1,0:T(8,128)(2,1)S(1)} all-to-all(bf16[8,480,128]{2,1,0:T(8,128)(2,1)S(1)} %project.1), channel_id=1, replica_groups=mesh['span'=4,'zh'=2,'y'=8,'core'=2,'head'=4] {'zh','head'}, dimensions={0} | all-to-all | bytes 1966080 | tf_op jit(solution)/shard_map/sum_heads/all_to_all | solution.py:162
  127.4 0.0 copy-start.3
  127.4 0.0 copy-done.1
  127.4 0.0 copy-done.2
  127.4 0.6 copy-done.3
  128.0 1.4 %finish.1 = bf16[192,320]{1,0:T(8,128)(2,1)} custom-call(s32[4]{0:T(128)S(1)} %copy-done.3, bf16[8,480,128]{2,1,0:T(8,128)(2,1)S(1)} %all_to_all.21.pieces_ref, f32[4,192]{1,0:T(4,128)S(1)} %copy-done.2, bf16[192,320]{1,0:T(8,128)(2,1)S(1)} %bitcast.21), custom_call_target="tpu_custom_call" | custom-call | tf_op jit(solution)/shard_map/finish/pallas_call | solution.py:163
  (2 shorter events, 0.0 us)
Async XLA Ops:
  0.0 12.4 %copy-start.8 = (bf16[1,40,768]{2,1,0:T(8,128)(2,1)S(1)}, bf16[1,40,768]{2,1,0:T(8,128)(2,1)}, u32[]{:S(2)}) copy-start(bf16[1,40,768]{2,1,0:T(8,128)(2,1)} %param.9) | copy-start | bytes 184324
  0.9 19.1 %collective-permute-start = (bf16[2,40,768]{2,1,0:T(8,128)(2,1)S(1)}, bf16[2,40,768]{2,1,0:T(8,128)(2,1)S(1)}, u32[]{:S(2)}, u32[]{:S(2)}) collective-permute-start(bf16[2,40,768]{2,1,0:T(8,128)(2,1)S(1)} %pad_maximum_fusion.1), channel_id=1, source_target_pairs={{0,64},{64,0},{1,65},{65,1},{2,66},{66,2},{3,67},{67,3},{4,68},{68... | collective-permute-start | bytes 368648 | tf_op jit(solution)/shard_map/fetch_kv/ppermute | solution.py:118
  13.2 28.0 %all-to-all-start = ((bf16[8,40,768]{2,1,0:T(8,128)(2,1)}), bf16[8,40,768]{2,1,0:T(8,128)(2,1)S(1)}, u32[]{:S(2)}, u32[]{:S(2)}) async-start(bf16[8,40,768]{2,1,0:T(8,128)(2,1)} %broadcast_in_dim.11), calls=%async_computation | async-start | bytes 983040 | tf_op jit(solution)/shard_map/gather_q/all_to_all | solution.py:120
  20.0 0.8 copy-start.6
  20.0 0.9 copy-start.7
  41.2 0.7 copy-start.4
  41.2 0.7 copy-start.5
  71.4 3.6 %copy-start = (bf16[768,192]{0,1:T(8,128)(2,1)S(1)}, bf16[768,192]{0,1:T(8,128)(2,1)}, u32[]{:S(2)}) copy-start(bf16[768,192]{0,1:T(8,128)(2,1)} %param.16) | copy-start | bytes 884740
  71.4 19.3 %all-to-all-start.2 = ((bf16[8,40,768]{2,1,0:T(8,128)(2,1)}), bf16[8,40,768]{2,1,0:T(8,128)(2,1)S(1)}, u32[]{:S(2)}, u32[]{:S(2)}) async-start(bf16[8,40,768]{2,1,0:T(8,128)(2,1)} %combine.1), calls=%async_computation.2 | async-start | bytes 983040 | tf_op jit(solution)/shard_map/gather_attended/all_to_all | solution.py:149
  75.0 19.8 %collective-permute-start.1 = (bf16[192,768]{1,0:T(8,128)(2,1)S(1)}, bf16[192,768]{1,0:T(8,128)(2,1)S(1)}, u32[]{:S(2)}, u32[]{:S(2)}) collective-permute-start(bf16[192,768]{1,0:T(8,128)(2,1)S(1)} %bitcast.19), channel_id=1, source_target_pairs={{0,64},{64,0},{1,65},{65,1},{2,66},{66,2},{3,67},{67,3},{4,68},{68... | collective-permute-start | bytes 884744 | tf_op jit(solution)/shard_map/fetch_weight/ppermute | solution.py:129
  95.6 31.8 %copy-start.1 = (bf16[1,320,192]{1,2,0:T(8,128)(2,1)S(1)}, bf16[1,320,192]{1,2,0:T(8,128)(2,1)}, u32[]{:S(2)}) copy-start(bf16[1,320,192]{1,2,0:T(8,128)(2,1)} %param.17) | copy-start | bytes 368644
  95.6 31.8 %copy-start.2 = (f32[4,192]{1,0:T(4,128)S(1)}, f32[4,192]{1,0:T(4,128)}, u32[]{:S(2)}) copy-start(f32[4,192]{1,0:T(4,128)} %gate_ref.1) | copy-start | bytes 9220
  127.4 0.7 copy-start.3

commit v4 on v2

--- a/solution.py
+++ b/solution.py
@@ -9,41 +9,44 @@
 CLOSED = -1e30
 LOWEST = -1e20
 AXES = ("span", "zh", "y2", "y1", "y0", "core", "head")
+ROW = ("y2", "y1", "y0")
 FRAME = ("zh", "y2", "y1")
+FRAMES = 8
 
 
-def attend_kernel(order_ref, valid_ref, q_ref, near_ref, far_ref, out_ref):
+def attend_kernel(order_ref, valid_ref, q_ref, keys_ref, values_ref, out_ref):
     blocks = order_ref.shape[0]
     rows, width = q_ref.shape
     heads = width // HD
-    slab = near_ref.shape[0] // (2 * blocks)
-    frame = lax.axis_index("zh") * 4 + lax.axis_index("y2") * 2 + lax.axis_index("y1")
+    count = keys_ref.shape[0]
+    slab = count // (2 * blocks)
+    zh = lax.axis_index("zh")
+    y = lax.axis_index("y2") * 4 + lax.axis_index("y1") * 2 + lax.axis_index("y0")
     order_here = order_ref[lax.axis_index("span")]
-    place = lax.broadcasted_iota(jnp.int32, (1, 2 * blocks * slab), 1)
+    place = lax.broadcasted_iota(jnp.int32, (1, count), 1)
     place = jnp.where(place >= blocks * slab, place - blocks * slab, place)
     bias = jnp.zeros(place.shape, jnp.float32)
     for block in range(blocks):
-        is_open = (order_ref[block] <= order_here) & (frame < valid_ref[block])
-        inside = (place >= block * slab) & (place < (block + 1) * slab)
-        bias = jnp.where(inside & jnp.logical_not(is_open), CLOSED, bias)
+        for turn in range(2):
+            frame = (zh ^ turn) * (FRAMES // 2) + y // 2
+            is_open = (order_ref[block] <= order_here) & (frame < valid_ref[block])
+            least = block * slab + turn * (slab // 2)
+            inside = (place >= least) & (place < least + slab // 2)
+            bias = jnp.where(inside & jnp.logical_not(is_open), CLOSED, bias)
     lane = lax.broadcasted_iota(jnp.int32, (rows, HD), 1)
     stats = jnp.zeros((rows, HD), jnp.float32)
     scale = 1.0 / HD**0.5
     for h in range(heads):
         cols = slice(h * HD, (h + 1) * HD)
-        k = jnp.concatenate(
-            [ref[2 * b * slab : (2 * b + 1) * slab, cols] for ref in (near_ref, far_ref) for b in range(blocks)]
+        s = lax.dot_general(
+            q_ref[:, cols], keys_ref[:, cols], (((1,), (1,)), ((), ())), preferred_element_type=jnp.float32
         )
-        v = jnp.concatenate(
-            [ref[(2 * b + 1) * slab : (2 * b + 2) * slab, cols] for ref in (near_ref, far_ref) for b in range(blocks)]
-        )
-        s = lax.dot_general(q_ref[:, cols], k, (((1,), (1,)), ((), ())), preferred_element_type=jnp.float32)
         s = s * scale + bias
         top = jnp.maximum(jnp.max(s, axis=1, keepdims=True), LOWEST)
         top = top.astype(jnp.bfloat16).astype(jnp.float32)
         w = jnp.exp(s - top)
         total = jnp.sum(w, axis=1, keepdims=True)
-        acc = jnp.dot(w.astype(jnp.bfloat16), v, preferred_element_type=jnp.float32)
+        acc = jnp.dot(w.astype(jnp.bfloat16), values_ref[:, cols], preferred_element_type=jnp.float32)
         out_ref[:, cols] = acc.astype(jnp.bfloat16)
         coarse = total.astype(jnp.bfloat16).astype(jnp.float32)
         stats = jnp.where(lane == h, top, stats)
@@ -110,7 +113,7 @@
 
 def shards(q, k, v, block_order, valid_frames, noise_steps, gate_table, out_weight, residual):
     tokens, width = q.shape[1:]
-    parts_n = 8
+    parts_n = lax.axis_size(ROW)
     nx = lax.axis_size("span")
     swap = [(0, 1), (1, 0)]
     vmem = pl.BlockSpec(memory_space=pltpu.VMEM)
@@ -120,13 +123,15 @@
 
     with jax.named_scope("fetch_kv"):
         kv = jnp.concatenate([k, v])
-        kv_far = lax.ppermute(kv, "y0", swap)
+        kv_far = lax.ppermute(kv, "zh", swap)
     with jax.named_scope("gather_q"):
-        queries = lax.all_to_all(jnp.broadcast_to(q, (parts_n, tokens, width)), FRAME, 0, 0, tiled=True)
+        queries = lax.all_to_all(jnp.broadcast_to(q, (parts_n, tokens, width)), ROW, 0, 0, tiled=True)
     with jax.named_scope("gather_kv"):
         kv = jnp.stack([kv[0], kv_far[0], kv[1], kv_far[1]])
-        near = lax.all_gather(kv, "span", axis=0, tiled=True).reshape(nx * 4 * tokens, width)
-        far = lax.ppermute(near, "core", swap)
+        kv = kv.reshape(2, 2 * tokens, width)
+        near = lax.all_gather(kv, "span", axis=1, tiled=True)
+        keys = lax.all_gather(near[0], "core", axis=0, tiled=True)
+        values = lax.all_gather(near[1], "core", axis=0, tiled=True)
     with jax.named_scope("fetch_weight"):
         weight = out_weight.T
         weight_far = lax.ppermute(weight, "y0", swap)
@@ -137,9 +142,9 @@
         out_specs=vmem,
         compiler_params=params,
         name="attend",
-    )(block_order, valid_frames, queries.reshape(parts_n * tokens, width), near, far)
+    )(block_order, valid_frames, queries.reshape(parts_n * tokens, width), keys, values)
     with jax.named_scope("return_parts"):
-        parts = lax.all_to_all(parts.reshape(parts_n, tokens, width + HD), FRAME, 0, 0, tiled=True)
+        parts = lax.all_to_all(parts.reshape(parts_n, tokens, width + HD), ROW, 0, 0, tiled=True)
     attended = pl.pallas_call(
         combine_kernel,
         out_shape=jax.ShapeDtypeStruct((parts_n, tokens, width), bf16),
@@ -176,7 +181,7 @@
 
 def solution(mesh):
     fine = Mesh(mesh.devices.reshape(4, 2, 2, 2, 2, 2, 4), AXES)
-    seq = ("zh", "y2", "y1", "y0", "core")
+    seq = ("zh",) + ROW + ("core",)
     placed = (
         P("span", seq, "head"),
         P("span", seq, "head"),

time: 142 us -> 123 us (0.87)
  blocking collectives: 91.6 us -> 69.3 us
  starting transfers between devices: 20.6 us -> 25.7 us
  waiting for transfers between devices: 19.1 us -> 15.1 us
  local copies, waits for them, and re-layouts: 1.39 us -> 3.05 us
    all_to_all x2 -> x1, blocking collectives: 59 us -> 24.8 us  [shards(): lax.all_to_all(parts.reshape(parts_n, tokens, width + HD), ROW, 0, 0, til...]
    all_gather x1 -> x3, blocking collectives: 12.2 us -> 20.2 us  [the longest x1 13.1 us: shards(): near = lax.all_gather(kv, 'span', axis=1, tiled=True)]
    all_to_all x0 -> x1, starting transfers between devices: none -> 6.82 us  [shards(): lax.all_to_all(jnp.broadcast_to(q, (parts_n, tokens, width)), ROW, 0, 0,...]
    ppermute x2 -> x1, starting transfers between devices: 15.1 us -> 11.5 us  [shards(): kv_far = lax.ppermute(kv, 'zh', swap)]
    all_gather x1, blocking collectives: 3.67 us -> 6.65 us  [shards(): lax.all_gather(attended, 'core', axis=1, tiled=True)]
    ppermute x2 -> x1, waiting for transfers between devices: 2.26 us -> 0.01 us  [shards(): kv_far = lax.ppermute(kv, 'zh', swap)]
    all_to_all x1, waiting for transfers between devices: 16.8 us -> 15.1 us  [shards(): attended = lax.all_to_all(attended, FRAME, 0, 0, tiled=True)]
  transfers between devices with their start and end apart: 4 -> 4, of which waited for: 2 -> 1; matrix products, arithmetic and copies ran while one was open for 0% -> 1% of each run, Pallas kernels for 0% -> 0%
where the time goes in v4:
time: 123 us; the launch traced here: 121 us
  blocking collectives  69.3 us (56%)
  starting transfers between devices  25.7 us (21%)
  waiting for transfers between devices  15.1 us (12%)
  Pallas kernels  7.13 us (6%)
  local copies, waits for them, and re-layouts  3.05 us (2%)
    all_to_all x1, blocking collectives, shards(): lax.all_to_all(parts.reshape(parts_n, tokens, width + HD), ROW, 0, 0, til...  24.8 us
    all_to_all x1, blocking collectives, shards(): pieces = lax.all_to_all(pieces, ('head', 'y0'), 0, 0, tiled=True)  17.6 us
    all_to_all x1, waiting for transfers between devices, shards(): attended = lax.all_to_all(attended, FRAME, 0, 0, tiled=True)  15.1 us
    all_gather x1, blocking collectives, shards(): near = lax.all_gather(kv, 'span', axis=1, tiled=True)  13.1 us
    ppermute x1, starting transfers between devices, shards(): kv_far = lax.ppermute(kv, 'zh', swap)  11.5 us
    all_to_all x1, starting transfers between devices, shards(): lax.all_to_all(jnp.broadcast_to(q, (parts_n, tokens, width)), ROW, 0, 0,...  6.82 us
    all_gather x1, blocking collectives, shards(): lax.all_gather(attended, 'core', axis=1, tiled=True)  6.65 us
    all_to_all x1, starting transfers between devices, shards(): attended = lax.all_to_all(attended, FRAME, 0, 0, tiled=True)  4.93 us
  transfers between devices with their start and end apart: 4, of which 1 were waited for; matrix products, arithmetic and copies ran while one was open for 1% of the time, Pallas kernels for 0%

profile of v4, /device:TPU:1, one launch (start us, length us, event | category | flops | bytes accessed | tf_op | source)
XLA Modules:
  0.0 121.2 jit_solution(5548473994392608577)
XLA Ops:
  0.0 0.0 copy-start.8
  0.0 0.9 pad_maximum_fusion.1
  0.9 11.5 %collective-permute-start = (bf16[2,40,768]{2,1,0:T(8,128)(2,1)S(1)}, bf16[2,40,768]{2,1,0:T(8,128)(2,1)S(1)}, u32[]{:S(2)}, u32[]{:S(2)}) collective-permute-start(bf16[2,40,768]{2,1,0:T(8,128)(2,1)S(1)} %pad_maximum_fusion.1), channel_id=1, source_target_pairs={{0,64},{64,0},{1,65},{65,1},{2,66},{66,2},{3,67},{67,3},{4,68},{68... | collective-permute-start | bytes 368648 | tf_op jit(solution)/shard_map/fetch_kv/ppermute | solution.py:126
  12.4 0.0 copy-done.8
  12.4 0.8 broadcast_in_dim.11
  13.2 6.8 %all-to-all-start = ((bf16[8,40,768]{2,1,0:T(8,128)(2,1)}), bf16[8,40,768]{2,1,0:T(8,128)(2,1)S(1)}, u32[]{:S(2)}, u32[]{:S(2)}) async-start(bf16[8,40,768]{2,1,0:T(8,128)(2,1)} %broadcast_in_dim.11), calls=%async_computation | async-start | bytes 983040 | tf_op jit(solution)/shard_map/gather_q/all_to_all | solution.py:128
  20.0 0.0 copy-start.6
  20.0 0.0 copy-start.7
  20.0 0.0 collective-permute-done
  20.0 0.8 copy-done.6
  20.8 0.0 copy-done.7
  20.9 13.1 %all_gather.12 = bf16[2,320,768]{2,1,0:T(8,128)(2,1)S(1)} all-gather(bf16[2,80,768]{2,1,0:T(8,128)(2,1)S(1)} %bitcast.22), channel_id=1, replica_groups=mesh['span'=4,'zh'=2,'y2'=2,'y1'=2,'y0'=2,'core'=2,'head'=4] {'span'}, dimensions={1}, use_global_device_ids=true | all-gather | bytes 1228800 | tf_op jit(solution)/shard_map/gather_kv/all_gather | solution.py:132
  34.0 0.1 fusion
  34.0 4.6 %all-gather = bf16[1,640,768]{2,1,0:T(8,128)(2,1)S(1)} all-gather(bf16[1,320,768]{2,1,0:T(8,128)(2,1)S(1)} %get-tuple-element.6), channel_id=2, replica_groups=mesh['span'=4,'zh'=2,'y2'=2,'y1'=2,'y0'=2,'core'=2,'head'=4] {'core'}, dimensions={1}, use_global_device_ids=true | all-gather | bytes 1474560 | tf_op jit(solution)/shard_map/gather_kv/all_gather | solution.py:133
  38.7 2.5 %all-gather.1 = bf16[1,640,768]{2,1,0:T(8,128)(2,1)S(1)} all-gather(bf16[1,320,768]{2,1,0:T(8,128)(2,1)S(1)} %get-tuple-element.5), channel_id=3, replica_groups=mesh['span'=4,'zh'=2,'y2'=2,'y1'=2,'y0'=2,'core'=2,'head'=4] {'core'}, dimensions={1}, use_global_device_ids=true | all-gather | bytes 1474560 | tf_op jit(solution)/shard_map/gather_kv/all_gather | solution.py:134
  41.2 0.0 all-to-all-done
  41.2 0.0 copy-start.4
  41.2 0.0 copy-start.5
  41.2 0.7 copy-done.4
  41.8 0.0 copy-done.5
  41.8 3.4 %attend.1 = bf16[320,896]{1,0:T(8,128)(2,1)S(1)} custom-call(s32[4]{0:T(128)S(1)} %copy-done.4, s32[4]{0:T(128)S(1)} %copy-done.5, bf16[320,768]{1,0:T(8,128)(2,1)S(1)} %bitcast.18, bf16[640,768]{1,0:T(8,128)(2,1)S(1)} %bitcast.15, bf16[640,768]{1,0:T(8,128)(2,1)S(1)} %bitcast.16), custom_call_target="tpu_custom_call" | custom-call | tf_op jit(solution)/shard_map/attend/pallas_call | solution.py:138
  45.3 24.8 %all_to_all.20.parts_ref = bf16[8,40,896]{2,1,0:T(8,128)(2,1)S(1)} all-to-all(bf16[8,40,896]{2,1,0:T(8,128)(2,1)S(1)} %bitcast.17), channel_id=1, replica_groups=mesh['span'=4,'zh'=2,'y2'=2,'y1'=2,'y0'=2,'core'=2,'head'=4] {'y2','y1',..., dimensions={0} | all-to-all | bytes 1146880 | tf_op jit(solution)/shard_map/return_parts/all_to_all | solution.py:147
  70.1 1.3 %combine.1 = bf16[8,40,768]{2,1,0:T(8,128)(2,1)} custom-call(bf16[8,40,896]{2,1,0:T(8,128)(2,1)S(1)} %all_to_all.20.parts_ref), custom_call_target="tpu_custom_call" | custom-call | tf_op jit(solution)/shard_map/combine/pallas_call | solution.py:148
  71.4 0.0 copy-start
  71.4 4.9 %all-to-all-start.2 = ((bf16[8,40,768]{2,1,0:T(8,128)(2,1)}), bf16[8,40,768]{2,1,0:T(8,128)(2,1)S(1)}, u32[]{:S(2)}, u32[]{:S(2)}) async-start(bf16[8,40,768]{2,1,0:T(8,128)(2,1)} %combine.1), calls=%async_computation.2 | async-start | bytes 983040 | tf_op jit(solution)/shard_map/gather_attended/all_to_all | solution.py:157
  76.3 0.0 copy-done
  76.3 2.4 %collective-permute-start.1 = (bf16[192,768]{1,0:T(8,128)(2,1)S(1)}, bf16[192,768]{1,0:T(8,128)(2,1)S(1)}, u32[]{:S(2)}, u32[]{:S(2)}) collective-permute-start(bf16[192,768]{1,0:T(8,128)(2,1)S(1)} %bitcast.19), channel_id=1, source_target_pairs={{0,8},{8,0},{1,9},{9,1},{2,10},{10,2},{3,11},{11,3},{4,12},{12,4},... | collective-permute-start | bytes 884744 | tf_op jit(solution)/shard_map/fetch_weight/ppermute | solution.py:137
  78.8 15.1 %all-to-all-done.2 = bf16[8,40,768]{2,1,0:T(8,128)(2,1)S(1)} async-done(((bf16[8,40,768]{2,1,0:T(8,128)(2,1)}), bf16[8,40,768]{2,1,0:T(8,128)(2,1)S(1)}, u32[]{:S(2)}, u32[]{:S(2)}) %all-to-all-start.2) | async-done | bytes 491552 | tf_op jit(solution)/shard_map/gather_attended/all_to_all | solution.py:157
  93.9 6.7 %all_gather.15 = bf16[8,80,768]{2,1,0:T(8,128)(2,1)S(1)} all-gather(bf16[8,40,768]{2,1,0:T(8,128)(2,1)S(1)} %all-to-all-done.2), channel_id=1, replica_groups=mesh['span'=4,'zh'=2,'y2'=2,'y1'=2,'y0'=2,'core'=2,'head'=4] {'core'}, dimensions={1}, use_global_device_ids=true | all-gather | bytes 1474560 | tf_op jit(solution)/shard_map/gather_attended/all_gather | solution.py:158
  100.5 0.0 collective-permute-done.1.far_ref
  100.5 1.0 project.1
  101.5 0.0 copy-start.1
  101.5 0.0 copy-start.2
  101.5 17.6 %all_to_all.21.pieces_ref = bf16[8,240,128]{2,1,0:T(8,128)(2,1)S(1)} all-to-all(bf16[8,240,128]{2,1,0:T(8,128)(2,1)S(1)} %project.1), channel_id=1, replica_groups=mesh['span'=4,'zh'=2,'y2'=2,'y1'=2,'y0'=2,'core'=2,'head'=4] {'head','y0'}, dimensions={0} | all-to-all | bytes 983040 | tf_op jit(solution)/shard_map/sum_heads/all_to_all | solution.py:170
  119.1 0.0 copy-start.3
  119.2 0.0 copy-done.1
  119.2 0.0 copy-done.2
  119.2 0.6 copy-done.3
  119.8 1.4 %finish.1 = bf16[192,320]{1,0:T(8,128)(2,1)} custom-call(s32[4]{0:T(128)S(1)} %copy-done.3, bf16[8,240,128]{2,1,0:T(8,128)(2,1)S(1)} %all_to_all.21.pieces_ref, f32[4,192]{1,0:T(4,128)S(1)} %copy-done.2, bf16[192,320]{1,0:T(8,128)(2,1)S(1)} %bitcast.21), custom_call_target="tpu_custom_call" | custom-call | tf_op jit(solution)/shard_map/finish/pallas_call | solution.py:171
  (2 shorter events, 0.0 us)
Async XLA Ops:
  0.0 12.4 %copy-start.8 = (bf16[1,40,768]{2,1,0:T(8,128)(2,1)S(1)}, bf16[1,40,768]{2,1,0:T(8,128)(2,1)}, u32[]{:S(2)}) copy-start(bf16[1,40,768]{2,1,0:T(8,128)(2,1)} %param.9) | copy-start | bytes 184324
  0.9 19.1 %collective-permute-start = (bf16[2,40,768]{2,1,0:T(8,128)(2,1)S(1)}, bf16[2,40,768]{2,1,0:T(8,128)(2,1)S(1)}, u32[]{:S(2)}, u32[]{:S(2)}) collective-permute-start(bf16[2,40,768]{2,1,0:T(8,128)(2,1)S(1)} %pad_maximum_fusion.1), channel_id=1, source_target_pairs={{0,64},{64,0},{1,65},{65,1},{2,66},{66,2},{3,67},{67,3},{4,68},{68... | collective-permute-start | bytes 368648 | tf_op jit(solution)/shard_map/fetch_kv/ppermute | solution.py:126
  13.2 28.0 %all-to-all-start = ((bf16[8,40,768]{2,1,0:T(8,128)(2,1)}), bf16[8,40,768]{2,1,0:T(8,128)(2,1)S(1)}, u32[]{:S(2)}, u32[]{:S(2)}) async-start(bf16[8,40,768]{2,1,0:T(8,128)(2,1)} %broadcast_in_dim.11), calls=%async_computation | async-start | bytes 983040 | tf_op jit(solution)/shard_map/gather_q/all_to_all | solution.py:128
  20.0 0.8 copy-start.6
  20.0 0.9 copy-start.7
  41.2 0.7 copy-start.4
  41.2 0.7 copy-start.5
  71.4 4.9 %copy-start = (bf16[768,192]{0,1:T(8,128)(2,1)S(1)}, bf16[768,192]{0,1:T(8,128)(2,1)}, u32[]{:S(2)}) copy-start(bf16[768,192]{0,1:T(8,128)(2,1)} %param.16) | copy-start | bytes 884740
  71.4 22.5 %all-to-all-start.2 = ((bf16[8,40,768]{2,1,0:T(8,128)(2,1)}), bf16[8,40,768]{2,1,0:T(8,128)(2,1)S(1)}, u32[]{:S(2)}, u32[]{:S(2)}) async-start(bf16[8,40,768]{2,1,0:T(8,128)(2,1)} %combine.1), calls=%async_computation.2 | async-start | bytes 983040 | tf_op jit(solution)/shard_map/gather_attended/all_to_all | solution.py:157
  76.3 24.2 %collective-permute-start.1 = (bf16[192,768]{1,0:T(8,128)(2,1)S(1)}, bf16[192,768]{1,0:T(8,128)(2,1)S(1)}, u32[]{:S(2)}, u32[]{:S(2)}) collective-permute-start(bf16[192,768]{1,0:T(8,128)(2,1)S(1)} %bitcast.19), channel_id=1, source_target_pairs={{0,8},{8,0},{1,9},{9,1},{2,10},{10,2},{3,11},{11,3},{4,12},{12,4},... | collective-permute-start | bytes 884744 | tf_op jit(solution)/shard_map/fetch_weight/ppermute | solution.py:137
  101.5 17.7 %copy-start.1 = (bf16[1,320,192]{1,2,0:T(8,128)(2,1)S(1)}, bf16[1,320,192]{1,2,0:T(8,128)(2,1)}, u32[]{:S(2)}) copy-start(bf16[1,320,192]{1,2,0:T(8,128)(2,1)} %param.17) | copy-start | bytes 368644
  101.5 17.7 %copy-start.2 = (f32[4,192]{1,0:T(4,128)S(1)}, f32[4,192]{1,0:T(4,128)}, u32[]{:S(2)}) copy-start(f32[4,192]{1,0:T(4,128)} %gate_ref.1) | copy-start | bytes 9220
  119.1 0.7 copy-start.3

commit v5 on v2

v5 whole, which is shorter than its diff:
```python
import jax
import jax.numpy as jnp
from jax import lax
from jax.experimental import pallas as pl
from jax.experimental.pallas import tpu as pltpu
from jax.sharding import Mesh, PartitionSpec as P

HD = 128
CLOSED = -1e30
LOWEST = -1e20
AXES = ("span", "zh", "y2", "y1", "y0", "core", "head")
ROW = ("y2", "y1", "y0")
FRAME = ("zh", "y2", "y1")
FRAMES = 8


def pack_kernel(q_ref, k_ref, v_ref, out_ref):
    heads = q_ref.shape[1] // HD
    for h in range(out_ref.shape[0]):
        for i, ref in enumerate((q_ref, k_ref, v_ref)):
            if h < heads:
                out_ref[h, i] = ref[:, h * HD : (h + 1) * HD]
            else:
                out_ref[h, i] = jnp.zeros(out_ref.shape[2:], out_ref.dtype)


def attend_kernel(order_ref, valid_ref, q_ref, near_ref, far_ref, out_ref):
    blocks, rows = q_ref.shape[:2]
    zh = lax.axis_index("zh")
    span = lax.axis_index("span")
    keys = jnp.concatenate([ref[i] for ref in (near_ref, far_ref) for i in (0, 2)])
    values = jnp.concatenate([ref[i] for ref in (near_ref, far_ref) for i in (1, 3)])
    place = lax.broadcasted_iota(jnp.int32, (1, 4 * rows), 1)
    inner = place
    for i in range(1, 4):
        inner = jnp.where(place >= i * rows, place - i * rows, inner)
    half = FRAMES // 2
    frame_rows = rows // half
    near_limit = (valid_ref[span] - half * zh) * frame_rows
    far_limit = (valid_ref[span] - half * (1 - zh)) * frame_rows
    limit = jnp.where(place < 2 * rows, near_limit, far_limit)
    bias = jnp.where(inner < limit, 0.0, CLOSED)
    lane = lax.broadcasted_iota(jnp.int32, (rows, HD), 1)
    scale = 1.0 / HD**0.5
    for block in range(blocks):
        is_open = order_ref[span] <= order_ref[block]

        @pl.when(is_open)
        def _():
            s = lax.dot_general(q_ref[block], keys, (((1,), (1,)), ((), ())), preferred_element_type=jnp.float32)
            s = s * scale + bias
            top = jnp.maximum(jnp.max(s, axis=1, keepdims=True), LOWEST)
            top = top.astype(jnp.bfloat16).astype(jnp.float32)
            w = jnp.exp(s - top)
            total = jnp.sum(w, axis=1, keepdims=True)
            acc = jnp.dot(w.astype(jnp.bfloat16), values, preferred_element_type=jnp.float32)
            coarse = total.astype(jnp.bfloat16).astype(jnp.float32)
            stats = jnp.where(lane == 0, top, jnp.where(lane == 1, coarse, total - coarse))
            out_ref[block, :, :HD] = acc.astype(jnp.bfloat16)
            out_ref[block, :, HD:] = stats.astype(jnp.bfloat16)

        @pl.when(jnp.logical_not(is_open))
        def _():
            out_ref[block, :, :HD] = jnp.zeros((rows, HD), jnp.bfloat16)
            out_ref[block, :, HD:] = jnp.where(lane == 0, LOWEST, 0.0).astype(jnp.bfloat16)


def combine_kernel(parts_ref, near_ref, send_ref):
    stats = parts_ref[:, :, HD:].astype(jnp.float32)
    top = stats[:, :, 0:1]
    factor = jnp.exp(top - jnp.max(top, axis=0, keepdims=True))
    denominator = jnp.sum(factor * (stats[:, :, 1:2] + stats[:, :, 2:3]), axis=0)
    summed = jnp.sum(factor * parts_ref[:, :, :HD].astype(jnp.float32), axis=0)
    done = summed / denominator
    tokens = done.shape[0] // FRAMES
    for y0 in range(2):
        piece = jnp.concatenate([done[(2 * i + y0) * tokens : (2 * i + y0 + 1) * tokens] for i in range(FRAMES // 2)])
        piece = piece.astype(jnp.bfloat16)
        send_ref[y0] = piece
        for i in range(FRAMES // 2):
            near_ref[2 * i + y0] = piece


def project_kernel(near_rows_ref, far_rows_ref, near_ref, far_ref, out_ref):
    zh = lax.axis_index("zh")
    y0 = lax.axis_index("y0")
    heads = near_ref.shape[1] // HD
    slots = near_rows_ref.shape[0] // 2
    rows = near_rows_ref.shape[1]
    quarter = rows // 4
    for side, rows_ref in enumerate((near_rows_ref, far_rows_ref)):
        left = [jnp.concatenate([rows_ref[c * slots + h] for h in range(heads)], axis=1) for c in range(2)]
        for turn, weight in enumerate((near_ref, far_ref)):
            first, second = [
                lax.dot_general(part, weight[...], (((1,), (1,)), ((), ())), preferred_element_type=jnp.float32)
                for part in left
            ]
            for y2 in range(2):
                a, b = 2 * y2 * quarter, (2 * y2 + 1) * quarter
                piece = jnp.concatenate(
                    [first[a : a + quarter], second[a : a + quarter], first[b : b + quarter], second[b : b + quarter]]
                )
                slot = (2 * (zh ^ side) + y2) * 2 + (y0 ^ turn)
                out_ref[slot, :rows, :] = piece[:, :HD].astype(jnp.bfloat16)
                tail = jnp.concatenate([piece[: rows // 2, HD:], piece[rows // 2 :, HD:]], axis=1)
                out_ref[slot, rows:, :] = tail.astype(jnp.bfloat16)


def finish_kernel(steps_ref, pieces_ref, gate_ref, residual_ref, out_ref):
    step = steps_ref[lax.axis_index("span")]
    gate = gate_ref[pl.ds(step, 1), :]
    rows = residual_ref.shape[1] // 2
    half = rows // 2
    sums = []
    for y0 in range(2):
        total = pieces_ref[y0].astype(jnp.float32)
        for head in range(1, 4):
            total = total + pieces_ref[2 * head + y0].astype(jnp.float32)
        sums.append(total)
    near, far = sums
    main = jnp.concatenate([near[:half], far[:half], near[half:rows], far[half:rows]])
    rest = HD // 2
    tail = jnp.concatenate([near[rows:, :rest], far[rows:, :rest], near[rows:, rest:], far[rows:, rest:]])
    main = (main * gate[:, :HD]).T
    tail = (tail * gate[:, HD:]).T
    out_ref[:HD, :] = (residual_ref[:HD, :].astype(jnp.float32) + main).astype(jnp.bfloat16)
    out_ref[HD:, :] = (residual_ref[HD:, :].astype(jnp.float32) + tail).astype(jnp.bfloat16)


def shards(q, k, v, block_order, valid_frames, noise_steps, gate_table, out_weight, residual):
    tokens, width = q.shape[1:]
    ny = lax.axis_size(ROW)
    nx = lax.axis_size("span")
    rows = ny * tokens
    swap = [(0, 1), (1, 0)]
    vmem = pl.BlockSpec(memory_space=pltpu.VMEM)
    smem = pl.BlockSpec(memory_space=pltpu.SMEM)
    bf16 = jnp.bfloat16
    params = pltpu.CompilerParams(vmem_limit_bytes=48 * 1024 * 1024)

    def call(kernel, shapes, in_specs, name):
        shapes = [jax.ShapeDtypeStruct(shape, bf16) for shape in shapes]
        return pl.pallas_call(
            kernel,
            out_shape=shapes if len(shapes) > 1 else shapes[0],
            in_specs=in_specs,
            out_specs=[vmem] * len(shapes) if len(shapes) > 1 else vmem,
            compiler_params=params,
            name=name,
        )

    packed = call(pack_kernel, [(ny, 3, tokens, HD)], [vmem] * 3, "pack")(q[0], k[0], v[0])
    with jax.named_scope("exchange_heads"):
        packed = lax.all_to_all(packed, ROW, 0, 0, tiled=True)
    with jax.named_scope("gather_q"):
        queries = jnp.broadcast_to(packed[:, 0].reshape(1, rows, HD), (nx, rows, HD))
        queries = lax.all_to_all(queries, "span", 0, 0, tiled=True)
    with jax.named_scope("gather_kv"):
        kv = jnp.swapaxes(packed[:, 1:], 0, 1).reshape(2, rows, HD)
        kv_far = lax.ppermute(kv, "zh", swap)
        near = lax.all_gather(kv, "core", axis=0, tiled=True)
        far = lax.all_gather(kv_far, "core", axis=0, tiled=True)
    with jax.named_scope("fetch_weight"):
        weight = out_weight.T
        weight_far = lax.ppermute(weight, "y0", swap)
    parts = call(attend_kernel, [(nx, rows, 2 * HD)], [smem, smem, vmem, vmem, vmem], "attend")(
        block_order, valid_frames, queries, near, far
    )
    with jax.named_scope("return_parts"):
        parts = lax.all_to_all(parts, "span", 0, 0, tiled=True)
    near, send = call(combine_kernel, [(ny, rows // 2, HD), (2, rows // 2, HD)], [vmem], "combine")(parts)
    with jax.named_scope("gather_attended"):
        far = lax.ppermute(send, "zh", swap)
        near = lax.all_to_all(near, ROW, 0, 0, tiled=True)
        far = jnp.broadcast_to(far, (ny // 2,) + far.shape).reshape(ny, rows // 2, HD)
        far = lax.all_to_all(far, ROW, 0, 0, tiled=True)
        near, far = lax.optimization_barrier((near, far))
        near = lax.all_gather(near, "core", axis=0, tiled=True)
        far = lax.all_gather(far, "core", axis=0, tiled=True)
    cols = weight.shape[0]
    pieces = call(project_kernel, [(8, 4 * tokens * cols // HD, HD)], [vmem] * 4, "project")(
        near, far, weight, weight_far
    )
    with jax.named_scope("sum_heads"):
        pieces = lax.all_to_all(pieces, ("head", "y0"), 0, 0, tiled=True)
    mixed = pl.pallas_call(
        finish_kernel,
        out_shape=jax.ShapeDtypeStruct(residual.shape[:0:-1], bf16),
        in_specs=[smem, vmem, vmem, vmem],
        out_specs=vmem,
        compiler_params=params,
        name="finish",
    )(noise_steps, pieces, gate_table, residual[0].T)
    return mixed.T[None]


def solution(mesh):
    fine = Mesh(mesh.devices.reshape(4, 2, 2, 2, 2, 2, 4), AXES)
    seq = ("zh",) + ROW + ("core",)
    placed = (
        P("span", seq, "head"),
        P("span", seq, "head"),
        P("span", seq, "head"),
        P(),
        P(),
        P(),
        P(None, seq),
        P("head", seq),
        P("span", "head", seq),
    )
    return jax.shard_map(
        shards, mesh=fine, in_specs=placed, out_specs=P("span", "head", seq), check_vma=False
    )
```

time: 142 us -> 124 us (0.87)
  blocking collectives: 91.6 us -> 64.3 us
  starting transfers between devices: 20.6 us -> 35.2 us
  waiting for transfers between devices: 19.1 us -> 9.78 us
  local copies, waits for them, and re-layouts: 1.39 us -> 4.74 us
    all_to_all x2, blocking collectives: 59 us -> 29.1 us  [the longest x1 16.5 us: shards(): packed = lax.all_to_all(packed, ROW, 0, 0, tiled=True)]
    all_to_all x1 -> x3, starting transfers between devices: 3.61 us -> 13.3 us  [the longest x1 5.82 us: shards(): far = lax.all_to_all(far, ROW, 0, 0, tiled=True)]
    all_to_all x1 -> x3, waiting for transfers between devices: 16.8 us -> 7.56 us  [the longest x1 6.69 us: shards(): far = lax.all_to_all(far, ROW, 0, 0, tiled=True)]
    ppermute x2, starting transfers between devices: 15.1 us -> 18.6 us  [the longest x1 11.6 us: shards(): kv_far = lax.ppermute(kv, 'zh', swap)]
    all_gather x2 -> x4, blocking collectives: 15.8 us -> 18.5 us  [the longest x1 9.33 us: shards(): near = lax.all_gather(near, 'core', axis=0, tiled=True)]
    unnamed x18, local copies, waits for them, and re-layouts: 1.35 us -> 3.16 us
    broadcast_in_dim x1 -> x2, local copies, waits for them, and re-layouts: 0.03 us -> 1.54 us  [the longest x1 0.77 us: shards(): jnp.broadcast_to(packed[:, 0].reshape(1, rows, HD), (nx, rows, HD))]
    ppermute x1, starting transfers between devices: 1.92 us -> 3.36 us  [shards(): weight_far = lax.ppermute(weight, 'y0', swap)]
  transfers between devices with their start and end apart: 4 -> 6, of which waited for: 2 -> 3; matrix products, arithmetic and copies ran while one was open for 0% -> 1% of each run, Pallas kernels for 0% -> 0%
where the time goes in v5:
time: 124 us; the launch traced here: 122 us
  blocking collectives  64.3 us (52%)
  starting transfers between devices  35.2 us (28%)
  waiting for transfers between devices  9.78 us (8%)
  Pallas kernels  8.17 us (7%)
  local copies, waits for them, and re-layouts  4.74 us (4%)
    all_to_all x1, blocking collectives, shards(): pieces = lax.all_to_all(pieces, ('head', 'y0'), 0, 0, tiled=True)  16.7 us
    all_to_all x1, blocking collectives, shards(): packed = lax.all_to_all(packed, ROW, 0, 0, tiled=True)  16.5 us
    all_to_all x1, blocking collectives, shards(): parts = lax.all_to_all(parts, 'span', 0, 0, tiled=True)  12.7 us
    ppermute x1, starting transfers between devices, shards(): kv_far = lax.ppermute(kv, 'zh', swap)  11.6 us
    all_gather x1, blocking collectives, shards(): near = lax.all_gather(near, 'core', axis=0, tiled=True)  9.33 us
    ppermute x1, starting transfers between devices, shards(): far = lax.ppermute(send, 'zh', swap)  6.96 us
    all_to_all x1, waiting for transfers between devices, shards(): far = lax.all_to_all(far, ROW, 0, 0, tiled=True)  6.69 us
    all_to_all x1, starting transfers between devices, shards(): far = lax.all_to_all(far, ROW, 0, 0, tiled=True)  5.82 us
  transfers between devices with their start and end apart: 6, of which 3 were waited for; matrix products, arithmetic and copies ran while one was open for 1% of the time, Pallas kernels for 0%

profile of v5, /device:TPU:1, one launch (start us, length us, event | category | flops | bytes accessed | tf_op | source)
XLA Modules:
  0.0 122.3 jit_solution(16792508816456045513)
XLA Ops:
  0.0 0.0 copy-start.2
  0.0 0.8 copy-done.2
  0.8 0.0 copy-start.3
  0.8 0.8 copy-done.3
  1.7 0.0 copy-start.4
  1.7 0.8 copy-done.4
  2.5 16.5 %all_to_all.30 = bf16[8,3,40,128]{3,2,1,0:T(8,128)(2,1)S(1)} all-to-all(bf16[8,3,40,128]{3,2,1,0:T(8,128)(2,1)S(1)} %pack.1), channel_id=1, replica_groups=mesh['span'=4,'zh'=2,'y2'=2,'y1'=2,'y0'=2,'core'=2,'head'=4] {'y2','y1',..., dimensions={0} | all-to-all | bytes 491520 | tf_op jit(solution)/shard_map/exchange_heads/all_to_all | solution.py:154
  19.0 11.6 %collective-permute-start = (bf16[2,320,128]{2,1,0:T(8,128)(2,1)S(1)}, bf16[2,320,128]{2,1,0:T(8,128)(2,1)S(1)}, u32[]{:S(2)}, u32[]{:S(2)}) collective-permute-start(bf16[2,320,128]{2,1,0:T(8,128)(2,1)S(1)} %bitcast.21), channel_id=1, source_target_pairs={{0,64},{64,0},{1,65},{65,1},{2,66},{66,2},{3,67},{67,3},{4,68},{68... | collective-permute-start | bytes 491528 | tf_op jit(solution)/shard_map/gather_kv/ppermute | solution.py:160
  30.7 0.8 broadcast_in_dim.14
  31.4 4.0 %all-to-all-start.1 = ((bf16[4,320,128]{2,1,0:T(8,128)(2,1)}), bf16[4,320,128]{2,1,0:T(8,128)(2,1)S(1)}, u32[]{:S(2)}, u32[]{:S(2)}) async-start(bf16[4,320,128]{2,1,0:T(8,128)(2,1)} %broadcast_in_dim.14), calls=%async_computation.1 | async-start | bytes 655360 | tf_op jit(solution)/shard_map/gather_q/all_to_all | solution.py:157
  35.5 4.7 %all_gather.12.near_ref = bf16[4,320,128]{2,1,0:T(8,128)(2,1)S(1)} all-gather(bf16[2,320,128]{2,1,0:T(8,128)(2,1)S(1)} %bitcast.22), channel_id=1, replica_groups=mesh['span'=4,'zh'=2,'y2'=2,'y1'=2,'y0'=2,'core'=2,'head'=4] {'core'}, dimensions={0}, use_global_device_ids=true | all-gather | bytes 491520 | tf_op jit(solution)/shard_map/gather_kv/all_gather | solution.py:161
  40.2 0.0 copy-start.6
  40.2 0.0 copy-start.7
  40.2 0.0 collective-permute-done
  40.2 2.2 %all_gather.13.far_ref = bf16[4,320,128]{2,1,0:T(8,128)(2,1)S(1)} all-gather(bf16[2,320,128]{2,1,0:T(8,128)(2,1)S(1)} %collective-permute-done), channel_id=1, replica_groups=mesh['span'=4,'zh'=2,'y2'=2,'y1'=2,'y0'=2,'core'=2,'head'=4] {'core'}, dimensions={0}, use_global_device_ids=true | all-gather | bytes 491520 | tf_op jit(solution)/shard_map/gather_kv/all_gather | solution.py:162
  42.3 0.0 all-to-all-done.1.q_ref
  42.3 0.0 copy-done.6
  42.3 0.0 copy-done.7
  42.4 4.5 %attend.1 = bf16[4,320,256]{2,1,0:T(8,128)(2,1)S(1)} custom-call(s32[4]{0:T(128)S(1)} %copy-done.6, s32[4]{0:T(128)S(1)} %copy-done.7, bf16[4,320,128]{2,1,0:T(8,128)(2,1)S(1)} %all-to-all-done.1.q_ref, bf16[4,320,128]{2,1,0:T(8,128)(2,1)S(1)} %all_gather.12.near_ref, bf16[4,320,128]{2,1,0:T(8,128)(2,1)S(1)} %all_gather.13.far_ref), custom_call_target="tpu_custom_call" | custom-call | tf_op jit(solution)/shard_map/attend/pallas_call | solution.py:166
  46.8 12.7 %all_to_all.31.parts_ref = bf16[4,320,256]{2,1,0:T(8,128)(2,1)S(1)} all-to-all(bf16[4,320,256]{2,1,0:T(8,128)(2,1)S(1)} %attend.1), channel_id=1, replica_groups=mesh['span'=4,'zh'=2,'y2'=2,'y1'=2,'y0'=2,'core'=2,'head'=4] {'span'}, dimensions={0} | all-to-all | bytes 1310720 | tf_op jit(solution)/shard_map/return_parts/all_to_all | solution.py:170
  59.5 1.3 %combine.1 = (bf16[8,160,128]{2,1,0:T(8,128)(2,1)}, bf16[2,160,128]{2,1,0:T(8,128)(2,1)S(1)}) custom-call(bf16[4,320,256]{2,1,0:T(8,128)(2,1)S(1)} %all_to_all.31.parts_ref), custom_call_target="tpu_custom_call" | custom-call | tf_op jit(solution)/shard_map/combine/pallas_call | solution.py:171
  60.8 3.4 %all-to-all-start.3 = ((bf16[8,160,128]{2,1,0:T(8,128)(2,1)}), bf16[8,160,128]{2,1,0:T(8,128)(2,1)S(1)}, u32[]{:S(2)}, u32[]{:S(2)}) async-start(bf16[8,160,128]{2,1,0:T(8,128)(2,1)} %get-tuple-element.9), calls=%async_computation.3 | async-start | bytes 655360 | tf_op jit(solution)/shard_map/gather_attended/all_to_all | solution.py:174
  64.2 7.0 %collective-permute-start.1 = (bf16[2,160,128]{2,1,0:T(8,128)(2,1)S(1)}, bf16[2,160,128]{2,1,0:T(8,128)(2,1)S(1)}, u32[]{:S(2)}, u32[]{:S(2)}) collective-permute-start(bf16[2,160,128]{2,1,0:T(8,128)(2,1)S(1)} %get-tuple-element.10), channel_id=1, source_target_pairs={{0,64},{64,0},{1,65},{65,1},{2,66},{66,2},{3,67},{67,3},{4,68},{68... | collective-permute-start | bytes 245768 | tf_op jit(solution)/shard_map/gather_attended/ppermute | solution.py:173
  71.2 2.2 %collective-permute-done.1 = bf16[2,160,128]{2,1,0:T(8,128)(2,1)S(1)} collective-permute-done((bf16[2,160,128]{2,1,0:T(8,128)(2,1)S(1)}, bf16[2,160,128]{2,1,0:T(8,128)(2,1)S(1)}, u32[]{:S(2)}, u32[]{:S(2)}) %collective-permute-start.1) | collective-permute-done | bytes 81952 | tf_op jit(solution)/shard_map/gather_attended/ppermute | solution.py:173
  73.4 0.9 all-to-all-done.3
  74.3 0.8 broadcast_in_dim.15
  75.0 0.0 copy-start
  75.1 5.8 %all-to-all-start.4 = ((bf16[8,160,128]{2,1,0:T(8,128)(2,1)}), bf16[8,160,128]{2,1,0:T(8,128)(2,1)S(1)}, u32[]{:S(2)}, u32[]{:S(2)}) async-start(bf16[8,160,128]{2,1,0:T(8,128)(2,1)} %bitcast.6), calls=%async_computation.4 | async-start | bytes 655360 | tf_op jit(solution)/shard_map/gather_attended/all_to_all | solution.py:176
  80.9 0.0 copy-done
  80.9 3.4 %collective-permute-start.2 = (bf16[192,768]{1,0:T(8,128)(2,1)S(1)}, bf16[192,768]{1,0:T(8,128)(2,1)S(1)}, u32[]{:S(2)}, u32[]{:S(2)}) collective-permute-start(bf16[192,768]{1,0:T(8,128)(2,1)S(1)} %bitcast.15), channel_id=1, source_target_pairs={{0,8},{8,0},{1,9},{9,1},{2,10},{10,2},{3,11},{11,3},{4,12},{12,4},... | collective-permute-start | bytes 884744 | tf_op jit(solution)/shard_map/fetch_weight/ppermute | solution.py:165
  84.2 6.7 %all-to-all-done.4 = bf16[8,160,128]{2,1,0:T(8,128)(2,1)S(1)} async-done(((bf16[8,160,128]{2,1,0:T(8,128)(2,1)}), bf16[8,160,128]{2,1,0:T(8,128)(2,1)S(1)}, u32[]{:S(2)}, u32[]{:S(2)}) %all-to-all-start.4) | async-done | bytes 327712 | tf_op jit(solution)/shard_map/gather_attended/all_to_all | solution.py:176
  90.9 9.3 %all_gather.14.near_rows_ref = bf16[16,160,128]{2,1,0:T(8,128)(2,1)S(1)} all-gather(bf16[8,160,128]{2,1,0:T(8,128)(2,1)S(1)} %all-to-all-done.3), channel_id=1, replica_groups=mesh['span'=4,'zh'=2,'y2'=2,'y1'=2,'y0'=2,'core'=2,'head'=4] {'core'}, dimensions={0}, use_global_device_ids=true | all-gather | bytes 983040 | tf_op jit(solution)/shard_map/gather_attended/all_gather | solution.py:178
  100.3 2.3 %all_gather.15.far_rows_ref = bf16[16,160,128]{2,1,0:T(8,128)(2,1)S(1)} all-gather(bf16[8,160,128]{2,1,0:T(8,128)(2,1)S(1)} %all-to-all-done.4), channel_id=1, replica_groups=mesh['span'=4,'zh'=2,'y2'=2,'y1'=2,'y0'=2,'core'=2,'head'=4] {'core'}, dimensions={0}, use_global_device_ids=true | all-gather | bytes 983040 | tf_op jit(solution)/shard_map/gather_attended/all_gather | solution.py:179
  102.5 0.0 collective-permute-done.2.far_ref
  102.5 1.0 project.1
  103.5 0.0 copy-start.1
  103.5 0.0 copy-start.5
  103.5 16.7 %all_to_all.32.pieces_ref = bf16[8,240,128]{2,1,0:T(8,128)(2,1)S(1)} all-to-all(bf16[8,240,128]{2,1,0:T(8,128)(2,1)S(1)} %project.1), channel_id=1, replica_groups=mesh['span'=4,'zh'=2,'y2'=2,'y1'=2,'y0'=2,'core'=2,'head'=4] {'head','y0'}, dimensions={0} | all-to-all | bytes 983040 | tf_op jit(solution)/shard_map/sum_heads/all_to_all | solution.py:185
  120.3 0.0 copy-start.8
  120.3 0.0 copy-done.1
  120.3 0.0 copy-done.5
  120.3 0.6 copy-done.8
  120.9 1.4 %finish.1 = bf16[192,320]{1,0:T(8,128)(2,1)} custom-call(s32[4]{0:T(128)S(1)} %copy-done.8, bf16[8,240,128]{2,1,0:T(8,128)(2,1)S(1)} %all_to_all.32.pieces_ref, f32[4,192]{1,0:T(4,128)S(1)} %copy-done.5, bf16[192,320]{1,0:T(8,128)(2,1)S(1)} %bitcast.17), custom_call_target="tpu_custom_call" | custom-call | tf_op jit(solution)/shard_map/finish/pallas_call | solution.py:186
  (4 shorter events, 0.1 us)
Async XLA Ops:
  0.0 0.8 copy-start.2
  0.8 0.8 copy-start.3
  1.7 0.8 copy-start.4
  19.0 21.1 %collective-permute-start = (bf16[2,320,128]{2,1,0:T(8,128)(2,1)S(1)}, bf16[2,320,128]{2,1,0:T(8,128)(2,1)S(1)}, u32[]{:S(2)}, u32[]{:S(2)}) collective-permute-start(bf16[2,320,128]{2,1,0:T(8,128)(2,1)S(1)} %bitcast.21), channel_id=1, source_target_pairs={{0,64},{64,0},{1,65},{65,1},{2,66},{66,2},{3,67},{67,3},{4,68},{68... | collective-permute-start | bytes 491528 | tf_op jit(solution)/shard_map/gather_kv/ppermute | solution.py:160
  31.4 10.9 %all-to-all-start.1 = ((bf16[4,320,128]{2,1,0:T(8,128)(2,1)}), bf16[4,320,128]{2,1,0:T(8,128)(2,1)S(1)}, u32[]{:S(2)}, u32[]{:S(2)}) async-start(bf16[4,320,128]{2,1,0:T(8,128)(2,1)} %broadcast_in_dim.14), calls=%async_computation.1 | async-start | bytes 655360 | tf_op jit(solution)/shard_map/gather_q/all_to_all | solution.py:157
  40.2 2.2 %copy-start.6 = (s32[4]{0:T(128)S(1)}, s32[4]{0:T(128)}, u32[]{:S(2)}) copy-start(s32[4]{0:T(128)} %order_ref.1) | copy-start | bytes 52
  40.2 2.2 %copy-start.7 = (s32[4]{0:T(128)S(1)}, s32[4]{0:T(128)}, u32[]{:S(2)}) copy-start(s32[4]{0:T(128)} %valid_ref.1) | copy-start | bytes 52
  60.8 13.5 %all-to-all-start.3 = ((bf16[8,160,128]{2,1,0:T(8,128)(2,1)}), bf16[8,160,128]{2,1,0:T(8,128)(2,1)S(1)}, u32[]{:S(2)}, u32[]{:S(2)}) async-start(bf16[8,160,128]{2,1,0:T(8,128)(2,1)} %get-tuple-element.9), calls=%async_computation.3 | async-start | bytes 655360 | tf_op jit(solution)/shard_map/gather_attended/all_to_all | solution.py:174
  64.2 9.2 %collective-permute-start.1 = (bf16[2,160,128]{2,1,0:T(8,128)(2,1)S(1)}, bf16[2,160,128]{2,1,0:T(8,128)(2,1)S(1)}, u32[]{:S(2)}, u32[]{:S(2)}) collective-permute-start(bf16[2,160,128]{2,1,0:T(8,128)(2,1)S(1)} %get-tuple-element.10), channel_id=1, source_target_pairs={{0,64},{64,0},{1,65},{65,1},{2,66},{66,2},{3,67},{67,3},{4,68},{68... | collective-permute-start | bytes 245768 | tf_op jit(solution)/shard_map/gather_attended/ppermute | solution.py:173
  75.0 5.8 %copy-start = (bf16[768,192]{0,1:T(8,128)(2,1)S(1)}, bf16[768,192]{0,1:T(8,128)(2,1)}, u32[]{:S(2)}) copy-start(bf16[768,192]{0,1:T(8,128)(2,1)} %param.16) | copy-start | bytes 884740
  75.1 15.9 %all-to-all-start.4 = ((bf16[8,160,128]{2,1,0:T(8,128)(2,1)}), bf16[8,160,128]{2,1,0:T(8,128)(2,1)S(1)}, u32[]{:S(2)}, u32[]{:S(2)}) async-start(bf16[8,160,128]{2,1,0:T(8,128)(2,1)} %bitcast.6), calls=%async_computation.4 | async-start | bytes 655360 | tf_op jit(solution)/shard_map/gather_attended/all_to_all | solution.py:176
  80.9 21.7 %collective-permute-start.2 = (bf16[192,768]{1,0:T(8,128)(2,1)S(1)}, bf16[192,768]{1,0:T(8,128)(2,1)S(1)}, u32[]{:S(2)}, u32[]{:S(2)}) collective-permute-start(bf16[192,768]{1,0:T(8,128)(2,1)S(1)} %bitcast.15), channel_id=1, source_target_pairs={{0,8},{8,0},{1,9},{9,1},{2,10},{10,2},{3,11},{11,3},{4,12},{12,4},... | collective-permute-start | bytes 884744 | tf_op jit(solution)/shard_map/fetch_weight/ppermute | solution.py:165
  103.5 16.7 %copy-start.1 = (bf16[1,320,192]{1,2,0:T(8,128)(2,1)S(1)}, bf16[1,320,192]{1,2,0:T(8,128)(2,1)}, u32[]{:S(2)}) copy-start(bf16[1,320,192]{1,2,0:T(8,128)(2,1)} %param.17) | copy-start | bytes 368644
  103.5 16.7 %copy-start.5 = (f32[4,192]{1,0:T(4,128)S(1)}, f32[4,192]{1,0:T(4,128)}, u32[]{:S(2)}) copy-start(f32[4,192]{1,0:T(4,128)} %gate_ref.1) | copy-start | bytes 9220
  120.3 0.7 copy-start.8

commit v6 on v5

--- a/solution.py
+++ b/solution.py
@@ -1,3 +1,5 @@
+import math
+
 import jax
 import jax.numpy as jnp
 from jax import lax
@@ -22,6 +24,14 @@
                 out_ref[h, i] = ref[:, h * HD : (h + 1) * HD]
             else:
                 out_ref[h, i] = jnp.zeros(out_ref.shape[2:], out_ref.dtype)
+
+
+def unpack_kernel(packed_ref, queries_ref, kv_ref):
+    for y in range(packed_ref.shape[0]):
+        for i in range(queries_ref.shape[0]):
+            queries_ref[i, y] = packed_ref[y, 0]
+        for i in range(2):
+            kv_ref[i, y] = packed_ref[y, 1 + i]
 
 
 def attend_kernel(order_ref, valid_ref, q_ref, near_ref, far_ref, out_ref):
@@ -41,55 +51,49 @@
     limit = jnp.where(place < 2 * rows, near_limit, far_limit)
     bias = jnp.where(inner < limit, 0.0, CLOSED)
     lane = lax.broadcasted_iota(jnp.int32, (rows, HD), 1)
-    scale = 1.0 / HD**0.5
+    scale = math.log2(math.e) / HD**0.5
     for block in range(blocks):
-        is_open = order_ref[span] <= order_ref[block]
-
-        @pl.when(is_open)
-        def _():
-            s = lax.dot_general(q_ref[block], keys, (((1,), (1,)), ((), ())), preferred_element_type=jnp.float32)
-            s = s * scale + bias
-            top = jnp.maximum(jnp.max(s, axis=1, keepdims=True), LOWEST)
-            top = top.astype(jnp.bfloat16).astype(jnp.float32)
-            w = jnp.exp(s - top)
-            total = jnp.sum(w, axis=1, keepdims=True)
-            acc = jnp.dot(w.astype(jnp.bfloat16), values, preferred_element_type=jnp.float32)
-            coarse = total.astype(jnp.bfloat16).astype(jnp.float32)
-            stats = jnp.where(lane == 0, top, jnp.where(lane == 1, coarse, total - coarse))
-            out_ref[block, :, :HD] = acc.astype(jnp.bfloat16)
-            out_ref[block, :, HD:] = stats.astype(jnp.bfloat16)
-
-        @pl.when(jnp.logical_not(is_open))
-        def _():
-            out_ref[block, :, :HD] = jnp.zeros((rows, HD), jnp.bfloat16)
-            out_ref[block, :, HD:] = jnp.where(lane == 0, LOWEST, 0.0).astype(jnp.bfloat16)
-
-
-def combine_kernel(parts_ref, near_ref, send_ref):
+        closed = jnp.where(order_ref[span] <= order_ref[block], 0.0, CLOSED)
+        s = lax.dot_general(q_ref[block], keys, (((1,), (1,)), ((), ())), preferred_element_type=jnp.float32)
+        s = s * scale + (bias + closed)
+        top = jnp.maximum(jnp.max(s, axis=1, keepdims=True), LOWEST)
+        top = top.astype(jnp.bfloat16).astype(jnp.float32)
+        w = jnp.exp2(s - top)
+        total = jnp.sum(w, axis=1, keepdims=True)
+        acc = jnp.dot(w.astype(jnp.bfloat16), values, preferred_element_type=jnp.float32)
+        coarse = total.astype(jnp.bfloat16).astype(jnp.float32)
+        stats = jnp.where(lane == 0, top, jnp.where(lane == 1, coarse, total - coarse))
+        out_ref[block, :, :HD] = acc.astype(jnp.bfloat16)
+        out_ref[block, :, HD:] = stats.astype(jnp.bfloat16)
+
+
+def combine_kernel(parts_ref, out_ref):
     stats = parts_ref[:, :, HD:].astype(jnp.float32)
     top = stats[:, :, 0:1]
-    factor = jnp.exp(top - jnp.max(top, axis=0, keepdims=True))
+    factor = jnp.exp2(top - jnp.max(top, axis=0, keepdims=True))
     denominator = jnp.sum(factor * (stats[:, :, 1:2] + stats[:, :, 2:3]), axis=0)
     summed = jnp.sum(factor * parts_ref[:, :, :HD].astype(jnp.float32), axis=0)
     done = summed / denominator
     tokens = done.shape[0] // FRAMES
     for y0 in range(2):
         piece = jnp.concatenate([done[(2 * i + y0) * tokens : (2 * i + y0 + 1) * tokens] for i in range(FRAMES // 2)])
-        piece = piece.astype(jnp.bfloat16)
-        send_ref[y0] = piece
-        for i in range(FRAMES // 2):
-            near_ref[2 * i + y0] = piece
-
-
-def project_kernel(near_rows_ref, far_rows_ref, near_ref, far_ref, out_ref):
+        out_ref[y0] = piece.astype(jnp.bfloat16)
+
+
+def spread_kernel(near_ref, far_ref, out_ref):
+    for y in range(out_ref.shape[0]):
+        out_ref[y, 0] = near_ref[y % 2]
+        out_ref[y, 1] = far_ref[y % 2]
+
+
+def project_kernel(rows_ref, near_ref, far_ref, out_ref):
     zh = lax.axis_index("zh")
     y0 = lax.axis_index("y0")
     heads = near_ref.shape[1] // HD
-    slots = near_rows_ref.shape[0] // 2
-    rows = near_rows_ref.shape[1]
+    rows = rows_ref.shape[2]
     quarter = rows // 4
-    for side, rows_ref in enumerate((near_rows_ref, far_rows_ref)):
-        left = [jnp.concatenate([rows_ref[c * slots + h] for h in range(heads)], axis=1) for c in range(2)]
+    for side in range(2):
+        left = [jnp.concatenate([rows_ref[c * heads + h, side] for h in range(heads)], axis=1) for c in range(2)]
         for turn, weight in enumerate((near_ref, far_ref)):
             first, second = [
                 lax.dot_general(part, weight[...], (((1,), (1,)), ((), ())), preferred_element_type=jnp.float32)
@@ -152,11 +156,11 @@
     packed = call(pack_kernel, [(ny, 3, tokens, HD)], [vmem] * 3, "pack")(q[0], k[0], v[0])
     with jax.named_scope("exchange_heads"):
         packed = lax.all_to_all(packed, ROW, 0, 0, tiled=True)
+    queries, kv = call(unpack_kernel, [(nx, ny, tokens, HD), (2, ny, tokens, HD)], [vmem], "unpack")(packed)
     with jax.named_scope("gather_q"):
-        queries = jnp.broadcast_to(packed[:, 0].reshape(1, rows, HD), (nx, rows, HD))
-        queries = lax.all_to_all(queries, "span", 0, 0, tiled=True)
+        queries = lax.all_to_all(queries.reshape(nx, rows, HD), "span", 0, 0, tiled=True)
     with jax.named_scope("gather_kv"):
-        kv = jnp.swapaxes(packed[:, 1:], 0, 1).reshape(2, rows, HD)
+        kv = kv.reshape(2, rows, HD)
         kv_far = lax.ppermute(kv, "zh", swap)
         near = lax.all_gather(kv, "core", axis=0, tiled=True)
         far = lax.all_gather(kv_far, "core", axis=0, tiled=True)
@@ -168,18 +172,15 @@
     )
     with jax.named_scope("return_parts"):
         parts = lax.all_to_all(parts, "span", 0, 0, tiled=True)
-    near, send = call(combine_kernel, [(ny, rows // 2, HD), (2, rows // 2, HD)], [vmem], "combine")(parts)
+    near = call(combine_kernel, [(2, rows // 2, HD)], [vmem], "combine")(parts)
     with jax.named_scope("gather_attended"):
-        far = lax.ppermute(send, "zh", swap)
-        near = lax.all_to_all(near, ROW, 0, 0, tiled=True)
-        far = jnp.broadcast_to(far, (ny // 2,) + far.shape).reshape(ny, rows // 2, HD)
-        far = lax.all_to_all(far, ROW, 0, 0, tiled=True)
-        near, far = lax.optimization_barrier((near, far))
-        near = lax.all_gather(near, "core", axis=0, tiled=True)
-        far = lax.all_gather(far, "core", axis=0, tiled=True)
+        far = lax.ppermute(near, "zh", swap)
+        both = call(spread_kernel, [(ny, 2, rows // 2, HD)], [vmem, vmem], "spread")(near, far)
+        both = lax.all_to_all(both, ROW, 0, 0, tiled=True)[: width // HD]
+        both = lax.all_gather(both, "core", axis=0, tiled=True)
     cols = weight.shape[0]
-    pieces = call(project_kernel, [(8, 4 * tokens * cols // HD, HD)], [vmem] * 4, "project")(
-        near, far, weight, weight_far
+    pieces = call(project_kernel, [(8, 4 * tokens * cols // HD, HD)], [vmem] * 3, "project")(
+        both, weight, weight_far
     )
     with jax.named_scope("sum_heads"):
         pieces = lax.all_to_all(pieces, ("head", "y0"), 0, 0, tiled=True)

time: 124 us -> 121 us (0.976)
  waiting for transfers between devices: 9.78 us -> 16.8 us
  starting transfers between devices: 35.2 us -> 29.6 us
  blocking collectives: 64.3 us -> 62 us
  local copies, waits for them, and re-layouts: 4.74 us -> 3.19 us
    all_to_all x3 -> x2, waiting for transfers between devices: 7.56 us -> 14.6 us  [the longest x1 14.6 us: shards(): both = lax.all_to_all(both, ROW, 0, 0, tiled=True)[:width // HD]]
    all_to_all x3 -> x2, starting transfers between devices: 13.3 us -> 7.7 us  [the longest x1 4.02 us: shards(): lax.all_to_all(queries.reshape(nx, rows, HD), 'span', 0, 0, tiled=True)]
    all_gather x2 -> x1, blocking collectives: 11.6 us -> 7.25 us  [shards(): both = lax.all_gather(both, 'core', axis=0, tiled=True)]
    broadcast_in_dim x2 -> x0, local copies, waits for them, and re-layouts: 1.54 us -> none  [the longest x1 0.77 us: shards(): jnp.broadcast_to(packed[:, 0].reshape(1, rows, HD), (nx, rows, HD))]
    pallas_call x2 -> x4, Pallas kernels: 2.26 us -> 3.23 us  [the longest x1 0.96 us: shards(): call(project_kernel, [(8, 4 * tokens * cols // HD, HD)], [vmem] * 3, 'pro...]
  transfers between devices with their start and end apart: 6 -> 5, of which waited for: 3 -> 2; matrix products, arithmetic and copies ran while one was open for 1% -> 0% of each run, Pallas kernels for 0% -> 0%
where the time goes in v6:
time: 121 us; the launch traced here: 120 us
  blocking collectives  62 us (51%)
  starting transfers between devices  29.6 us (24%)
  waiting for transfers between devices  16.8 us (14%)
  Pallas kernels  7.99 us (7%)
  local copies, waits for them, and re-layouts  3.19 us (3%)
    all_to_all x1, blocking collectives, shards(): pieces = lax.all_to_all(pieces, ('head', 'y0'), 0, 0, tiled=True)  17.7 us
    all_to_all x1, blocking collectives, shards(): packed = lax.all_to_all(packed, ROW, 0, 0, tiled=True)  16.5 us
    all_to_all x1, waiting for transfers between devices, shards(): both = lax.all_to_all(both, ROW, 0, 0, tiled=True)[:width // HD]  14.6 us
    all_to_all x1, blocking collectives, shards(): parts = lax.all_to_all(parts, 'span', 0, 0, tiled=True)  13.7 us
    ppermute x1, starting transfers between devices, shards(): kv_far = lax.ppermute(kv, 'zh', swap)  11.6 us
    all_gather x1, blocking collectives, shards(): both = lax.all_gather(both, 'core', axis=0, tiled=True)  7.25 us
    ppermute x1, starting transfers between devices, shards(): far = lax.ppermute(near, 'zh', swap)  7.03 us
    all_gather x1, blocking collectives, shards(): near = lax.all_gather(kv, 'core', axis=0, tiled=True)  4.7 us
  transfers between devices with their start and end apart: 5, of which 2 were waited for; matrix products, arithmetic and copies ran while one was open for 0% of the time, Pallas kernels for 0%

profile of v6, /device:TPU:1, one launch (start us, length us, event | category | flops | bytes accessed | tf_op | source)
XLA Modules:
  0.0 119.6 jit_solution(9963935474119173075)
XLA Ops:
  0.0 0.0 copy-start.2
  0.0 0.8 copy-done.2
  0.8 0.0 copy-start.3
  0.8 0.8 copy-done.3
  1.7 0.0 copy-start.4
  1.7 0.8 copy-done.4
  2.5 16.5 %all_to_all.25.packed_ref = bf16[8,3,40,128]{3,2,1,0:T(8,128)(2,1)S(1)} all-to-all(bf16[8,3,40,128]{3,2,1,0:T(8,128)(2,1)S(1)} %pack.1), channel_id=1, replica_groups=mesh['span'=4,'zh'=2,'y2'=2,'y1'=2,'y0'=2,'core'=2,'head'=4] {'y2','y1',..., dimensions={0} | all-to-all | bytes 491520 | tf_op jit(solution)/shard_map/exchange_heads/all_to_all | solution.py:158
  19.0 0.8 unpack.1
  19.8 11.6 %collective-permute-start = (bf16[2,320,128]{2,1,0:T(8,128)(2,1)S(1)}, bf16[2,320,128]{2,1,0:T(8,128)(2,1)S(1)}, u32[]{:S(2)}, u32[]{:S(2)}) collective-permute-start(bf16[2,320,128]{2,1,0:T(8,128)(2,1)S(1)} %bitcast.14), channel_id=1, source_target_pairs={{0,64},{64,0},{1,65},{65,1},{2,66},{66,2},{3,67},{67,3},{4,68},{68... | collective-permute-start | bytes 491528 | tf_op jit(solution)/shard_map/gather_kv/ppermute | solution.py:164
  31.4 4.0 %all-to-all-start.1 = ((bf16[4,320,128]{2,1,0:T(8,128)(2,1)}), bf16[4,320,128]{2,1,0:T(8,128)(2,1)S(1)}, u32[]{:S(2)}, u32[]{:S(2)}) async-start(bf16[4,320,128]{2,1,0:T(8,128)(2,1)} %bitcast.3), calls=%async_computation.1 | async-start | bytes 655360 | tf_op jit(solution)/shard_map/gather_q/all_to_all | solution.py:161
  35.4 4.7 %all_gather.9.near_ref = bf16[4,320,128]{2,1,0:T(8,128)(2,1)S(1)} all-gather(bf16[2,320,128]{2,1,0:T(8,128)(2,1)S(1)} %bitcast.15), channel_id=1, replica_groups=mesh['span'=4,'zh'=2,'y2'=2,'y1'=2,'y0'=2,'core'=2,'head'=4] {'core'}, dimensions={0}, use_global_device_ids=true | all-gather | bytes 491520 | tf_op jit(solution)/shard_map/gather_kv/all_gather | solution.py:165
  40.1 0.0 copy-start.6
  40.1 0.0 copy-start.7
  40.1 0.0 collective-permute-done
  40.1 2.2 %all_gather.10.far_ref = bf16[4,320,128]{2,1,0:T(8,128)(2,1)S(1)} all-gather(bf16[2,320,128]{2,1,0:T(8,128)(2,1)S(1)} %collective-permute-done), channel_id=1, replica_groups=mesh['span'=4,'zh'=2,'y2'=2,'y1'=2,'y0'=2,'core'=2,'head'=4] {'core'}, dimensions={0}, use_global_device_ids=true | all-gather | bytes 491520 | tf_op jit(solution)/shard_map/gather_kv/all_gather | solution.py:166
  42.3 0.0 all-to-all-done.1.q_ref
  42.3 0.0 copy-done.6
  42.3 0.0 copy-done.7
  42.3 3.3 %attend.1 = bf16[4,320,256]{2,1,0:T(8,128)(2,1)S(1)} custom-call(s32[4]{0:T(128)S(1)} %copy-done.6, s32[4]{0:T(128)S(1)} %copy-done.7, bf16[4,320,128]{2,1,0:T(8,128)(2,1)S(1)} %all-to-all-done.1.q_ref, bf16[4,320,128]{2,1,0:T(8,128)(2,1)S(1)} %all_gather.9.near_ref, bf16[4,320,128]{2,1,0:T(8,128)(2,1)S(1)} %all_gather.10.far_ref), custom_call_target="tpu_custom_call" | custom-call | tf_op jit(solution)/shard_map/attend/pallas_call | solution.py:170
  45.6 13.7 %all_to_all.26.parts_ref = bf16[4,320,256]{2,1,0:T(8,128)(2,1)S(1)} all-to-all(bf16[4,320,256]{2,1,0:T(8,128)(2,1)S(1)} %attend.1), channel_id=1, replica_groups=mesh['span'=4,'zh'=2,'y2'=2,'y1'=2,'y0'=2,'core'=2,'head'=4] {'span'}, dimensions={0} | all-to-all | bytes 1310720 | tf_op jit(solution)/shard_map/return_parts/all_to_all | solution.py:174
  59.3 0.6 combine.1.near_ref
  59.9 7.0 %collective-permute-start.1 = (bf16[2,160,128]{2,1,0:T(8,128)(2,1)S(1)}, bf16[2,160,128]{2,1,0:T(8,128)(2,1)S(1)}, u32[]{:S(2)}, u32[]{:S(2)}) collective-permute-start(bf16[2,160,128]{2,1,0:T(8,128)(2,1)S(1)} %combine.1.near_ref), channel_id=1, source_target_pairs={{0,64},{64,0},{1,65},{65,1},{2,66},{66,2},{3,67},{67,3},{4,68},{68... | collective-permute-start | bytes 245768 | tf_op jit(solution)/shard_map/gather_attended/ppermute | solution.py:177
  66.9 2.1 %collective-permute-done.1.far_ref = bf16[2,160,128]{2,1,0:T(8,128)(2,1)S(1)} collective-permute-done((bf16[2,160,128]{2,1,0:T(8,128)(2,1)S(1)}, bf16[2,160,128]{2,1,0:T(8,128)(2,1)S(1)}, u32[]{:S(2)}, u32[]{:S(2)}) %collective-permute-start.1) | collective-permute-done | bytes 81952 | tf_op jit(solution)/shard_map/gather_attended/ppermute | solution.py:177
  69.0 0.9 spread.1
  70.0 0.0 copy-start
  70.0 3.7 %all-to-all-start.3 = ((bf16[8,2,160,128]{3,2,1,0:T(8,128)(2,1)}), bf16[8,2,160,128]{3,2,1,0:T(8,128)(2,1)S(1)}, u32[]{:S(2)}, u32[]{:S(2)}) async-start(bf16[8,2,160,128]{3,2,1,0:T(8,128)(2,1)} %spread.1), calls=%async_computation.3 | async-start | bytes 1310720 | tf_op jit(solution)/shard_map/gather_attended/all_to_all | solution.py:179
  73.7 0.0 copy-done
  73.7 3.2 %collective-permute-start.2 = (bf16[192,768]{1,0:T(8,128)(2,1)S(1)}, bf16[192,768]{1,0:T(8,128)(2,1)S(1)}, u32[]{:S(2)}, u32[]{:S(2)}) collective-permute-start(bf16[192,768]{1,0:T(8,128)(2,1)S(1)} %bitcast.12), channel_id=1, source_target_pairs={{0,8},{8,0},{1,9},{9,1},{2,10},{10,2},{3,11},{11,3},{4,12},{12,4},... | collective-permute-start | bytes 884744 | tf_op jit(solution)/shard_map/fetch_weight/ppermute | solution.py:169
  76.9 14.6 %all-to-all-done.3 = bf16[8,2,160,128]{3,2,1,0:T(8,128)(2,1)S(1)} async-done(((bf16[8,2,160,128]{3,2,1,0:T(8,128)(2,1)}), bf16[8,2,160,128]{3,2,1,0:T(8,128)(2,1)S(1)}, u32[]{:S(2)}, u32[]{:S(2)}) %all-to-all-start.3) | async-done | bytes 655392 | tf_op jit(solution)/shard_map/gather_attended/all_to_all | solution.py:179
  91.6 7.3 %all_gather.11.rows_ref = bf16[12,2,160,128]{3,2,1,0:T(8,128)(2,1)S(1)} all-gather(bf16[6,2,160,128]{3,2,1,0:T(8,128)(2,1)S(1)} %slice.4), channel_id=1, replica_groups=mesh['span'=4,'zh'=2,'y2'=2,'y1'=2,'y0'=2,'core'=2,'head'=4] {'core'}, dimensions={0}, use_global_device_ids=true | all-gather | bytes 1474560 | tf_op jit(solution)/shard_map/gather_attended/all_gather | solution.py:180
  98.8 0.0 collective-permute-done.2.far_ref
  98.8 1.0 project.1
  99.8 0.0 copy-start.1
  99.8 0.0 copy-start.5
  99.8 17.7 %all_to_all.27.pieces_ref = bf16[8,240,128]{2,1,0:T(8,128)(2,1)S(1)} all-to-all(bf16[8,240,128]{2,1,0:T(8,128)(2,1)S(1)} %project.1), channel_id=1, replica_groups=mesh['span'=4,'zh'=2,'y2'=2,'y1'=2,'y0'=2,'core'=2,'head'=4] {'head','y0'}, dimensions={0} | all-to-all | bytes 983040 | tf_op jit(solution)/shard_map/sum_heads/all_to_all | solution.py:186
  117.6 0.0 copy-start.8
  117.6 0.0 copy-done.1
  117.6 0.0 copy-done.5
  117.6 0.6 copy-done.8
  118.2 1.4 %finish.1 = bf16[192,320]{1,0:T(8,128)(2,1)} custom-call(s32[4]{0:T(128)S(1)} %copy-done.8, bf16[8,240,128]{2,1,0:T(8,128)(2,1)S(1)} %all_to_all.27.pieces_ref, f32[4,192]{1,0:T(4,128)S(1)} %copy-done.5, bf16[192,320]{1,0:T(8,128)(2,1)S(1)} %bitcast.16), custom_call_target="tpu_custom_call" | custom-call | tf_op jit(solution)/shard_map/finish/pallas_call | solution.py:187
  (2 shorter events, 0.1 us)
Async XLA Ops:
  0.0 0.8 copy-start.2
  0.8 0.8 copy-start.3
  1.7 0.8 copy-start.4
  19.8 20.3 %collective-permute-start = (bf16[2,320,128]{2,1,0:T(8,128)(2,1)S(1)}, bf16[2,320,128]{2,1,0:T(8,128)(2,1)S(1)}, u32[]{:S(2)}, u32[]{:S(2)}) collective-permute-start(bf16[2,320,128]{2,1,0:T(8,128)(2,1)S(1)} %bitcast.14), channel_id=1, source_target_pairs={{0,64},{64,0},{1,65},{65,1},{2,66},{66,2},{3,67},{67,3},{4,68},{68... | collective-permute-start | bytes 491528 | tf_op jit(solution)/shard_map/gather_kv/ppermute | solution.py:164
  31.4 10.9 %all-to-all-start.1 = ((bf16[4,320,128]{2,1,0:T(8,128)(2,1)}), bf16[4,320,128]{2,1,0:T(8,128)(2,1)S(1)}, u32[]{:S(2)}, u32[]{:S(2)}) async-start(bf16[4,320,128]{2,1,0:T(8,128)(2,1)} %bitcast.3), calls=%async_computation.1 | async-start | bytes 655360 | tf_op jit(solution)/shard_map/gather_q/all_to_all | solution.py:161
  40.1 2.2 %copy-start.6 = (s32[4]{0:T(128)S(1)}, s32[4]{0:T(128)}, u32[]{:S(2)}) copy-start(s32[4]{0:T(128)} %order_ref.1) | copy-start | bytes 52
  40.1 2.2 %copy-start.7 = (s32[4]{0:T(128)S(1)}, s32[4]{0:T(128)}, u32[]{:S(2)}) copy-start(s32[4]{0:T(128)} %valid_ref.1) | copy-start | bytes 52
  59.9 9.2 %collective-permute-start.1 = (bf16[2,160,128]{2,1,0:T(8,128)(2,1)S(1)}, bf16[2,160,128]{2,1,0:T(8,128)(2,1)S(1)}, u32[]{:S(2)}, u32[]{:S(2)}) collective-permute-start(bf16[2,160,128]{2,1,0:T(8,128)(2,1)S(1)} %combine.1.near_ref), channel_id=1, source_target_pairs={{0,64},{64,0},{1,65},{65,1},{2,66},{66,2},{3,67},{67,3},{4,68},{68... | collective-permute-start | bytes 245768 | tf_op jit(solution)/shard_map/gather_attended/ppermute | solution.py:177
  70.0 3.7 %copy-start = (bf16[768,192]{0,1:T(8,128)(2,1)S(1)}, bf16[768,192]{0,1:T(8,128)(2,1)}, u32[]{:S(2)}) copy-start(bf16[768,192]{0,1:T(8,128)(2,1)} %param.16) | copy-start | bytes 884740
  70.0 21.6 %all-to-all-start.3 = ((bf16[8,2,160,128]{3,2,1,0:T(8,128)(2,1)}), bf16[8,2,160,128]{3,2,1,0:T(8,128)(2,1)S(1)}, u32[]{:S(2)}, u32[]{:S(2)}) async-start(bf16[8,2,160,128]{3,2,1,0:T(8,128)(2,1)} %spread.1), calls=%async_computation.3 | async-start | bytes 1310720 | tf_op jit(solution)/shard_map/gather_attended/all_to_all | solution.py:179
  73.7 25.2 %collective-permute-start.2 = (bf16[192,768]{1,0:T(8,128)(2,1)S(1)}, bf16[192,768]{1,0:T(8,128)(2,1)S(1)}, u32[]{:S(2)}, u32[]{:S(2)}) collective-permute-start(bf16[192,768]{1,0:T(8,128)(2,1)S(1)} %bitcast.12), channel_id=1, source_target_pairs={{0,8},{8,0},{1,9},{9,1},{2,10},{10,2},{3,11},{11,3},{4,12},{12,4},... | collective-permute-start | bytes 884744 | tf_op jit(solution)/shard_map/fetch_weight/ppermute | solution.py:169
  99.8 17.8 %copy-start.1 = (bf16[1,320,192]{1,2,0:T(8,128)(2,1)S(1)}, bf16[1,320,192]{1,2,0:T(8,128)(2,1)}, u32[]{:S(2)}) copy-start(bf16[1,320,192]{1,2,0:T(8,128)(2,1)} %param.17) | copy-start | bytes 368644
  99.8 17.8 %copy-start.5 = (f32[4,192]{1,0:T(4,128)S(1)}, f32[4,192]{1,0:T(4,128)}, u32[]{:S(2)}) copy-start(f32[4,192]{1,0:T(4,128)} %gate_ref.1) | copy-start | bytes 9220
  117.6 0.7 copy-start.8

commit v7 on v6

--- a/solution.py
+++ b/solution.py
@@ -75,58 +75,62 @@
     summed = jnp.sum(factor * parts_ref[:, :, :HD].astype(jnp.float32), axis=0)
     done = summed / denominator
     tokens = done.shape[0] // FRAMES
-    for y0 in range(2):
-        piece = jnp.concatenate([done[(2 * i + y0) * tokens : (2 * i + y0 + 1) * tokens] for i in range(FRAMES // 2)])
-        out_ref[y0] = piece.astype(jnp.bfloat16)
+    places = out_ref.shape[0]
+    for i in range(places):
+        piece = jnp.concatenate([done[j * tokens : (j + 1) * tokens] for j in range(i, FRAMES, places)])
+        out_ref[i] = piece.astype(jnp.bfloat16)
 
 
 def spread_kernel(near_ref, far_ref, out_ref):
     for y in range(out_ref.shape[0]):
-        out_ref[y, 0] = near_ref[y % 2]
-        out_ref[y, 1] = far_ref[y % 2]
-
-
-def project_kernel(rows_ref, near_ref, far_ref, out_ref):
+        place = y % near_ref.shape[0]
+        out_ref[y, 0] = near_ref[place]
+        out_ref[y, 1] = far_ref[place]
+
+
+def project_kernel(rows_ref, weights_ref, out_ref):
     zh = lax.axis_index("zh")
-    y0 = lax.axis_index("y0")
-    heads = near_ref.shape[1] // HD
+    heads = weights_ref.shape[2] // HD
     rows = rows_ref.shape[2]
-    quarter = rows // 4
-    for side in range(2):
-        left = [jnp.concatenate([rows_ref[c * heads + h, side] for h in range(heads)], axis=1) for c in range(2)]
-        for turn, weight in enumerate((near_ref, far_ref)):
-            first, second = [
-                lax.dot_general(part, weight[...], (((1,), (1,)), ((), ())), preferred_element_type=jnp.float32)
-                for part in left
-            ]
+    half = rows // 2
+    left = jnp.concatenate(
+        [
+            jnp.concatenate([rows_ref[c * heads + h, side] for h in range(heads)], axis=1)
+            for side in range(2)
+            for c in range(2)
+        ]
+    )
+    places = weights_ref.shape[0]
+    for place in range(places):
+        product = lax.dot_general(
+            left, weights_ref[place], (((1,), (1,)), ((), ())), preferred_element_type=jnp.float32
+        )
+        for side in range(2):
             for y2 in range(2):
-                a, b = 2 * y2 * quarter, (2 * y2 + 1) * quarter
-                piece = jnp.concatenate(
-                    [first[a : a + quarter], second[a : a + quarter], first[b : b + quarter], second[b : b + quarter]]
-                )
-                slot = (2 * (zh ^ side) + y2) * 2 + (y0 ^ turn)
-                out_ref[slot, :rows, :] = piece[:, :HD].astype(jnp.bfloat16)
-                tail = jnp.concatenate([piece[: rows // 2, HD:], piece[rows // 2 :, HD:]], axis=1)
+                a = 2 * side * rows + y2 * half
+                first, second = product[a : a + half], product[a + rows : a + rows + half]
+                slot = (2 * (zh ^ side) + y2) * places + place
+                main = jnp.concatenate([first[:, :HD], second[:, :HD]])
+                out_ref[slot, :rows, :] = main.astype(jnp.bfloat16)
+                tail = jnp.concatenate([first[:, HD:], second[:, HD:]], axis=1)
                 out_ref[slot, rows:, :] = tail.astype(jnp.bfloat16)
 
 
 def finish_kernel(steps_ref, pieces_ref, gate_ref, residual_ref, out_ref):
     step = steps_ref[lax.axis_index("span")]
     gate = gate_ref[pl.ds(step, 1), :]
-    rows = residual_ref.shape[1] // 2
-    half = rows // 2
-    sums = []
-    for y0 in range(2):
-        total = pieces_ref[y0].astype(jnp.float32)
+    places = pieces_ref.shape[0] // 4
+    rows = residual_ref.shape[1] // places
+    rest = HD // 2
+    mains, tails = [], []
+    for place in range(places):
+        total = pieces_ref[place].astype(jnp.float32)
         for head in range(1, 4):
-            total = total + pieces_ref[2 * head + y0].astype(jnp.float32)
-        sums.append(total)
-    near, far = sums
-    main = jnp.concatenate([near[:half], far[:half], near[half:rows], far[half:rows]])
-    rest = HD // 2
-    tail = jnp.concatenate([near[rows:, :rest], far[rows:, :rest], near[rows:, rest:], far[rows:, rest:]])
-    main = (main * gate[:, :HD]).T
-    tail = (tail * gate[:, HD:]).T
+            total = total + pieces_ref[places * head + place].astype(jnp.float32)
+        mains.append(total[:rows])
+        tails += [total[rows:, :rest], total[rows:, rest:]]
+    main = (jnp.concatenate(mains) * gate[:, :HD]).T
+    tail = (jnp.concatenate(tails) * gate[:, HD:]).T
     out_ref[:HD, :] = (residual_ref[:HD, :].astype(jnp.float32) + main).astype(jnp.bfloat16)
     out_ref[HD:, :] = (residual_ref[HD:, :].astype(jnp.float32) + tail).astype(jnp.bfloat16)
 
@@ -165,25 +169,23 @@
         near = lax.all_gather(kv, "core", axis=0, tiled=True)
         far = lax.all_gather(kv_far, "core", axis=0, tiled=True)
     with jax.named_scope("fetch_weight"):
-        weight = out_weight.T
-        weight_far = lax.ppermute(weight, "y0", swap)
+        weight, kv = lax.optimization_barrier((out_weight.T, kv))
+        weights = lax.all_gather(weight, ("y1", "y0"), axis=0, tiled=False)
     parts = call(attend_kernel, [(nx, rows, 2 * HD)], [smem, smem, vmem, vmem, vmem], "attend")(
         block_order, valid_frames, queries, near, far
     )
     with jax.named_scope("return_parts"):
         parts = lax.all_to_all(parts, "span", 0, 0, tiled=True)
-    near = call(combine_kernel, [(2, rows // 2, HD)], [vmem], "combine")(parts)
+    near = call(combine_kernel, [(4, rows // 4, HD)], [vmem], "combine")(parts)
     with jax.named_scope("gather_attended"):
         far = lax.ppermute(near, "zh", swap)
-        both = call(spread_kernel, [(ny, 2, rows // 2, HD)], [vmem, vmem], "spread")(near, far)
+        both = call(spread_kernel, [(ny, 2, rows // 4, HD)], [vmem, vmem], "spread")(near, far)
         both = lax.all_to_all(both, ROW, 0, 0, tiled=True)[: width // HD]
         both = lax.all_gather(both, "core", axis=0, tiled=True)
     cols = weight.shape[0]
-    pieces = call(project_kernel, [(8, 4 * tokens * cols // HD, HD)], [vmem] * 3, "project")(
-        both, weight, weight_far
-    )
+    pieces = call(project_kernel, [(16, 2 * tokens * cols // HD, HD)], [vmem] * 2, "project")(both, weights)
     with jax.named_scope("sum_heads"):
-        pieces = lax.all_to_all(pieces, ("head", "y0"), 0, 0, tiled=True)
+        pieces = lax.all_to_all(pieces, ("head", "y1", "y0"), 0, 0, tiled=True)
     mixed = pl.pallas_call(
         finish_kernel,
         out_shape=jax.ShapeDtypeStruct(residual.shape[:0:-1], bf16),

time: 121 us -> 125 us (1.033)
  waiting for transfers between devices: 16.8 us -> 1.94 us
  blocking collectives: 62 us -> 75.6 us
  between operations: 0.09 us -> 13.5 us
  starting transfers between devices: 29.6 us -> 23.1 us
    all_to_all x1 -> x2, blocking collectives: 17.7 us -> 32.3 us  [the longest x1 19.9 us: shards(): pieces = lax.all_to_all(pieces, ('head', 'y1', 'y0'), 0, 0, tiled=True)]
    all_to_all x1 -> x0, waiting for transfers between devices: 14.6 us -> none  [shards(): both = lax.all_to_all(both, ROW, 0, 0, tiled=True)[:width // HD]]
    all_to_all x1 -> x0, starting transfers between devices: 3.67 us -> none  [shards(): both = lax.all_to_all(both, ROW, 0, 0, tiled=True)[:width // HD]]
    ppermute x1 -> x0, starting transfers between devices: 3.25 us -> none  [shards(): weight_far = lax.ppermute(weight, 'y0', swap)]
  transfers between devices with their start and end apart: 5 -> 4, of which waited for: 2 -> 1; matrix products, arithmetic and copies ran while one was open for 0% -> 0% of each run, Pallas kernels for 0% -> 3%
where the time goes in v7:
time: 125 us
  blocking collectives  75.6 us (60%)
  starting transfers between devices  23.1 us (18%)
  between operations  13.5 us (11%)
  Pallas kernels  6.92 us (6%)
  local copies, waits for them, and re-layouts  3.79 us (3%)
  waiting for transfers between devices  1.94 us (2%)
    all_to_all x1, blocking collectives, shards(): pieces = lax.all_to_all(pieces, ('head', 'y1', 'y0'), 0, 0, tiled=True)  19.9 us
    all_to_all x1, blocking collectives, shards(): packed = lax.all_to_all(packed, ROW, 0, 0, tiled=True)  16.5 us
    all_to_all x1, blocking collectives, shards(): parts = lax.all_to_all(parts, 'span', 0, 0, tiled=True)  13.5 us
    all_to_all x1, blocking collectives, shards(): both = lax.all_to_all(both, ROW, 0, 0, tiled=True)[:width // HD]  12.4 us
    ppermute x1, starting transfers between devices, shards(): kv_far = lax.ppermute(kv, 'zh', swap)  11.6 us
    ppermute x1, starting transfers between devices, shards(): far = lax.ppermute(near, 'zh', swap)  7.48 us
    all_gather x1, blocking collectives, shards(): both = lax.all_gather(both, 'core', axis=0, tiled=True)  6.47 us
    all_gather x1, blocking collectives, shards(): near = lax.all_gather(kv, 'core', axis=0, tiled=True)  4.7 us
  transfers between devices with their start and end apart: 4, of which 1 were waited for; matrix products, arithmetic and copies ran while one was open for 0% of the time, Pallas kernels for 3%

profile of v7, /device:TPU:1, one launch (start us, length us, event | category | flops | bytes accessed | tf_op | source)
XLA Modules:
  0.0 124.8 jit_solution(4518460369919005781)
XLA Ops:
  6.5 0.0 all-gather.3.cloned.1.call-start
  6.5 0.0 copy-start.2
  6.5 0.8 copy-done.2
  7.4 0.0 copy-start.3
  7.4 0.8 copy-done.3
  8.2 0.0 copy-start.4
  8.2 0.8 copy-done.4
  9.1 16.5 %all_to_all.25.packed_ref = bf16[8,3,40,128]{3,2,1,0:T(8,128)(2,1)S(1)} all-to-all(bf16[8,3,40,128]{3,2,1,0:T(8,128)(2,1)S(1)} %pack.1), channel_id=1, replica_groups=mesh['span'=4,'zh'=2,'y2'=2,'y1'=2,'y0'=2,'core'=2,'head'=4] {'y2','y1',..., dimensions={0} | all-to-all | bytes 491520 | tf_op jit(solution)/shard_map/exchange_heads/all_to_all | solution.py:162
  25.5 0.0 copy-start.6
  25.5 0.0 copy-start.7
  25.5 0.8 unpack.1
  26.3 0.0 all-gather.3.cloned.1.call-update
  26.4 11.6 %collective-permute-start = (bf16[2,320,128]{2,1,0:T(8,128)(2,1)S(1)}, bf16[2,320,128]{2,1,0:T(8,128)(2,1)S(1)}, u32[]{:S(2)}, u32[]{:S(2)}) collective-permute-start(bf16[2,320,128]{2,1,0:T(8,128)(2,1)S(1)} %bitcast.14), channel_id=1, source_target_pairs={{0,64},{64,0},{1,65},{65,1},{2,66},{66,2},{3,67},{67,3},{4,68},{68... | collective-permute-start | bytes 491528 | tf_op jit(solution)/shard_map/gather_kv/ppermute | solution.py:168
  38.0 4.0 %all-to-all-start.1 = ((bf16[4,320,128]{2,1,0:T(8,128)(2,1)}), bf16[4,320,128]{2,1,0:T(8,128)(2,1)S(1)}, u32[]{:S(2)}, u32[]{:S(2)}) async-start(bf16[4,320,128]{2,1,0:T(8,128)(2,1)} %bitcast.3), calls=%async_computation.1 | async-start | bytes 655360 | tf_op jit(solution)/shard_map/gather_q/all_to_all | solution.py:165
  42.0 4.7 %all_gather.15.near_ref = bf16[4,320,128]{2,1,0:T(8,128)(2,1)S(1)} all-gather(bf16[2,320,128]{2,1,0:T(8,128)(2,1)S(1)} %bitcast.15), channel_id=1, replica_groups=mesh['span'=4,'zh'=2,'y2'=2,'y1'=2,'y0'=2,'core'=2,'head'=4] {'core'}, dimensions={0}, use_global_device_ids=true | all-gather | bytes 491520 | tf_op jit(solution)/shard_map/gather_kv/all_gather | solution.py:169
  46.7 0.0 collective-permute-done
  46.7 2.0 %all_gather.16.far_ref = bf16[4,320,128]{2,1,0:T(8,128)(2,1)S(1)} all-gather(bf16[2,320,128]{2,1,0:T(8,128)(2,1)S(1)} %collective-permute-done), channel_id=1, replica_groups=mesh['span'=4,'zh'=2,'y2'=2,'y1'=2,'y0'=2,'core'=2,'head'=4] {'core'}, dimensions={0}, use_global_device_ids=true | all-gather | bytes 491520 | tf_op jit(solution)/shard_map/gather_kv/all_gather | solution.py:170
  48.7 0.0 all-to-all-done.1.q_ref
  48.7 0.0 copy-done.6
  48.7 0.0 copy-done.7
  48.8 3.3 %attend.1 = bf16[4,320,256]{2,1,0:T(8,128)(2,1)S(1)} custom-call(s32[4]{0:T(128)S(1)} %copy-done.6, s32[4]{0:T(128)S(1)} %copy-done.7, bf16[4,320,128]{2,1,0:T(8,128)(2,1)S(1)} %all-to-all-done.1.q_ref, bf16[4,320,128]{2,1,0:T(8,128)(2,1)S(1)} %all_gather.15.near_ref, bf16[4,320,128]{2,1,0:T(8,128)(2,1)S(1)} %all_gather.16.far_ref), custom_call_target="tpu_custom_call" | custom-call | tf_op jit(solution)/shard_map/attend/pallas_call | solution.py:174
  52.1 13.5 %all_to_all.26.parts_ref = bf16[4,320,256]{2,1,0:T(8,128)(2,1)S(1)} all-to-all(bf16[4,320,256]{2,1,0:T(8,128)(2,1)S(1)} %attend.1), channel_id=1, replica_groups=mesh['span'=4,'zh'=2,'y2'=2,'y1'=2,'y0'=2,'core'=2,'head'=4] {'span'}, dimensions={0} | all-to-all | bytes 1310720 | tf_op jit(solution)/shard_map/return_parts/all_to_all | solution.py:178
  65.6 0.5 combine.1.near_ref
  66.2 7.5 %collective-permute-start.1 = (bf16[4,80,128]{2,1,0:T(8,128)(2,1)S(1)}, bf16[4,80,128]{2,1,0:T(8,128)(2,1)S(1)}, u32[]{:S(2)}, u32[]{:S(2)}) collective-permute-start(bf16[4,80,128]{2,1,0:T(8,128)(2,1)S(1)} %combine.1.near_ref), channel_id=1, source_target_pairs={{0,64},{64,0},{1,65},{65,1},{2,66},{66,2},{3,67},{67,3},{4,68},{68... | collective-permute-start | bytes 245768 | tf_op jit(solution)/shard_map/gather_attended/ppermute | solution.py:181
  73.6 1.9 %collective-permute-done.1.far_ref = bf16[4,80,128]{2,1,0:T(8,128)(2,1)S(1)} collective-permute-done((bf16[4,80,128]{2,1,0:T(8,128)(2,1)S(1)}, bf16[4,80,128]{2,1,0:T(8,128)(2,1)S(1)}, u32[]{:S(2)}, u32[]{:S(2)}) %collective-permute-start.1) | collective-permute-done | bytes 81952 | tf_op jit(solution)/shard_map/gather_attended/ppermute | solution.py:181
  75.6 12.4 %all_to_all.27 = bf16[8,2,80,128]{3,2,1,0:T(8,128)(2,1)S(1)} all-to-all(bf16[8,2,80,128]{3,2,1,0:T(8,128)(2,1)S(1)} %spread.1), channel_id=1, replica_groups=mesh['span'=4,'zh'=2,'y2'=2,'y1'=2,'y0'=2,'core'=2,'head'=4] {'y2','y1',..., dimensions={0} | all-to-all | bytes 655360 | tf_op jit(solution)/shard_map/gather_attended/all_to_all | solution.py:183
  88.1 6.5 %all_gather.17.rows_ref = bf16[12,2,80,128]{3,2,1,0:T(8,128)(2,1)S(1)} all-gather(bf16[6,2,80,128]{3,2,1,0:T(8,128)(2,1)S(1)} %slice.4), channel_id=1, replica_groups=mesh['span'=4,'zh'=2,'y2'=2,'y1'=2,'y0'=2,'core'=2,'head'=4] {'core'}, dimensions={0}, use_global_device_ids=true | all-gather | bytes 737280 | tf_op jit(solution)/shard_map/gather_attended/all_gather | solution.py:184
  94.5 0.0 all-gather.3.cloned.1.call-done
  94.5 0.0 copy-start
  94.5 1.3 %copy-done = bf16[768,768]{1,0:T(8,128)(2,1)S(1)} copy-done((bf16[768,768]{1,0:T(8,128)(2,1)S(1)}, bf16[768,768]{1,0:T(8,128)(2,1)}, u32[]{:S(2)}) %copy-start) | copy-done | bytes 1179672
  95.8 0.0 copy-start.1
  95.8 0.0 copy-start.5
  95.8 0.0 copy-start.8
  95.8 0.8 project.1
  96.6 19.9 %all_to_all.28.pieces_ref = bf16[16,120,128]{2,1,0:T(8,128)(2,1)S(1)} all-to-all(bf16[16,120,128]{2,1,0:T(8,128)(2,1)S(1)} %project.1), channel_id=1, replica_groups=mesh['span'=4,'zh'=2,'y2'=2,'y1'=2,'y0'=2,'core'=2,'head'=4] {'head','y1..., dimensions={0} | all-to-all | bytes 983040 | tf_op jit(solution)/shard_map/sum_heads/all_to_all | solution.py:188
  116.5 0.0 copy-done.1
  116.5 0.0 copy-done.5
  116.5 0.0 copy-done.8
  116.5 1.4 %finish.1 = bf16[192,320]{1,0:T(8,128)(2,1)} custom-call(s32[4]{0:T(128)S(1)} %copy-done.8, bf16[16,120,128]{2,1,0:T(8,128)(2,1)S(1)} %all_to_all.28.pieces_ref, f32[4,192]{1,0:T(4,128)S(1)} %copy-done.5, bf16[192,320]{1,0:T(8,128)(2,1)S(1)} %bitcast.16), custom_call_target="tpu_custom_call" | custom-call | tf_op jit(solution)/shard_map/finish/pallas_call | solution.py:189
  (3 shorter events, 0.1 us)
Async XLA Ops:
  6.5 88.0 %all-gather.3.cloned.1.call-start = ((), (), s32[]{:S(2)}) async-start(), calls=%async_computation.5 | async-start | bytes 1474560 | tf_op jit(solution)/shard_map/fetch_weight/all_gather | solution.py:173
  6.5 0.8 copy-start.2
  7.4 0.8 copy-start.3
  8.2 0.8 copy-start.4
  25.5 23.2 %copy-start.6 = (s32[4]{0:T(128)S(1)}, s32[4]{0:T(128)}, u32[]{:S(2)}) copy-start(s32[4]{0:T(128)} %order_ref.1) | copy-start | bytes 52
  25.5 23.2 %copy-start.7 = (s32[4]{0:T(128)S(1)}, s32[4]{0:T(128)}, u32[]{:S(2)}) copy-start(s32[4]{0:T(128)} %valid_ref.1) | copy-start | bytes 52
  26.4 20.3 %collective-permute-start = (bf16[2,320,128]{2,1,0:T(8,128)(2,1)S(1)}, bf16[2,320,128]{2,1,0:T(8,128)(2,1)S(1)}, u32[]{:S(2)}, u32[]{:S(2)}) collective-permute-start(bf16[2,320,128]{2,1,0:T(8,128)(2,1)S(1)} %bitcast.14), channel_id=1, source_target_pairs={{0,64},{64,0},{1,65},{65,1},{2,66},{66,2},{3,67},{67,3},{4,68},{68... | collective-permute-start | bytes 491528 | tf_op jit(solution)/shard_map/gather_kv/ppermute | solution.py:168
  38.0 10.8 %all-to-all-start.1 = ((bf16[4,320,128]{2,1,0:T(8,128)(2,1)}), bf16[4,320,128]{2,1,0:T(8,128)(2,1)S(1)}, u32[]{:S(2)}, u32[]{:S(2)}) async-start(bf16[4,320,128]{2,1,0:T(8,128)(2,1)} %bitcast.3), calls=%async_computation.1 | async-start | bytes 655360 | tf_op jit(solution)/shard_map/gather_q/all_to_all | solution.py:165
  66.2 9.4 %collective-permute-start.1 = (bf16[4,80,128]{2,1,0:T(8,128)(2,1)S(1)}, bf16[4,80,128]{2,1,0:T(8,128)(2,1)S(1)}, u32[]{:S(2)}, u32[]{:S(2)}) collective-permute-start(bf16[4,80,128]{2,1,0:T(8,128)(2,1)S(1)} %combine.1.near_ref), channel_id=1, source_target_pairs={{0,64},{64,0},{1,65},{65,1},{2,66},{66,2},{3,67},{67,3},{4,68},{68... | collective-permute-start | bytes 245768 | tf_op jit(solution)/shard_map/gather_attended/ppermute | solution.py:181
  94.5 1.3 %copy-start = (bf16[768,768]{1,0:T(8,128)(2,1)S(1)}, bf16[768,768]{1,0:T(8,128)(2,1)}, u32[]{:S(2)}) copy-start(bf16[768,768]{1,0:T(8,128)(2,1)} %all-gather.3.cloned.1.call-done) | copy-start | bytes 3538948
  95.8 20.7 %copy-start.1 = (bf16[1,320,192]{1,2,0:T(8,128)(2,1)S(1)}, bf16[1,320,192]{1,2,0:T(8,128)(2,1)}, u32[]{:S(2)}) copy-start(bf16[1,320,192]{1,2,0:T(8,128)(2,1)} %param.17) | copy-start | bytes 368644
  95.8 20.7 %copy-start.5 = (f32[4,192]{1,0:T(4,128)S(1)}, f32[4,192]{1,0:T(4,128)}, u32[]{:S(2)}) copy-start(f32[4,192]{1,0:T(4,128)} %gate_ref.1) | copy-start | bytes 9220
  95.8 20.7 %copy-start.8 = (s32[4]{0:T(128)S(1)}, s32[4]{0:T(128)}, u32[]{:S(2)}) copy-start(s32[4]{0:T(128)} %steps_ref.1) | copy-start | bytes 52
Sparse Core Ops, SparseCore 0:
  26.5 40.1 all-gather.2

commit v8 on v6

--- a/solution.py
+++ b/solution.py
@@ -165,13 +165,14 @@
         near = lax.all_gather(kv, "core", axis=0, tiled=True)
         far = lax.all_gather(kv_far, "core", axis=0, tiled=True)
     with jax.named_scope("fetch_weight"):
-        weight = out_weight.T
+        weight, near = lax.optimization_barrier((out_weight.T, near))
         weight_far = lax.ppermute(weight, "y0", swap)
     parts = call(attend_kernel, [(nx, rows, 2 * HD)], [smem, smem, vmem, vmem, vmem], "attend")(
         block_order, valid_frames, queries, near, far
     )
     with jax.named_scope("return_parts"):
         parts = lax.all_to_all(parts, "span", 0, 0, tiled=True)
+        parts, weight_far = lax.optimization_barrier((parts, weight_far))
     near = call(combine_kernel, [(2, rows // 2, HD)], [vmem], "combine")(parts)
     with jax.named_scope("gather_attended"):
         far = lax.ppermute(near, "zh", swap)

time: 121 us -> 117 us (0.967)
  waiting for transfers between devices: 16.8 us -> 8.22 us
  blocking collectives: 62 us -> 65.7 us
    all_to_all x1, waiting for transfers between devices: 14.6 us -> 0.29 us  [shards(): parts = lax.all_to_all(parts, 'span', 0, 0, tiled=True)]
    ppermute x1, waiting for transfers between devices: 0.01 us -> 6.01 us  [shards(): weight_far = lax.ppermute(weight, 'y0', swap)]
    all_to_all x1, blocking collectives: 13.7 us -> 18.7 us  [shards(): both = lax.all_to_all(both, ROW, 0, 0, tiled=True)[:width // HD]]
  transfers between devices with their start and end apart: 5 -> 5, of which waited for: 2 -> 3; matrix products, arithmetic and copies ran while one was open for 0% -> 0% of each run, Pallas kernels for 0% -> 0%
where the time goes in v8:
time: 117 us; the launch traced here: 116 us
  blocking collectives  65.7 us (56%)
  starting transfers between devices  30.6 us (26%)
  waiting for transfers between devices  8.22 us (7%)
  Pallas kernels  7.98 us (7%)
  local copies, waits for them, and re-layouts  3.19 us (3%)
    all_to_all x1, blocking collectives, shards(): both = lax.all_to_all(both, ROW, 0, 0, tiled=True)[:width // HD]  18.7 us
    all_to_all x1, blocking collectives, shards(): pieces = lax.all_to_all(pieces, ('head', 'y0'), 0, 0, tiled=True)  16.6 us
    all_to_all x1, blocking collectives, shards(): packed = lax.all_to_all(packed, ROW, 0, 0, tiled=True)  16.5 us
    ppermute x1, starting transfers between devices, shards(): kv_far = lax.ppermute(kv, 'zh', swap)  11.6 us
    ppermute x1, starting transfers between devices, shards(): far = lax.ppermute(near, 'zh', swap)  8.17 us
    all_gather x1, blocking collectives, shards(): both = lax.all_gather(both, 'core', axis=0, tiled=True)  7.04 us
    ppermute x1, waiting for transfers between devices, shards(): weight_far = lax.ppermute(weight, 'y0', swap)  6.01 us
    all_gather x1, blocking collectives, shards(): near = lax.all_gather(kv, 'core', axis=0, tiled=True)  4.7 us
  transfers between devices with their start and end apart: 5, of which 3 were waited for; matrix products, arithmetic and copies ran while one was open for 0% of the time, Pallas kernels for 0%

profile of v8, /device:TPU:1, one launch (start us, length us, event | category | flops | bytes accessed | tf_op | source)
XLA Modules:
  0.0 115.8 jit_solution(10020145012707068916)
XLA Ops:
  0.0 0.0 copy-start.2
  0.0 0.8 copy-done.2
  0.8 0.0 copy-start.3
  0.8 0.8 copy-done.3
  1.7 0.0 copy-start.4
  1.7 0.8 copy-done.4
  2.5 16.5 %all_to_all.25.packed_ref = bf16[8,3,40,128]{3,2,1,0:T(8,128)(2,1)S(1)} all-to-all(bf16[8,3,40,128]{3,2,1,0:T(8,128)(2,1)S(1)} %pack.1), channel_id=1, replica_groups=mesh['span'=4,'zh'=2,'y2'=2,'y1'=2,'y0'=2,'core'=2,'head'=4] {'y2','y1',..., dimensions={0} | all-to-all | bytes 491520 | tf_op jit(solution)/shard_map/exchange_heads/all_to_all | solution.py:158
  19.0 0.8 unpack.1
  19.8 11.6 %collective-permute-start = (bf16[2,320,128]{2,1,0:T(8,128)(2,1)S(1)}, bf16[2,320,128]{2,1,0:T(8,128)(2,1)S(1)}, u32[]{:S(2)}, u32[]{:S(2)}) collective-permute-start(bf16[2,320,128]{2,1,0:T(8,128)(2,1)S(1)} %bitcast.14), channel_id=1, source_target_pairs={{0,64},{64,0},{1,65},{65,1},{2,66},{66,2},{3,67},{67,3},{4,68},{68... | collective-permute-start | bytes 491528 | tf_op jit(solution)/shard_map/gather_kv/ppermute | solution.py:164
  31.4 4.0 %all-to-all-start.1 = ((bf16[4,320,128]{2,1,0:T(8,128)(2,1)}), bf16[4,320,128]{2,1,0:T(8,128)(2,1)S(1)}, u32[]{:S(2)}, u32[]{:S(2)}) async-start(bf16[4,320,128]{2,1,0:T(8,128)(2,1)} %bitcast.3), calls=%async_computation.1 | async-start | bytes 655360 | tf_op jit(solution)/shard_map/gather_q/all_to_all | solution.py:161
  35.4 4.7 %all_gather.9.near_ref = bf16[4,320,128]{2,1,0:T(8,128)(2,1)S(1)} all-gather(bf16[2,320,128]{2,1,0:T(8,128)(2,1)S(1)} %bitcast.15), channel_id=1, replica_groups=mesh['span'=4,'zh'=2,'y2'=2,'y1'=2,'y0'=2,'core'=2,'head'=4] {'core'}, dimensions={0}, use_global_device_ids=true | all-gather | bytes 491520 | tf_op jit(solution)/shard_map/gather_kv/all_gather | solution.py:165
  40.1 0.0 copy-start.6
  40.1 0.0 copy-start.7
  40.1 0.0 collective-permute-done
  40.1 2.2 %all_gather.10.far_ref = bf16[4,320,128]{2,1,0:T(8,128)(2,1)S(1)} all-gather(bf16[2,320,128]{2,1,0:T(8,128)(2,1)S(1)} %collective-permute-done), channel_id=1, replica_groups=mesh['span'=4,'zh'=2,'y2'=2,'y1'=2,'y0'=2,'core'=2,'head'=4] {'core'}, dimensions={0}, use_global_device_ids=true | all-gather | bytes 491520 | tf_op jit(solution)/shard_map/gather_kv/all_gather | solution.py:166
  42.3 0.0 all-to-all-done.1.q_ref
  42.3 0.0 copy-done.6
  42.3 0.0 copy-done.7
  42.3 4.2 %attend.1 = bf16[4,320,256]{2,1,0:T(8,128)(2,1)} custom-call(s32[4]{0:T(128)S(1)} %copy-done.6, s32[4]{0:T(128)S(1)} %copy-done.7, bf16[4,320,128]{2,1,0:T(8,128)(2,1)S(1)} %all-to-all-done.1.q_ref, bf16[4,320,128]{2,1,0:T(8,128)(2,1)S(1)} %all_gather.9.near_ref, bf16[4,320,128]{2,1,0:T(8,128)(2,1)S(1)} %all_gather.10.far_ref), custom_call_target="tpu_custom_call" | custom-call | tf_op jit(solution)/shard_map/attend/pallas_call | solution.py:170
  46.5 0.0 copy-start
  46.5 4.7 %all-to-all-start.2 = ((bf16[4,320,256]{2,1,0:T(8,128)(2,1)}), bf16[4,320,256]{2,1,0:T(8,128)(2,1)S(1)}, u32[]{:S(2)}, u32[]{:S(2)}) async-start(bf16[4,320,256]{2,1,0:T(8,128)(2,1)} %attend.1), calls=%async_computation.2 | async-start | bytes 1310720 | tf_op jit(solution)/shard_map/return_parts/all_to_all | solution.py:174
  51.1 0.0 copy-done
  51.1 2.2 %collective-permute-start.1 = (bf16[192,768]{1,0:T(8,128)(2,1)S(1)}, bf16[192,768]{1,0:T(8,128)(2,1)S(1)}, u32[]{:S(2)}, u32[]{:S(2)}) collective-permute-start(bf16[192,768]{1,0:T(8,128)(2,1)S(1)} %bitcast.12), channel_id=1, source_target_pairs={{0,8},{8,0},{1,9},{9,1},{2,10},{10,2},{3,11},{11,3},{4,12},{12,4},... | collective-permute-start | bytes 884744 | tf_op jit(solution)/shard_map/fetch_weight/ppermute | solution.py:169
  53.3 6.0 %collective-permute-done.1.far_ref = bf16[192,768]{1,0:T(8,128)(2,1)S(1)} collective-permute-done((bf16[192,768]{1,0:T(8,128)(2,1)S(1)}, bf16[192,768]{1,0:T(8,128)(2,1)S(1)}, u32[]{:S(2)}, u32[]{:S(2)}) %collective-permute-start.1) | collective-permute-done | bytes 294944 | tf_op jit(solution)/shard_map/fetch_weight/ppermute | solution.py:169
  59.3 0.3 all-to-all-done.2.parts_ref
  59.6 0.6 combine.1.near_ref
  60.2 8.2 %collective-permute-start.2 = (bf16[2,160,128]{2,1,0:T(8,128)(2,1)S(1)}, bf16[2,160,128]{2,1,0:T(8,128)(2,1)S(1)}, u32[]{:S(2)}, u32[]{:S(2)}) collective-permute-start(bf16[2,160,128]{2,1,0:T(8,128)(2,1)S(1)} %combine.1.near_ref), channel_id=1, source_target_pairs={{0,64},{64,0},{1,65},{65,1},{2,66},{66,2},{3,67},{67,3},{4,68},{68... | collective-permute-start | bytes 245768 | tf_op jit(solution)/shard_map/gather_attended/ppermute | solution.py:178
  68.4 1.9 %collective-permute-done.2.far_ref = bf16[2,160,128]{2,1,0:T(8,128)(2,1)S(1)} collective-permute-done((bf16[2,160,128]{2,1,0:T(8,128)(2,1)S(1)}, bf16[2,160,128]{2,1,0:T(8,128)(2,1)S(1)}, u32[]{:S(2)}, u32[]{:S(2)}) %collective-permute-start.2) | collective-permute-done | bytes 81952 | tf_op jit(solution)/shard_map/gather_attended/ppermute | solution.py:178
  70.3 0.1 spread.1
  70.4 18.7 %all_to_all.26 = bf16[8,2,160,128]{3,2,1,0:T(8,128)(2,1)S(1)} all-to-all(bf16[8,2,160,128]{3,2,1,0:T(8,128)(2,1)S(1)} %spread.1), channel_id=1, replica_groups=mesh['span'=4,'zh'=2,'y2'=2,'y1'=2,'y0'=2,'core'=2,'head'=4] {'y2','y1',..., dimensions={0} | all-to-all | bytes 1310720 | tf_op jit(solution)/shard_map/gather_attended/all_to_all | solution.py:180
  89.2 7.0 %all_gather.11.rows_ref = bf16[12,2,160,128]{3,2,1,0:T(8,128)(2,1)S(1)} all-gather(bf16[6,2,160,128]{3,2,1,0:T(8,128)(2,1)S(1)} %slice.4), channel_id=1, replica_groups=mesh['span'=4,'zh'=2,'y2'=2,'y1'=2,'y0'=2,'core'=2,'head'=4] {'core'}, dimensions={0}, use_global_device_ids=true | all-gather | bytes 1474560 | tf_op jit(solution)/shard_map/gather_attended/all_gather | solution.py:181
  96.2 0.9 project.1
  97.1 0.0 copy-start.1
  97.2 0.0 copy-start.5
  97.2 16.6 %all_to_all.27.pieces_ref = bf16[8,240,128]{2,1,0:T(8,128)(2,1)S(1)} all-to-all(bf16[8,240,128]{2,1,0:T(8,128)(2,1)S(1)} %project.1), channel_id=1, replica_groups=mesh['span'=4,'zh'=2,'y2'=2,'y1'=2,'y0'=2,'core'=2,'head'=4] {'head','y0'}, dimensions={0} | all-to-all | bytes 983040 | tf_op jit(solution)/shard_map/sum_heads/all_to_all | solution.py:187
  113.7 0.0 copy-start.8
  113.7 0.0 copy-done.1
  113.7 0.0 copy-done.5
  113.7 0.6 copy-done.8
  114.4 1.4 %finish.1 = bf16[192,320]{1,0:T(8,128)(2,1)} custom-call(s32[4]{0:T(128)S(1)} %copy-done.8, bf16[8,240,128]{2,1,0:T(8,128)(2,1)S(1)} %all_to_all.27.pieces_ref, f32[4,192]{1,0:T(4,128)S(1)} %copy-done.5, bf16[192,320]{1,0:T(8,128)(2,1)S(1)} %bitcast.16), custom_call_target="tpu_custom_call" | custom-call | tf_op jit(solution)/shard_map/finish/pallas_call | solution.py:188
  (2 shorter events, 0.1 us)
Async XLA Ops:
  0.0 0.8 copy-start.2
  0.8 0.8 copy-start.3
  1.7 0.8 copy-start.4
  19.8 20.3 %collective-permute-start = (bf16[2,320,128]{2,1,0:T(8,128)(2,1)S(1)}, bf16[2,320,128]{2,1,0:T(8,128)(2,1)S(1)}, u32[]{:S(2)}, u32[]{:S(2)}) collective-permute-start(bf16[2,320,128]{2,1,0:T(8,128)(2,1)S(1)} %bitcast.14), channel_id=1, source_target_pairs={{0,64},{64,0},{1,65},{65,1},{2,66},{66,2},{3,67},{67,3},{4,68},{68... | collective-permute-start | bytes 491528 | tf_op jit(solution)/shard_map/gather_kv/ppermute | solution.py:164
  31.4 10.9 %all-to-all-start.1 = ((bf16[4,320,128]{2,1,0:T(8,128)(2,1)}), bf16[4,320,128]{2,1,0:T(8,128)(2,1)S(1)}, u32[]{:S(2)}, u32[]{:S(2)}) async-start(bf16[4,320,128]{2,1,0:T(8,128)(2,1)} %bitcast.3), calls=%async_computation.1 | async-start | bytes 655360 | tf_op jit(solution)/shard_map/gather_q/all_to_all | solution.py:161
  40.1 2.2 %copy-start.6 = (s32[4]{0:T(128)S(1)}, s32[4]{0:T(128)}, u32[]{:S(2)}) copy-start(s32[4]{0:T(128)} %order_ref.1) | copy-start | bytes 52
  40.1 2.2 %copy-start.7 = (s32[4]{0:T(128)S(1)}, s32[4]{0:T(128)}, u32[]{:S(2)}) copy-start(s32[4]{0:T(128)} %valid_ref.1) | copy-start | bytes 52
  46.5 4.7 %copy-start = (bf16[768,192]{0,1:T(8,128)(2,1)S(1)}, bf16[768,192]{0,1:T(8,128)(2,1)}, u32[]{:S(2)}) copy-start(bf16[768,192]{0,1:T(8,128)(2,1)} %param.16) | copy-start | bytes 884740
  46.5 13.1 %all-to-all-start.2 = ((bf16[4,320,256]{2,1,0:T(8,128)(2,1)}), bf16[4,320,256]{2,1,0:T(8,128)(2,1)S(1)}, u32[]{:S(2)}, u32[]{:S(2)}) async-start(bf16[4,320,256]{2,1,0:T(8,128)(2,1)} %attend.1), calls=%async_computation.2 | async-start | bytes 1310720 | tf_op jit(solution)/shard_map/return_parts/all_to_all | solution.py:174
  51.1 8.2 %collective-permute-start.1 = (bf16[192,768]{1,0:T(8,128)(2,1)S(1)}, bf16[192,768]{1,0:T(8,128)(2,1)S(1)}, u32[]{:S(2)}, u32[]{:S(2)}) collective-permute-start(bf16[192,768]{1,0:T(8,128)(2,1)S(1)} %bitcast.12), channel_id=1, source_target_pairs={{0,8},{8,0},{1,9},{9,1},{2,10},{10,2},{3,11},{11,3},{4,12},{12,4},... | collective-permute-start | bytes 884744 | tf_op jit(solution)/shard_map/fetch_weight/ppermute | solution.py:169
  60.2 10.1 %collective-permute-start.2 = (bf16[2,160,128]{2,1,0:T(8,128)(2,1)S(1)}, bf16[2,160,128]{2,1,0:T(8,128)(2,1)S(1)}, u32[]{:S(2)}, u32[]{:S(2)}) collective-permute-start(bf16[2,160,128]{2,1,0:T(8,128)(2,1)S(1)} %combine.1.near_ref), channel_id=1, source_target_pairs={{0,64},{64,0},{1,65},{65,1},{2,66},{66,2},{3,67},{67,3},{4,68},{68... | collective-permute-start | bytes 245768 | tf_op jit(solution)/shard_map/gather_attended/ppermute | solution.py:178
  97.1 16.6 %copy-start.1 = (bf16[1,320,192]{1,2,0:T(8,128)(2,1)S(1)}, bf16[1,320,192]{1,2,0:T(8,128)(2,1)}, u32[]{:S(2)}) copy-start(bf16[1,320,192]{1,2,0:T(8,128)(2,1)} %param.17) | copy-start | bytes 368644
  97.2 16.6 %copy-start.5 = (f32[4,192]{1,0:T(4,128)S(1)}, f32[4,192]{1,0:T(4,128)}, u32[]{:S(2)}) copy-start(f32[4,192]{1,0:T(4,128)} %gate_ref.1) | copy-start | bytes 9220
  113.7 0.7 copy-start.8

commit v9 on v7

--- a/solution.py
+++ b/solution.py
@@ -26,12 +26,16 @@
                 out_ref[h, i] = jnp.zeros(out_ref.shape[2:], out_ref.dtype)
 
 
-def unpack_kernel(packed_ref, queries_ref, kv_ref):
+def keep_kv_kernel(packed_ref, kv_ref):
+    for y in range(packed_ref.shape[0]):
+        for i in range(2):
+            kv_ref[i, y] = packed_ref[y, 1 + i]
+
+
+def repeat_q_kernel(packed_ref, queries_ref):
     for y in range(packed_ref.shape[0]):
         for i in range(queries_ref.shape[0]):
             queries_ref[i, y] = packed_ref[y, 0]
-        for i in range(2):
-            kv_ref[i, y] = packed_ref[y, 1 + i]
 
 
 def attend_kernel(order_ref, valid_ref, q_ref, near_ref, far_ref, out_ref):
@@ -88,28 +92,31 @@
         out_ref[y, 1] = far_ref[place]
 
 
-def project_kernel(rows_ref, weights_ref, out_ref):
+def project_kernel(rows_ref, near_ref, far_ref, out_ref):
     zh = lax.axis_index("zh")
-    heads = weights_ref.shape[2] // HD
+    mine = 2 * lax.axis_index("y1") + lax.axis_index("y0")
+    heads = near_ref.shape[2] // HD
     rows = rows_ref.shape[2]
+    slots = rows_ref.shape[0] // 2
     half = rows // 2
     left = jnp.concatenate(
         [
-            jnp.concatenate([rows_ref[c * heads + h, side] for h in range(heads)], axis=1)
+            jnp.concatenate([rows_ref[c * slots + h, side] for h in range(heads)], axis=1)
             for side in range(2)
             for c in range(2)
         ]
     )
-    places = weights_ref.shape[0]
-    for place in range(places):
+    places = 4
+    for turn in range(places):
+        weight = (far_ref if turn > 1 else near_ref)[turn % 2]
         product = lax.dot_general(
-            left, weights_ref[place], (((1,), (1,)), ((), ())), preferred_element_type=jnp.float32
+            left, weight, (((1,), (1,)), ((), ())), preferred_element_type=jnp.float32
         )
         for side in range(2):
             for y2 in range(2):
                 a = 2 * side * rows + y2 * half
                 first, second = product[a : a + half], product[a + rows : a + rows + half]
-                slot = (2 * (zh ^ side) + y2) * places + place
+                slot = (2 * (zh ^ side) + y2) * places + (mine ^ turn)
                 main = jnp.concatenate([first[:, :HD], second[:, :HD]])
                 out_ref[slot, :rows, :] = main.astype(jnp.bfloat16)
                 tail = jnp.concatenate([first[:, HD:], second[:, HD:]], axis=1)
@@ -160,17 +167,20 @@
     packed = call(pack_kernel, [(ny, 3, tokens, HD)], [vmem] * 3, "pack")(q[0], k[0], v[0])
     with jax.named_scope("exchange_heads"):
         packed = lax.all_to_all(packed, ROW, 0, 0, tiled=True)
-    queries, kv = call(unpack_kernel, [(nx, ny, tokens, HD), (2, ny, tokens, HD)], [vmem], "unpack")(packed)
+    with jax.named_scope("gather_kv"):
+        kv = call(keep_kv_kernel, [(2, ny, tokens, HD)], [vmem], "keep_kv")(packed).reshape(2, rows, HD)
+        kv_far = lax.ppermute(kv, "zh", swap)
     with jax.named_scope("gather_q"):
+        packed, kv = lax.optimization_barrier((packed, kv))
+        queries = call(repeat_q_kernel, [(nx, ny, tokens, HD)], [vmem], "repeat_q")(packed)
         queries = lax.all_to_all(queries.reshape(nx, rows, HD), "span", 0, 0, tiled=True)
     with jax.named_scope("gather_kv"):
-        kv = kv.reshape(2, rows, HD)
-        kv_far = lax.ppermute(kv, "zh", swap)
         near = lax.all_gather(kv, "core", axis=0, tiled=True)
         far = lax.all_gather(kv_far, "core", axis=0, tiled=True)
     with jax.named_scope("fetch_weight"):
-        weight, kv = lax.optimization_barrier((out_weight.T, kv))
-        weights = lax.all_gather(weight, ("y1", "y0"), axis=0, tiled=False)
+        weight = out_weight.T
+        weights = jnp.stack([weight, lax.ppermute(weight, "y0", swap)])
+        weights_far = lax.ppermute(weights, "y1", swap)
     parts = call(attend_kernel, [(nx, rows, 2 * HD)], [smem, smem, vmem, vmem, vmem], "attend")(
         block_order, valid_frames, queries, near, far
     )
@@ -179,11 +189,14 @@
     near = call(combine_kernel, [(4, rows // 4, HD)], [vmem], "combine")(parts)
     with jax.named_scope("gather_attended"):
         far = lax.ppermute(near, "zh", swap)
+        far, weights_far = lax.optimization_barrier((far, weights_far))
         both = call(spread_kernel, [(ny, 2, rows // 4, HD)], [vmem, vmem], "spread")(near, far)
-        both = lax.all_to_all(both, ROW, 0, 0, tiled=True)[: width // HD]
+        both = lax.all_to_all(both, ROW, 0, 0, tiled=True)
         both = lax.all_gather(both, "core", axis=0, tiled=True)
     cols = weight.shape[0]
-    pieces = call(project_kernel, [(16, 2 * tokens * cols // HD, HD)], [vmem] * 2, "project")(both, weights)
+    pieces = call(project_kernel, [(16, 2 * tokens * cols // HD, HD)], [vmem] * 3, "project")(
+        both, weights, weights_far
+    )
     with jax.named_scope("sum_heads"):
         pieces = lax.all_to_all(pieces, ("head", "y1", "y0"), 0, 0, tiled=True)
     mixed = pl.pallas_call(

time: 125 us -> 118 us (0.944)
  between operations: 13.5 us -> 0.11 us
  blocking collectives: 75.6 us -> 62.4 us
  waiting for transfers between devices: 1.94 us -> 12.9 us
  starting transfers between devices: 23.1 us -> 30.9 us
    all_to_all x2 -> x1, blocking collectives: 28.9 us -> 13.8 us  [shards(): both = lax.all_to_all(both, ROW, 0, 0, tiled=True)]
    all_to_all x0 -> x1, starting transfers between devices: none -> 7.78 us  [shards(): packed = lax.all_to_all(packed, ROW, 0, 0, tiled=True)]
    all_to_all x0 -> x1, waiting for transfers between devices: none -> 5.85 us  [shards(): packed = lax.all_to_all(packed, ROW, 0, 0, tiled=True)]
    ppermute x0 -> x2, starting transfers between devices: none -> 5.28 us  [the longest x1 3.36 us: shards(): weights = jnp.stack([weight, lax.ppermute(weight, 'y0', swap)])]
    ppermute x1, waiting for transfers between devices: 1.91 us -> 7.09 us  [shards(): far = lax.ppermute(near, 'zh', swap)]
    ppermute x1, starting transfers between devices: 7.48 us -> 2.38 us  [shards(): far = lax.ppermute(near, 'zh', swap)]
    all_gather x1, blocking collectives: 4.7 us -> 5.99 us  [shards(): near = lax.all_gather(kv, 'core', axis=0, tiled=True)]
  transfers between devices with their start and end apart: 4 -> 6, of which waited for: 1 -> 2; matrix products, arithmetic and copies ran while one was open for 0% -> 0% of each run, Pallas kernels for 3% -> 4%
where the time goes in v9:
time: 118 us; the launch traced here: 117 us
  blocking collectives  62.4 us (53%)
  starting transfers between devices  30.9 us (26%)
  waiting for transfers between devices  12.9 us (11%)
  Pallas kernels  7.6 us (6%)
  local copies, waits for them, and re-layouts  3.16 us (3%)
    all_to_all x1, blocking collectives, shards(): pieces = lax.all_to_all(pieces, ('head', 'y1', 'y0'), 0, 0, tiled=True)  19.8 us
    all_to_all x1, blocking collectives, shards(): parts = lax.all_to_all(parts, 'span', 0, 0, tiled=True)  14.3 us
    all_to_all x1, blocking collectives, shards(): both = lax.all_to_all(both, ROW, 0, 0, tiled=True)  13.8 us
    ppermute x1, starting transfers between devices, shards(): kv_far = lax.ppermute(kv, 'zh', swap)  11.4 us
    all_to_all x1, starting transfers between devices, shards(): packed = lax.all_to_all(packed, ROW, 0, 0, tiled=True)  7.78 us
    ppermute x1, waiting for transfers between devices, shards(): far = lax.ppermute(near, 'zh', swap)  7.09 us
    all_gather x1, blocking collectives, shards(): both = lax.all_gather(both, 'core', axis=0, tiled=True)  6.25 us
    all_gather x1, blocking collectives, shards(): near = lax.all_gather(kv, 'core', axis=0, tiled=True)  5.99 us
  transfers between devices with their start and end apart: 6, of which 2 were waited for; matrix products, arithmetic and copies ran while one was open for 0% of the time, Pallas kernels for 4%

profile of v9, /device:TPU:1, one launch (start us, length us, event | category | flops | bytes accessed | tf_op | source)
XLA Modules:
  0.0 117.1 jit_solution(3207302389925307345)
XLA Ops:
  0.0 0.0 copy-start.1
  0.0 0.8 copy-done.1
  0.8 0.0 copy-start.2
  0.8 0.8 copy-done.2
  1.7 0.0 copy-start.3
  1.7 0.8 copy-done.3
  2.5 0.7 pack.1
  3.2 0.0 copy-start.8
  3.2 7.8 %all-to-all-start = ((bf16[8,3,40,128]{3,2,1,0:T(8,128)(2,1)}), bf16[8,3,40,128]{3,2,1,0:T(8,128)(2,1)S(1)}, u32[]{:S(2)}, u32[]{:S(2)}) async-start(bf16[8,3,40,128]{3,2,1,0:T(8,128)(2,1)} %pack.1), calls=%async_computation | async-start | bytes 491520 | tf_op jit(solution)/shard_map/exchange_heads/all_to_all | solution.py:169
  11.0 0.0 copy-done.8
  11.0 3.4 %collective-permute-start.2 = (bf16[192,768]{1,0:T(8,128)(2,1)S(1)}, bf16[192,768]{1,0:T(8,128)(2,1)S(1)}, u32[]{:S(2)}, u32[]{:S(2)}) collective-permute-start(bf16[192,768]{1,0:T(8,128)(2,1)S(1)} %bitcast.21), channel_id=1, source_target_pairs={{0,8},{8,0},{1,9},{9,1},{2,10},{10,2},{3,11},{11,3},{4,12},{12,4},... | collective-permute-start | bytes 884744 | tf_op jit(solution)/shard_map/fetch_weight/ppermute | solution.py:182
  14.4 5.8 %all-to-all-done.packed_ref = bf16[8,3,40,128]{3,2,1,0:T(8,128)(2,1)S(1)} async-done(((bf16[8,3,40,128]{3,2,1,0:T(8,128)(2,1)}), bf16[8,3,40,128]{3,2,1,0:T(8,128)(2,1)S(1)}, u32[]{:S(2)}, u32[]{:S(2)}) %all-to-all-start) | async-done | bytes 245792 | tf_op jit(solution)/shard_map/exchange_heads/all_to_all | solution.py:169
  20.2 11.4 %collective-permute-start = (bf16[2,320,128]{2,1,0:T(8,128)(2,1)S(1)}, bf16[2,320,128]{2,1,0:T(8,128)(2,1)S(1)}, u32[]{:S(2)}, u32[]{:S(2)}) collective-permute-start(bf16[2,320,128]{2,1,0:T(8,128)(2,1)S(1)} %bitcast.15), channel_id=1, source_target_pairs={{0,64},{64,0},{1,65},{65,1},{2,66},{66,2},{3,67},{67,3},{4,68},{68... | collective-permute-start | bytes 491528 | tf_op jit(solution)/shard_map/gather_kv/ppermute | solution.py:172
  31.7 0.8 repeat_q.1
  32.4 4.0 %all-to-all-start.1 = ((bf16[4,320,128]{2,1,0:T(8,128)(2,1)}), bf16[4,320,128]{2,1,0:T(8,128)(2,1)S(1)}, u32[]{:S(2)}, u32[]{:S(2)}) async-start(bf16[4,320,128]{2,1,0:T(8,128)(2,1)} %bitcast.4), calls=%async_computation.1 | async-start | bytes 655360 | tf_op jit(solution)/shard_map/gather_q/all_to_all | solution.py:176
  36.5 0.0 collective-permute-done.2
  36.5 0.1 pad_maximum_fusion.near_ref
  36.5 1.9 %collective-permute-start.3 = (bf16[2,192,768]{2,1,0:T(8,128)(2,1)S(1)}, bf16[2,192,768]{2,1,0:T(8,128)(2,1)S(1)}, u32[]{:S(2)}, u32[]{:S(2)}) collective-permute-start(bf16[2,192,768]{2,1,0:T(8,128)(2,1)S(1)} %pad_maximum_fusion.near_ref), channel_id=1, source_target_pairs={{0,16},{16,0},{1,17},{17,1},{2,18},{18,2},{3,19},{19,3},{4,20},{20... | collective-permute-start | bytes 1769480 | tf_op jit(solution)/shard_map/fetch_weight/ppermute | solution.py:183
  38.4 6.0 %all_gather.9.near_ref = bf16[4,320,128]{2,1,0:T(8,128)(2,1)S(1)} all-gather(bf16[2,320,128]{2,1,0:T(8,128)(2,1)S(1)} %bitcast.16), channel_id=1, replica_groups=mesh['span'=4,'zh'=2,'y2'=2,'y1'=2,'y0'=2,'core'=2,'head'=4] {'core'}, dimensions={0}, use_global_device_ids=true | all-gather | bytes 491520 | tf_op jit(solution)/shard_map/gather_kv/all_gather | solution.py:178
  44.4 0.0 copy-start.5
  44.4 0.0 copy-start.6
  44.4 0.0 collective-permute-done
  44.4 2.2 %all_gather.10.far_ref = bf16[4,320,128]{2,1,0:T(8,128)(2,1)S(1)} all-gather(bf16[2,320,128]{2,1,0:T(8,128)(2,1)S(1)} %collective-permute-done), channel_id=1, replica_groups=mesh['span'=4,'zh'=2,'y2'=2,'y1'=2,'y0'=2,'core'=2,'head'=4] {'core'}, dimensions={0}, use_global_device_ids=true | all-gather | bytes 491520 | tf_op jit(solution)/shard_map/gather_kv/all_gather | solution.py:179
  46.6 0.0 all-to-all-done.1.q_ref
  46.6 0.0 copy-done.5
  46.6 0.0 copy-done.6
  46.6 3.3 %attend.1 = bf16[4,320,256]{2,1,0:T(8,128)(2,1)S(1)} custom-call(s32[4]{0:T(128)S(1)} %copy-done.5, s32[4]{0:T(128)S(1)} %copy-done.6, bf16[4,320,128]{2,1,0:T(8,128)(2,1)S(1)} %all-to-all-done.1.q_ref, bf16[4,320,128]{2,1,0:T(8,128)(2,1)S(1)} %all_gather.9.near_ref, bf16[4,320,128]{2,1,0:T(8,128)(2,1)S(1)} %all_gather.10.far_ref), custom_call_target="tpu_custom_call" | custom-call | tf_op jit(solution)/shard_map/attend/pallas_call | solution.py:184
  49.9 14.3 %all_to_all.25.parts_ref = bf16[4,320,256]{2,1,0:T(8,128)(2,1)S(1)} all-to-all(bf16[4,320,256]{2,1,0:T(8,128)(2,1)S(1)} %attend.1), channel_id=1, replica_groups=mesh['span'=4,'zh'=2,'y2'=2,'y1'=2,'y0'=2,'core'=2,'head'=4] {'span'}, dimensions={0} | all-to-all | bytes 1310720 | tf_op jit(solution)/shard_map/return_parts/all_to_all | solution.py:188
  64.3 0.5 combine.1.near_ref
  64.8 2.4 %collective-permute-start.1 = (bf16[4,80,128]{2,1,0:T(8,128)(2,1)S(1)}, bf16[4,80,128]{2,1,0:T(8,128)(2,1)S(1)}, u32[]{:S(2)}, u32[]{:S(2)}) collective-permute-start(bf16[4,80,128]{2,1,0:T(8,128)(2,1)S(1)} %combine.1.near_ref), channel_id=1, source_target_pairs={{0,64},{64,0},{1,65},{65,1},{2,66},{66,2},{3,67},{67,3},{4,68},{68... | collective-permute-start | bytes 245768 | tf_op jit(solution)/shard_map/gather_attended/ppermute | solution.py:191
  67.2 0.0 collective-permute-done.3.far_ref
  67.2 7.1 %collective-permute-done.1.far_ref = bf16[4,80,128]{2,1,0:T(8,128)(2,1)S(1)} collective-permute-done((bf16[4,80,128]{2,1,0:T(8,128)(2,1)S(1)}, bf16[4,80,128]{2,1,0:T(8,128)(2,1)S(1)}, u32[]{:S(2)}, u32[]{:S(2)}) %collective-permute-start.1) | collective-permute-done | bytes 81952 | tf_op jit(solution)/shard_map/gather_attended/ppermute | solution.py:191
  74.4 13.8 %all_to_all.26 = bf16[8,2,80,128]{3,2,1,0:T(8,128)(2,1)S(1)} all-to-all(bf16[8,2,80,128]{3,2,1,0:T(8,128)(2,1)S(1)} %spread.1), channel_id=1, replica_groups=mesh['span'=4,'zh'=2,'y2'=2,'y1'=2,'y0'=2,'core'=2,'head'=4] {'y2','y1',..., dimensions={0} | all-to-all | bytes 655360 | tf_op jit(solution)/shard_map/gather_attended/all_to_all | solution.py:194
  88.2 6.3 %all_gather.11.rows_ref = bf16[16,2,80,128]{3,2,1,0:T(8,128)(2,1)S(1)} all-gather(bf16[8,2,80,128]{3,2,1,0:T(8,128)(2,1)S(1)} %all_to_all.26), channel_id=1, replica_groups=mesh['span'=4,'zh'=2,'y2'=2,'y1'=2,'y0'=2,'core'=2,'head'=4] {'core'}, dimensions={0}, use_global_device_ids=true | all-gather | bytes 983040 | tf_op jit(solution)/shard_map/gather_attended/all_gather | solution.py:195
  94.4 0.8 project.1
  95.2 0.0 copy-start
  95.2 0.0 copy-start.4
  95.2 19.8 %all_to_all.27.pieces_ref = bf16[16,120,128]{2,1,0:T(8,128)(2,1)S(1)} all-to-all(bf16[16,120,128]{2,1,0:T(8,128)(2,1)S(1)} %project.1), channel_id=1, replica_groups=mesh['span'=4,'zh'=2,'y2'=2,'y1'=2,'y0'=2,'core'=2,'head'=4] {'head','y1..., dimensions={0} | all-to-all | bytes 983040 | tf_op jit(solution)/shard_map/sum_heads/all_to_all | solution.py:201
  115.1 0.0 copy-start.7
  115.1 0.0 copy-done
  115.1 0.0 copy-done.4
  115.1 0.6 copy-done.7
  115.7 1.4 %finish.1 = bf16[192,320]{1,0:T(8,128)(2,1)} custom-call(s32[4]{0:T(128)S(1)} %copy-done.7, bf16[16,120,128]{2,1,0:T(8,128)(2,1)S(1)} %all_to_all.27.pieces_ref, f32[4,192]{1,0:T(4,128)S(1)} %copy-done.4, bf16[192,320]{1,0:T(8,128)(2,1)S(1)} %bitcast.17), custom_call_target="tpu_custom_call" | custom-call | tf_op jit(solution)/shard_map/finish/pallas_call | solution.py:202
  (2 shorter events, 0.1 us)
Async XLA Ops:
  0.0 0.8 copy-start.1
  0.8 0.8 copy-start.2
  1.7 0.8 copy-start.3
  3.2 7.8 %copy-start.8 = (bf16[768,192]{0,1:T(8,128)(2,1)S(1)}, bf16[768,192]{0,1:T(8,128)(2,1)}, u32[]{:S(2)}) copy-start(bf16[768,192]{0,1:T(8,128)(2,1)} %param.16) | copy-start | bytes 884740
  3.2 17.0 %all-to-all-start = ((bf16[8,3,40,128]{3,2,1,0:T(8,128)(2,1)}), bf16[8,3,40,128]{3,2,1,0:T(8,128)(2,1)S(1)}, u32[]{:S(2)}, u32[]{:S(2)}) async-start(bf16[8,3,40,128]{3,2,1,0:T(8,128)(2,1)} %pack.1), calls=%async_computation | async-start | bytes 491520 | tf_op jit(solution)/shard_map/exchange_heads/all_to_all | solution.py:169
  11.0 25.4 %collective-permute-start.2 = (bf16[192,768]{1,0:T(8,128)(2,1)S(1)}, bf16[192,768]{1,0:T(8,128)(2,1)S(1)}, u32[]{:S(2)}, u32[]{:S(2)}) collective-permute-start(bf16[192,768]{1,0:T(8,128)(2,1)S(1)} %bitcast.21), channel_id=1, source_target_pairs={{0,8},{8,0},{1,9},{9,1},{2,10},{10,2},{3,11},{11,3},{4,12},{12,4},... | collective-permute-start | bytes 884744 | tf_op jit(solution)/shard_map/fetch_weight/ppermute | solution.py:182
  20.2 24.2 %collective-permute-start = (bf16[2,320,128]{2,1,0:T(8,128)(2,1)S(1)}, bf16[2,320,128]{2,1,0:T(8,128)(2,1)S(1)}, u32[]{:S(2)}, u32[]{:S(2)}) collective-permute-start(bf16[2,320,128]{2,1,0:T(8,128)(2,1)S(1)} %bitcast.15), channel_id=1, source_target_pairs={{0,64},{64,0},{1,65},{65,1},{2,66},{66,2},{3,67},{67,3},{4,68},{68... | collective-permute-start | bytes 491528 | tf_op jit(solution)/shard_map/gather_kv/ppermute | solution.py:172
  32.4 14.2 %all-to-all-start.1 = ((bf16[4,320,128]{2,1,0:T(8,128)(2,1)}), bf16[4,320,128]{2,1,0:T(8,128)(2,1)S(1)}, u32[]{:S(2)}, u32[]{:S(2)}) async-start(bf16[4,320,128]{2,1,0:T(8,128)(2,1)} %bitcast.4), calls=%async_computation.1 | async-start | bytes 655360 | tf_op jit(solution)/shard_map/gather_q/all_to_all | solution.py:176
  36.5 30.7 %collective-permute-start.3 = (bf16[2,192,768]{2,1,0:T(8,128)(2,1)S(1)}, bf16[2,192,768]{2,1,0:T(8,128)(2,1)S(1)}, u32[]{:S(2)}, u32[]{:S(2)}) collective-permute-start(bf16[2,192,768]{2,1,0:T(8,128)(2,1)S(1)} %pad_maximum_fusion.near_ref), channel_id=1, source_target_pairs={{0,16},{16,0},{1,17},{17,1},{2,18},{18,2},{3,19},{19,3},{4,20},{20... | collective-permute-start | bytes 1769480 | tf_op jit(solution)/shard_map/fetch_weight/ppermute | solution.py:183
  44.4 2.2 %copy-start.5 = (s32[4]{0:T(128)S(1)}, s32[4]{0:T(128)}, u32[]{:S(2)}) copy-start(s32[4]{0:T(128)} %order_ref.1) | copy-start | bytes 52
  44.4 2.2 %copy-start.6 = (s32[4]{0:T(128)S(1)}, s32[4]{0:T(128)}, u32[]{:S(2)}) copy-start(s32[4]{0:T(128)} %valid_ref.1) | copy-start | bytes 52
  64.8 9.5 %collective-permute-start.1 = (bf16[4,80,128]{2,1,0:T(8,128)(2,1)S(1)}, bf16[4,80,128]{2,1,0:T(8,128)(2,1)S(1)}, u32[]{:S(2)}, u32[]{:S(2)}) collective-permute-start(bf16[4,80,128]{2,1,0:T(8,128)(2,1)S(1)} %combine.1.near_ref), channel_id=1, source_target_pairs={{0,64},{64,0},{1,65},{65,1},{2,66},{66,2},{3,67},{67,3},{4,68},{68... | collective-permute-start | bytes 245768 | tf_op jit(solution)/shard_map/gather_attended/ppermute | solution.py:191
  95.2 19.8 %copy-start = (bf16[1,320,192]{1,2,0:T(8,128)(2,1)S(1)}, bf16[1,320,192]{1,2,0:T(8,128)(2,1)}, u32[]{:S(2)}) copy-start(bf16[1,320,192]{1,2,0:T(8,128)(2,1)} %param.17) | copy-start | bytes 368644
  95.2 19.8 %copy-start.4 = (f32[4,192]{1,0:T(4,128)S(1)}, f32[4,192]{1,0:T(4,128)}, u32[]{:S(2)}) copy-start(f32[4,192]{1,0:T(4,128)} %gate_ref.1) | copy-start | bytes 9220
  115.1 0.7 copy-start.7

commit v10 on v8

--- a/solution.py
+++ b/solution.py
@@ -1,3 +1,4 @@
+import functools
 import math
 
 import jax
@@ -10,6 +11,7 @@
 HD = 128
 CLOSED = -1e30
 LOWEST = -1e20
+SPACE = 16
 AXES = ("span", "zh", "y2", "y1", "y0", "core", "head")
 ROW = ("y2", "y1", "y0")
 FRAME = ("zh", "y2", "y1")
@@ -26,12 +28,16 @@
                 out_ref[h, i] = jnp.zeros(out_ref.shape[2:], out_ref.dtype)
 
 
-def unpack_kernel(packed_ref, queries_ref, kv_ref):
+def keep_kv_kernel(packed_ref, kv_ref):
+    for y in range(packed_ref.shape[0]):
+        for i in range(2):
+            kv_ref[i, y] = packed_ref[y, 1 + i]
+
+
+def repeat_q_kernel(packed_ref, queries_ref):
     for y in range(packed_ref.shape[0]):
         for i in range(queries_ref.shape[0]):
             queries_ref[i, y] = packed_ref[y, 0]
-        for i in range(2):
-            kv_ref[i, y] = packed_ref[y, 1 + i]
 
 
 def attend_kernel(order_ref, valid_ref, q_ref, near_ref, far_ref, out_ref):
@@ -51,6 +57,7 @@
     limit = jnp.where(place < 2 * rows, near_limit, far_limit)
     bias = jnp.where(inner < limit, 0.0, CLOSED)
     lane = lax.broadcasted_iota(jnp.int32, (rows, HD), 1)
+    stats = jnp.zeros((rows, HD), jnp.float32)
     scale = math.log2(math.e) / HD**0.5
     for block in range(blocks):
         closed = jnp.where(order_ref[span] <= order_ref[block], 0.0, CLOSED)
@@ -61,18 +68,39 @@
         w = jnp.exp2(s - top)
         total = jnp.sum(w, axis=1, keepdims=True)
         acc = jnp.dot(w.astype(jnp.bfloat16), values, preferred_element_type=jnp.float32)
+        out_ref[block, :rows, :] = acc.astype(jnp.bfloat16)
         coarse = total.astype(jnp.bfloat16).astype(jnp.float32)
-        stats = jnp.where(lane == 0, top, jnp.where(lane == 1, coarse, total - coarse))
-        out_ref[block, :, :HD] = acc.astype(jnp.bfloat16)
-        out_ref[block, :, HD:] = stats.astype(jnp.bfloat16)
+        stats = jnp.where(lane == SPACE * block, top, stats)
+        stats = jnp.where(lane == SPACE * block + 1, coarse, stats)
+        stats = jnp.where(lane == SPACE * block + 2, total - coarse, stats)
+    places = out_ref.shape[1] - rows
+    wide = jnp.concatenate([stats, jnp.zeros((places // SPACE * HD - rows, HD), jnp.float32)]).T
+    wide = wide.astype(jnp.bfloat16)
+    for block in range(blocks):
+        for i in range(places // SPACE):
+            piece = wide[SPACE * block : SPACE * (block + 1), i * HD : (i + 1) * HD]
+            out_ref[block, rows + SPACE * i : rows + SPACE * (i + 1), :] = piece
 
 
 def combine_kernel(parts_ref, out_ref):
-    stats = parts_ref[:, :, HD:].astype(jnp.float32)
-    top = stats[:, :, 0:1]
-    factor = jnp.exp2(top - jnp.max(top, axis=0, keepdims=True))
-    denominator = jnp.sum(factor * (stats[:, :, 1:2] + stats[:, :, 2:3]), axis=0)
-    summed = jnp.sum(factor * parts_ref[:, :, :HD].astype(jnp.float32), axis=0)
+    blocks = parts_ref.shape[0]
+    rows = out_ref.shape[0] * out_ref.shape[1]
+    count = (parts_ref.shape[1] - rows) // SPACE
+    wide = jnp.concatenate(
+        [
+            jnp.concatenate([parts_ref[b, rows + SPACE * i : rows + SPACE * (i + 1), :] for i in range(count)], axis=1)
+            for b in range(blocks)
+        ]
+    )
+    stats = wide.astype(jnp.float32).T[:rows]
+    tops = [stats[:, SPACE * b : SPACE * b + 1] for b in range(blocks)]
+    highest = functools.reduce(jnp.maximum, tops)
+    denominator, summed = 0.0, 0.0
+    for b in range(blocks):
+        factor = jnp.exp2(tops[b] - highest)
+        place = SPACE * b
+        denominator = denominator + factor * (stats[:, place + 1 : place + 2] + stats[:, place + 2 : place + 3])
+        summed = summed + factor * parts_ref[b, :rows, :].astype(jnp.float32)
     done = summed / denominator
     tokens = done.shape[0] // FRAMES
     for y0 in range(2):
@@ -156,18 +184,20 @@
     packed = call(pack_kernel, [(ny, 3, tokens, HD)], [vmem] * 3, "pack")(q[0], k[0], v[0])
     with jax.named_scope("exchange_heads"):
         packed = lax.all_to_all(packed, ROW, 0, 0, tiled=True)
-    queries, kv = call(unpack_kernel, [(nx, ny, tokens, HD), (2, ny, tokens, HD)], [vmem], "unpack")(packed)
+    with jax.named_scope("gather_kv"):
+        kv = call(keep_kv_kernel, [(2, ny, tokens, HD)], [vmem], "keep_kv")(packed).reshape(2, rows, HD)
+        kv_far = lax.ppermute(kv, "zh", swap)
     with jax.named_scope("gather_q"):
+        packed, kv = lax.optimization_barrier((packed, kv))
+        queries = call(repeat_q_kernel, [(nx, ny, tokens, HD)], [vmem], "repeat_q")(packed)
         queries = lax.all_to_all(queries.reshape(nx, rows, HD), "span", 0, 0, tiled=True)
     with jax.named_scope("gather_kv"):
-        kv = kv.reshape(2, rows, HD)
-        kv_far = lax.ppermute(kv, "zh", swap)
         near = lax.all_gather(kv, "core", axis=0, tiled=True)
         far = lax.all_gather(kv_far, "core", axis=0, tiled=True)
     with jax.named_scope("fetch_weight"):
         weight, near = lax.optimization_barrier((out_weight.T, near))
         weight_far = lax.ppermute(weight, "y0", swap)
-    parts = call(attend_kernel, [(nx, rows, 2 * HD)], [smem, smem, vmem, vmem, vmem], "attend")(
+    parts = call(attend_kernel, [(nx, rows + SPACE * -(-rows // HD), HD)], [smem, smem, vmem, vmem, vmem], "attend")(
         block_order, valid_frames, queries, near, far
     )
     with jax.named_scope("return_parts"):

time: 117 us -> 118 us (level)
  waiting for transfers between devices: 8.22 us -> 13.9 us
  starting transfers between devices: 30.6 us -> 25.4 us
    all_to_all x1, waiting for transfers between devices: 0.29 us -> 7.03 us  [shards(): parts = lax.all_to_all(parts, 'span', 0, 0, tiled=True)]
    ppermute x1, waiting for transfers between devices: 6.01 us -> 0.01 us  [shards(): weight_far = lax.ppermute(weight, 'y0', swap)]
    ppermute x1, starting transfers between devices: 8.17 us -> 2.98 us  [shards(): far = lax.ppermute(near, 'zh', swap)]
    ppermute x1, waiting for transfers between devices: 1.92 us -> 6.82 us  [shards(): far = lax.ppermute(near, 'zh', swap)]
    pallas_call x2 -> x3, Pallas kernels: 4.95 us -> 4.83 us  [the longest x1 4.06 us: shards(): call(attend_kernel, [(nx, rows + SPACE * -(-rows // HD), HD)], [smem, sme...]
  transfers between devices with their start and end apart: 5 -> 5, of which waited for: 3 -> 2; matrix products, arithmetic and copies ran while one was open for 0% -> 0% of each run, Pallas kernels for 0% -> 4%
where the time goes in v10:
time: 118 us; the launch traced here: 117 us
  blocking collectives  66.5 us (56%)
  starting transfers between devices  25.4 us (22%)
  waiting for transfers between devices  13.9 us (12%)
  Pallas kernels  8.26 us (7%)
  local copies, waits for them, and re-layouts  3.19 us (3%)
    all_to_all x1, blocking collectives, shards(): both = lax.all_to_all(both, ROW, 0, 0, tiled=True)[:width // HD]  19.1 us
    all_to_all x1, blocking collectives, shards(): pieces = lax.all_to_all(pieces, ('head', 'y0'), 0, 0, tiled=True)  17 us
    all_to_all x1, blocking collectives, shards(): packed = lax.all_to_all(packed, ROW, 0, 0, tiled=True)  16.5 us
    ppermute x1, starting transfers between devices, shards(): kv_far = lax.ppermute(kv, 'zh', swap)  11.6 us
    all_to_all x1, waiting for transfers between devices, shards(): parts = lax.all_to_all(parts, 'span', 0, 0, tiled=True)  7.03 us
    ppermute x1, waiting for transfers between devices, shards(): far = lax.ppermute(near, 'zh', swap)  6.82 us
    all_gather x1, blocking collectives, shards(): both = lax.all_gather(both, 'core', axis=0, tiled=True)  6.67 us
    all_gather x1, blocking collectives, shards(): near = lax.all_gather(kv, 'core', axis=0, tiled=True)  4.84 us
  transfers between devices with their start and end apart: 5, of which 2 were waited for; matrix products, arithmetic and copies ran while one was open for 0% of the time, Pallas kernels for 4%

profile of v10, /device:TPU:1, one launch (start us, length us, event | category | flops | bytes accessed | tf_op | source)
XLA Modules:
  0.0 117.3 jit_solution(3042460941819454584)
XLA Ops:
  0.0 0.0 copy-start.2
  0.0 0.8 copy-done.2
  0.8 0.0 copy-start.3
  0.8 0.8 copy-done.3
  1.7 0.0 copy-start.4
  1.7 0.8 copy-done.4
  2.5 16.5 %all_to_all.25.packed_ref = bf16[8,3,40,128]{3,2,1,0:T(8,128)(2,1)S(1)} all-to-all(bf16[8,3,40,128]{3,2,1,0:T(8,128)(2,1)S(1)} %pack.1), channel_id=1, replica_groups=mesh['span'=4,'zh'=2,'y2'=2,'y1'=2,'y0'=2,'core'=2,'head'=4] {'y2','y1',..., dimensions={0} | all-to-all | bytes 491520 | tf_op jit(solution)/shard_map/exchange_heads/all_to_all | solution.py:186
  19.0 11.6 %collective-permute-start = (bf16[2,320,128]{2,1,0:T(8,128)(2,1)S(1)}, bf16[2,320,128]{2,1,0:T(8,128)(2,1)S(1)}, u32[]{:S(2)}, u32[]{:S(2)}) collective-permute-start(bf16[2,320,128]{2,1,0:T(8,128)(2,1)S(1)} %bitcast.12), channel_id=1, source_target_pairs={{0,64},{64,0},{1,65},{65,1},{2,66},{66,2},{3,67},{67,3},{4,68},{68... | collective-permute-start | bytes 491528 | tf_op jit(solution)/shard_map/gather_kv/ppermute | solution.py:189
  30.6 0.8 repeat_q.1
  31.4 4.0 %all-to-all-start.1 = ((bf16[4,320,128]{2,1,0:T(8,128)(2,1)}), bf16[4,320,128]{2,1,0:T(8,128)(2,1)S(1)}, u32[]{:S(2)}, u32[]{:S(2)}) async-start(bf16[4,320,128]{2,1,0:T(8,128)(2,1)} %bitcast.4), calls=%async_computation.1 | async-start | bytes 655360 | tf_op jit(solution)/shard_map/gather_q/all_to_all | solution.py:193
  35.4 0.0 copy-start
  35.4 4.8 %all_gather.9.near_ref = bf16[4,320,128]{2,1,0:T(8,128)(2,1)S(1)} all-gather(bf16[2,320,128]{2,1,0:T(8,128)(2,1)S(1)} %bitcast.13), channel_id=1, replica_groups=mesh['span'=4,'zh'=2,'y2'=2,'y1'=2,'y0'=2,'core'=2,'head'=4] {'core'}, dimensions={0}, use_global_device_ids=true | all-gather | bytes 491520 | tf_op jit(solution)/shard_map/gather_kv/all_gather | solution.py:195
  40.3 0.0 copy-done
  40.3 0.0 copy-start.6
  40.3 0.0 copy-start.7
  40.3 2.3 %collective-permute-start.1 = (bf16[192,768]{1,0:T(8,128)(2,1)S(1)}, bf16[192,768]{1,0:T(8,128)(2,1)S(1)}, u32[]{:S(2)}, u32[]{:S(2)}) collective-permute-start(bf16[192,768]{1,0:T(8,128)(2,1)S(1)} %bitcast.14), channel_id=1, source_target_pairs={{0,8},{8,0},{1,9},{9,1},{2,10},{10,2},{3,11},{11,3},{4,12},{12,4},... | collective-permute-start | bytes 884744 | tf_op jit(solution)/shard_map/fetch_weight/ppermute | solution.py:199
  42.6 0.0 collective-permute-done
  42.6 2.3 %all_gather.10.far_ref = bf16[4,320,128]{2,1,0:T(8,128)(2,1)S(1)} all-gather(bf16[2,320,128]{2,1,0:T(8,128)(2,1)S(1)} %collective-permute-done), channel_id=1, replica_groups=mesh['span'=4,'zh'=2,'y2'=2,'y1'=2,'y0'=2,'core'=2,'head'=4] {'core'}, dimensions={0}, use_global_device_ids=true | all-gather | bytes 491520 | tf_op jit(solution)/shard_map/gather_kv/all_gather | solution.py:196
  44.9 0.0 all-to-all-done.1.q_ref
  44.9 0.0 copy-done.6
  44.9 0.0 copy-done.7
  44.9 4.1 %attend.1 = bf16[4,368,128]{2,1,0:T(8,128)(2,1)} custom-call(s32[4]{0:T(128)S(1)} %copy-done.6, s32[4]{0:T(128)S(1)} %copy-done.7, bf16[4,320,128]{2,1,0:T(8,128)(2,1)S(1)} %all-to-all-done.1.q_ref, bf16[4,320,128]{2,1,0:T(8,128)(2,1)S(1)} %all_gather.9.near_ref, bf16[4,320,128]{2,1,0:T(8,128)(2,1)S(1)} %all_gather.10.far_ref), custom_call_target="tpu_custom_call" | custom-call | tf_op jit(solution)/shard_map/attend/pallas_call | solution.py:200
  49.0 4.5 %all-to-all-start.2 = ((bf16[4,368,128]{2,1,0:T(8,128)(2,1)}), bf16[4,368,128]{2,1,0:T(8,128)(2,1)S(1)}, u32[]{:S(2)}, u32[]{:S(2)}) async-start(bf16[4,368,128]{2,1,0:T(8,128)(2,1)} %attend.1), calls=%async_computation.2 | async-start | bytes 753664 | tf_op jit(solution)/shard_map/return_parts/all_to_all | solution.py:204
  53.5 0.0 collective-permute-done.1.far_ref
  53.5 7.0 %all-to-all-done.2.parts_ref = bf16[4,368,128]{2,1,0:T(8,128)(2,1)S(1)} async-done(((bf16[4,368,128]{2,1,0:T(8,128)(2,1)}), bf16[4,368,128]{2,1,0:T(8,128)(2,1)S(1)}, u32[]{:S(2)}, u32[]{:S(2)}) %all-to-all-start.2) | async-done | bytes 376864 | tf_op jit(solution)/shard_map/return_parts/all_to_all | solution.py:204
  60.5 0.9 combine.1.near_ref
  61.5 3.0 %collective-permute-start.2 = (bf16[2,160,128]{2,1,0:T(8,128)(2,1)S(1)}, bf16[2,160,128]{2,1,0:T(8,128)(2,1)S(1)}, u32[]{:S(2)}, u32[]{:S(2)}) collective-permute-start(bf16[2,160,128]{2,1,0:T(8,128)(2,1)S(1)} %combine.1.near_ref), channel_id=1, source_target_pairs={{0,64},{64,0},{1,65},{65,1},{2,66},{66,2},{3,67},{67,3},{4,68},{68... | collective-permute-start | bytes 245768 | tf_op jit(solution)/shard_map/gather_attended/ppermute | solution.py:208
  64.5 6.8 %collective-permute-done.2.far_ref = bf16[2,160,128]{2,1,0:T(8,128)(2,1)S(1)} collective-permute-done((bf16[2,160,128]{2,1,0:T(8,128)(2,1)S(1)}, bf16[2,160,128]{2,1,0:T(8,128)(2,1)S(1)}, u32[]{:S(2)}, u32[]{:S(2)}) %collective-permute-start.2) | collective-permute-done | bytes 81952 | tf_op jit(solution)/shard_map/gather_attended/ppermute | solution.py:208
  71.3 0.1 spread.1
  71.4 19.1 %all_to_all.26 = bf16[8,2,160,128]{3,2,1,0:T(8,128)(2,1)S(1)} all-to-all(bf16[8,2,160,128]{3,2,1,0:T(8,128)(2,1)S(1)} %spread.1), channel_id=1, replica_groups=mesh['span'=4,'zh'=2,'y2'=2,'y1'=2,'y0'=2,'core'=2,'head'=4] {'y2','y1',..., dimensions={0} | all-to-all | bytes 1310720 | tf_op jit(solution)/shard_map/gather_attended/all_to_all | solution.py:210
  90.6 6.7 %all_gather.11.rows_ref = bf16[12,2,160,128]{3,2,1,0:T(8,128)(2,1)S(1)} all-gather(bf16[6,2,160,128]{3,2,1,0:T(8,128)(2,1)S(1)} %slice.4), channel_id=1, replica_groups=mesh['span'=4,'zh'=2,'y2'=2,'y1'=2,'y0'=2,'core'=2,'head'=4] {'core'}, dimensions={0}, use_global_device_ids=true | all-gather | bytes 1474560 | tf_op jit(solution)/shard_map/gather_attended/all_gather | solution.py:211
  97.2 1.0 project.1
  98.2 0.0 copy-start.1
  98.2 0.0 copy-start.5
  98.2 17.0 %all_to_all.27.pieces_ref = bf16[8,240,128]{2,1,0:T(8,128)(2,1)S(1)} all-to-all(bf16[8,240,128]{2,1,0:T(8,128)(2,1)S(1)} %project.1), channel_id=1, replica_groups=mesh['span'=4,'zh'=2,'y2'=2,'y1'=2,'y0'=2,'core'=2,'head'=4] {'head','y0'}, dimensions={0} | all-to-all | bytes 983040 | tf_op jit(solution)/shard_map/sum_heads/all_to_all | solution.py:217
  115.2 0.0 copy-start.8
  115.2 0.0 copy-done.1
  115.2 0.0 copy-done.5
  115.2 0.6 copy-done.8
  115.9 1.4 %finish.1 = bf16[192,320]{1,0:T(8,128)(2,1)} custom-call(s32[4]{0:T(128)S(1)} %copy-done.8, bf16[8,240,128]{2,1,0:T(8,128)(2,1)S(1)} %all_to_all.27.pieces_ref, f32[4,192]{1,0:T(4,128)S(1)} %copy-done.5, bf16[192,320]{1,0:T(8,128)(2,1)S(1)} %bitcast.16), custom_call_target="tpu_custom_call" | custom-call | tf_op jit(solution)/shard_map/finish/pallas_call | solution.py:218
  (3 shorter events, 0.1 us)
Async XLA Ops:
  0.0 0.8 copy-start.2
  0.8 0.8 copy-start.3
  1.7 0.8 copy-start.4
  19.0 23.6 %collective-permute-start = (bf16[2,320,128]{2,1,0:T(8,128)(2,1)S(1)}, bf16[2,320,128]{2,1,0:T(8,128)(2,1)S(1)}, u32[]{:S(2)}, u32[]{:S(2)}) collective-permute-start(bf16[2,320,128]{2,1,0:T(8,128)(2,1)S(1)} %bitcast.12), channel_id=1, source_target_pairs={{0,64},{64,0},{1,65},{65,1},{2,66},{66,2},{3,67},{67,3},{4,68},{68... | collective-permute-start | bytes 491528 | tf_op jit(solution)/shard_map/gather_kv/ppermute | solution.py:189
  31.4 13.5 %all-to-all-start.1 = ((bf16[4,320,128]{2,1,0:T(8,128)(2,1)}), bf16[4,320,128]{2,1,0:T(8,128)(2,1)S(1)}, u32[]{:S(2)}, u32[]{:S(2)}) async-start(bf16[4,320,128]{2,1,0:T(8,128)(2,1)} %bitcast.4), calls=%async_computation.1 | async-start | bytes 655360 | tf_op jit(solution)/shard_map/gather_q/all_to_all | solution.py:193
  35.4 4.8 %copy-start = (bf16[768,192]{0,1:T(8,128)(2,1)S(1)}, bf16[768,192]{0,1:T(8,128)(2,1)}, u32[]{:S(2)}) copy-start(bf16[768,192]{0,1:T(8,128)(2,1)} %param.16) | copy-start | bytes 884740
  40.3 4.7 %copy-start.6 = (s32[4]{0:T(128)S(1)}, s32[4]{0:T(128)}, u32[]{:S(2)}) copy-start(s32[4]{0:T(128)} %order_ref.1) | copy-start | bytes 52
  40.3 4.7 %copy-start.7 = (s32[4]{0:T(128)S(1)}, s32[4]{0:T(128)}, u32[]{:S(2)}) copy-start(s32[4]{0:T(128)} %valid_ref.1) | copy-start | bytes 52
  40.3 13.2 %collective-permute-start.1 = (bf16[192,768]{1,0:T(8,128)(2,1)S(1)}, bf16[192,768]{1,0:T(8,128)(2,1)S(1)}, u32[]{:S(2)}, u32[]{:S(2)}) collective-permute-start(bf16[192,768]{1,0:T(8,128)(2,1)S(1)} %bitcast.14), channel_id=1, source_target_pairs={{0,8},{8,0},{1,9},{9,1},{2,10},{10,2},{3,11},{11,3},{4,12},{12,4},... | collective-permute-start | bytes 884744 | tf_op jit(solution)/shard_map/fetch_weight/ppermute | solution.py:199
  49.0 11.6 %all-to-all-start.2 = ((bf16[4,368,128]{2,1,0:T(8,128)(2,1)}), bf16[4,368,128]{2,1,0:T(8,128)(2,1)S(1)}, u32[]{:S(2)}, u32[]{:S(2)}) async-start(bf16[4,368,128]{2,1,0:T(8,128)(2,1)} %attend.1), calls=%async_computation.2 | async-start | bytes 753664 | tf_op jit(solution)/shard_map/return_parts/all_to_all | solution.py:204
  61.5 9.8 %collective-permute-start.2 = (bf16[2,160,128]{2,1,0:T(8,128)(2,1)S(1)}, bf16[2,160,128]{2,1,0:T(8,128)(2,1)S(1)}, u32[]{:S(2)}, u32[]{:S(2)}) collective-permute-start(bf16[2,160,128]{2,1,0:T(8,128)(2,1)S(1)} %combine.1.near_ref), channel_id=1, source_target_pairs={{0,64},{64,0},{1,65},{65,1},{2,66},{66,2},{3,67},{67,3},{4,68},{68... | collective-permute-start | bytes 245768 | tf_op jit(solution)/shard_map/gather_attended/ppermute | solution.py:208
  98.2 17.0 %copy-start.1 = (bf16[1,320,192]{1,2,0:T(8,128)(2,1)S(1)}, bf16[1,320,192]{1,2,0:T(8,128)(2,1)}, u32[]{:S(2)}) copy-start(bf16[1,320,192]{1,2,0:T(8,128)(2,1)} %param.17) | copy-start | bytes 368644
  98.2 17.0 %copy-start.5 = (f32[4,192]{1,0:T(4,128)S(1)}, f32[4,192]{1,0:T(4,128)}, u32[]{:S(2)}) copy-start(f32[4,192]{1,0:T(4,128)} %gate_ref.1) | copy-start | bytes 9220
  115.2 0.7 copy-start.8

commit v11 on v8

--- a/solution.py
+++ b/solution.py
@@ -16,14 +16,20 @@
 FRAMES = 8
 
 
-def pack_kernel(q_ref, k_ref, v_ref, out_ref):
+def pack_kernel(q_ref, k_ref, v_ref, out_ref, sems):
     heads = q_ref.shape[1] // HD
-    for h in range(out_ref.shape[0]):
+    copies = []
+    for h in range(heads):
         for i, ref in enumerate((q_ref, k_ref, v_ref)):
-            if h < heads:
-                out_ref[h, i] = ref[:, h * HD : (h + 1) * HD]
-            else:
-                out_ref[h, i] = jnp.zeros(out_ref.shape[2:], out_ref.dtype)
+            copies.append(
+                pltpu.make_async_copy(ref.at[:, h * HD : (h + 1) * HD], out_ref.at[h, i], sems.at[3 * h + i])
+            )
+    for copy in copies:
+        copy.start()
+    for h in range(heads, out_ref.shape[0]):
+        out_ref[h] = jnp.zeros(out_ref.shape[1:], out_ref.dtype)
+    for copy in copies:
+        copy.wait()
 
 
 def unpack_kernel(packed_ref, queries_ref, kv_ref):
@@ -86,7 +92,8 @@
         out_ref[y, 1] = far_ref[y % 2]
 
 
-def project_kernel(rows_ref, near_ref, far_ref, out_ref):
+def project_kernel(steps_ref, gates_ref, rows_ref, near_ref, far_ref, out_ref, gate_ref):
+    gate_ref[...] = gates_ref[pl.ds(steps_ref[lax.axis_index("span")], 1), :]
     zh = lax.axis_index("zh")
     y0 = lax.axis_index("y0")
     heads = near_ref.shape[1] // HD
@@ -110,9 +117,8 @@
                 out_ref[slot, rows:, :] = tail.astype(jnp.bfloat16)
 
 
-def finish_kernel(steps_ref, pieces_ref, gate_ref, residual_ref, out_ref):
-    step = steps_ref[lax.axis_index("span")]
-    gate = gate_ref[pl.ds(step, 1), :]
+def finish_kernel(pieces_ref, gate_ref, residual_ref, out_ref):
+    gate = gate_ref[...]
     rows = residual_ref.shape[1] // 2
     half = rows // 2
     sums = []
@@ -153,7 +159,15 @@
             name=name,
         )
 
-    packed = call(pack_kernel, [(ny, 3, tokens, HD)], [vmem] * 3, "pack")(q[0], k[0], v[0])
+    packed = pl.pallas_call(
+        pack_kernel,
+        out_shape=jax.ShapeDtypeStruct((ny, 3, tokens, HD), bf16),
+        in_specs=[pl.BlockSpec(memory_space=pltpu.HBM)] * 3,
+        out_specs=vmem,
+        scratch_shapes=[pltpu.SemaphoreType.DMA((3 * width // HD,))],
+        compiler_params=pltpu.CompilerParams(vmem_limit_bytes=60 * 1024 * 1024),
+        name="pack",
+    )(q[0], k[0], v[0])
     with jax.named_scope("exchange_heads"):
         packed = lax.all_to_all(packed, ROW, 0, 0, tiled=True)
     queries, kv = call(unpack_kernel, [(nx, ny, tokens, HD), (2, ny, tokens, HD)], [vmem], "unpack")(packed)
@@ -180,19 +194,27 @@
         both = lax.all_to_all(both, ROW, 0, 0, tiled=True)[: width // HD]
         both = lax.all_gather(both, "core", axis=0, tiled=True)
     cols = weight.shape[0]
-    pieces = call(project_kernel, [(8, 4 * tokens * cols // HD, HD)], [vmem] * 3, "project")(
-        both, weight, weight_far
-    )
+    pieces, gate = pl.pallas_call(
+        project_kernel,
+        out_shape=(
+            jax.ShapeDtypeStruct((8, 4 * tokens * cols // HD, HD), bf16),
+            jax.ShapeDtypeStruct((1, cols), jnp.float32),
+        ),
+        in_specs=[smem] + [vmem] * 4,
+        out_specs=(vmem, vmem),
+        compiler_params=params,
+        name="project",
+    )(noise_steps, gate_table, both, weight, weight_far)
     with jax.named_scope("sum_heads"):
         pieces = lax.all_to_all(pieces, ("head", "y0"), 0, 0, tiled=True)
     mixed = pl.pallas_call(
         finish_kernel,
         out_shape=jax.ShapeDtypeStruct(residual.shape[:0:-1], bf16),
-        in_specs=[smem, vmem, vmem, vmem],
+        in_specs=[vmem, vmem, vmem],
         out_specs=vmem,
         compiler_params=params,
         name="finish",
-    )(noise_steps, pieces, gate_table, residual[0].T)
+    )(pieces, gate, residual[0].T)
     return mixed.T[None]
 
 

time: 117 us -> 116 us (level)
  local copies, waits for them, and re-layouts: 3.19 us -> 0.06 us
  Pallas kernels: 7.98 us -> 9.75 us
    unnamed x18 -> x12, local copies, waits for them, and re-layouts: 3.16 us -> 0.03 us
    pallas_call x2, Pallas kernels: 0.99 us -> 3.25 us  [the longest x1 1.72 us: shards(): pl.pallas_call(pack_kernel, out_shape=jax.ShapeDtypeStruct((ny, 3, tokens...]
where the time goes in v11:
time: 116 us; the launch traced here: 115 us
  blocking collectives  66.1 us (57%)
  starting transfers between devices  30.4 us (26%)
  Pallas kernels  9.75 us (8%)
  waiting for transfers between devices  8.23 us (7%)
    all_to_all x1, blocking collectives, shards(): both = lax.all_to_all(both, ROW, 0, 0, tiled=True)[:width // HD]  18.7 us
    all_to_all x1, blocking collectives, shards(): packed = lax.all_to_all(packed, ROW, 0, 0, tiled=True)  16.9 us
    all_to_all x1, blocking collectives, shards(): pieces = lax.all_to_all(pieces, ('head', 'y0'), 0, 0, tiled=True)  16.5 us
    ppermute x1, starting transfers between devices, shards(): kv_far = lax.ppermute(kv, 'zh', swap)  11.4 us
    ppermute x1, starting transfers between devices, shards(): far = lax.ppermute(near, 'zh', swap)  8.17 us
    all_gather x1, blocking collectives, shards(): both = lax.all_gather(both, 'core', axis=0, tiled=True)  7.04 us
    ppermute x1, waiting for transfers between devices, shards(): weight_far = lax.ppermute(weight, 'y0', swap)  6.02 us
    all_gather x1, blocking collectives, shards(): near = lax.all_gather(kv, 'core', axis=0, tiled=True)  4.7 us
  transfers between devices with their start and end apart: 5, of which 3 were waited for; matrix products, arithmetic and copies ran while one was open for 0% of the time, Pallas kernels for 0%

profile of v11, /device:TPU:1, one launch (start us, length us, event | category | flops | bytes accessed | tf_op | source)
XLA Modules:
  0.0 114.6 jit_solution(7870536276175166998)
XLA Ops:
  0.0 1.7 %pack.1 = bf16[8,3,40,128]{3,2,1,0:T(8,128)(2,1)} custom-call(bf16[40,768]{1,0:T(8,128)(2,1)} %bitcast.17, bf16[40,768]{1,0:T(8,128)(2,1)} %bitcast.18, bf16[40,768]{1,0:T(8,128)(2,1)} %bitcast.19), custom_call_target="tpu_custom_call" | custom-call | tf_op jit(solution)/shard_map/pack/pallas_call | solution.py:162
  1.7 16.9 %all_to_all.25.packed_ref = bf16[8,3,40,128]{3,2,1,0:T(8,128)(2,1)S(1)} all-to-all(bf16[8,3,40,128]{3,2,1,0:T(8,128)(2,1)} %pack.1), channel_id=1, replica_groups=mesh['span'=4,'zh'=2,'y2'=2,'y1'=2,'y0'=2,'core'=2,'head'=4] {'y2','y1',..., dimensions={0} | all-to-all | bytes 491520 | tf_op jit(solution)/shard_map/exchange_heads/all_to_all | solution.py:172
  18.6 0.8 unpack.1
  19.4 11.4 %collective-permute-start = (bf16[2,320,128]{2,1,0:T(8,128)(2,1)S(1)}, bf16[2,320,128]{2,1,0:T(8,128)(2,1)S(1)}, u32[]{:S(2)}, u32[]{:S(2)}) collective-permute-start(bf16[2,320,128]{2,1,0:T(8,128)(2,1)S(1)} %bitcast.14), channel_id=1, source_target_pairs={{0,64},{64,0},{1,65},{65,1},{2,66},{66,2},{3,67},{67,3},{4,68},{68... | collective-permute-start | bytes 491528 | tf_op jit(solution)/shard_map/gather_kv/ppermute | solution.py:178
  30.8 4.0 %all-to-all-start.1 = ((bf16[4,320,128]{2,1,0:T(8,128)(2,1)}), bf16[4,320,128]{2,1,0:T(8,128)(2,1)S(1)}, u32[]{:S(2)}, u32[]{:S(2)}) async-start(bf16[4,320,128]{2,1,0:T(8,128)(2,1)} %bitcast.3), calls=%async_computation.1 | async-start | bytes 655360 | tf_op jit(solution)/shard_map/gather_q/all_to_all | solution.py:175
  34.8 4.7 %all_gather.9.near_ref = bf16[4,320,128]{2,1,0:T(8,128)(2,1)S(1)} all-gather(bf16[2,320,128]{2,1,0:T(8,128)(2,1)S(1)} %bitcast.15), channel_id=1, replica_groups=mesh['span'=4,'zh'=2,'y2'=2,'y1'=2,'y0'=2,'core'=2,'head'=4] {'core'}, dimensions={0}, use_global_device_ids=true | all-gather | bytes 491520 | tf_op jit(solution)/shard_map/gather_kv/all_gather | solution.py:179
  39.5 0.0 copy-start.3
  39.5 0.0 copy-start.4
  39.5 0.0 collective-permute-done
  39.5 2.2 %all_gather.10.far_ref = bf16[4,320,128]{2,1,0:T(8,128)(2,1)S(1)} all-gather(bf16[2,320,128]{2,1,0:T(8,128)(2,1)S(1)} %collective-permute-done), channel_id=1, replica_groups=mesh['span'=4,'zh'=2,'y2'=2,'y1'=2,'y0'=2,'core'=2,'head'=4] {'core'}, dimensions={0}, use_global_device_ids=true | all-gather | bytes 491520 | tf_op jit(solution)/shard_map/gather_kv/all_gather | solution.py:180
  41.7 0.0 all-to-all-done.1.q_ref
  41.7 0.0 copy-done.3
  41.7 0.0 copy-done.4
  41.7 4.2 %attend.1 = bf16[4,320,256]{2,1,0:T(8,128)(2,1)} custom-call(s32[4]{0:T(128)S(1)} %copy-done.3, s32[4]{0:T(128)S(1)} %copy-done.4, bf16[4,320,128]{2,1,0:T(8,128)(2,1)S(1)} %all-to-all-done.1.q_ref, bf16[4,320,128]{2,1,0:T(8,128)(2,1)S(1)} %all_gather.9.near_ref, bf16[4,320,128]{2,1,0:T(8,128)(2,1)S(1)} %all_gather.10.far_ref), custom_call_target="tpu_custom_call" | custom-call | tf_op jit(solution)/shard_map/attend/pallas_call | solution.py:184
  45.9 0.0 copy-start
  45.9 4.6 %all-to-all-start.2 = ((bf16[4,320,256]{2,1,0:T(8,128)(2,1)}), bf16[4,320,256]{2,1,0:T(8,128)(2,1)S(1)}, u32[]{:S(2)}, u32[]{:S(2)}) async-start(bf16[4,320,256]{2,1,0:T(8,128)(2,1)} %attend.1), calls=%async_computation.2 | async-start | bytes 1310720 | tf_op jit(solution)/shard_map/return_parts/all_to_all | solution.py:188
  50.6 0.0 copy-done
  50.6 2.2 %collective-permute-start.1 = (bf16[192,768]{1,0:T(8,128)(2,1)S(1)}, bf16[192,768]{1,0:T(8,128)(2,1)S(1)}, u32[]{:S(2)}, u32[]{:S(2)}) collective-permute-start(bf16[192,768]{1,0:T(8,128)(2,1)S(1)} %bitcast.12), channel_id=1, source_target_pairs={{0,8},{8,0},{1,9},{9,1},{2,10},{10,2},{3,11},{11,3},{4,12},{12,4},... | collective-permute-start | bytes 884744 | tf_op jit(solution)/shard_map/fetch_weight/ppermute | solution.py:183
  52.8 6.0 %collective-permute-done.1.far_ref = bf16[192,768]{1,0:T(8,128)(2,1)S(1)} collective-permute-done((bf16[192,768]{1,0:T(8,128)(2,1)S(1)}, bf16[192,768]{1,0:T(8,128)(2,1)S(1)}, u32[]{:S(2)}, u32[]{:S(2)}) %collective-permute-start.1) | collective-permute-done | bytes 294944 | tf_op jit(solution)/shard_map/fetch_weight/ppermute | solution.py:183
  58.8 0.3 all-to-all-done.2.parts_ref
  59.1 0.6 combine.1.near_ref
  59.6 8.2 %collective-permute-start.2 = (bf16[2,160,128]{2,1,0:T(8,128)(2,1)S(1)}, bf16[2,160,128]{2,1,0:T(8,128)(2,1)S(1)}, u32[]{:S(2)}, u32[]{:S(2)}) collective-permute-start(bf16[2,160,128]{2,1,0:T(8,128)(2,1)S(1)} %combine.1.near_ref), channel_id=1, source_target_pairs={{0,64},{64,0},{1,65},{65,1},{2,66},{66,2},{3,67},{67,3},{4,68},{68... | collective-permute-start | bytes 245768 | tf_op jit(solution)/shard_map/gather_attended/ppermute | solution.py:192
  67.8 1.9 %collective-permute-done.2.far_ref = bf16[2,160,128]{2,1,0:T(8,128)(2,1)S(1)} collective-permute-done((bf16[2,160,128]{2,1,0:T(8,128)(2,1)S(1)}, bf16[2,160,128]{2,1,0:T(8,128)(2,1)S(1)}, u32[]{:S(2)}, u32[]{:S(2)}) %collective-permute-start.2) | collective-permute-done | bytes 81952 | tf_op jit(solution)/shard_map/gather_attended/ppermute | solution.py:192
  69.7 0.1 spread.1
  69.8 18.7 %all_to_all.26 = bf16[8,2,160,128]{3,2,1,0:T(8,128)(2,1)S(1)} all-to-all(bf16[8,2,160,128]{3,2,1,0:T(8,128)(2,1)S(1)} %spread.1), channel_id=1, replica_groups=mesh['span'=4,'zh'=2,'y2'=2,'y1'=2,'y0'=2,'core'=2,'head'=4] {'y2','y1',..., dimensions={0} | all-to-all | bytes 1310720 | tf_op jit(solution)/shard_map/gather_attended/all_to_all | solution.py:194
  88.6 0.0 copy-start.2
  88.6 0.0 copy-start.5
  88.6 7.0 %all_gather.11.rows_ref = bf16[12,2,160,128]{3,2,1,0:T(8,128)(2,1)S(1)} all-gather(bf16[6,2,160,128]{3,2,1,0:T(8,128)(2,1)S(1)} %slice.4), channel_id=1, replica_groups=mesh['span'=4,'zh'=2,'y2'=2,'y1'=2,'y0'=2,'core'=2,'head'=4] {'core'}, dimensions={0}, use_global_device_ids=true | all-gather | bytes 1474560 | tf_op jit(solution)/shard_map/gather_attended/all_gather | solution.py:195
  95.7 0.0 copy-done.2
  95.7 0.0 copy-done.5
  95.7 1.5 %project.1 = (bf16[8,240,128]{2,1,0:T(8,128)(2,1)S(1)}, f32[1,192]{1,0:T(1,128)S(1)}) custom-call(s32[4]{0:T(128)S(1)} %copy-done.5, f32[4,192]{1,0:T(4,128)S(1)} %copy-done.2, bf16[12,2,160,128]{3,2,1,0:T(8,128)(2,1)S(1)} %all_gather.11.rows_ref, bf16[192,768]{1,0:T(8,128)(2,1)S(1)} %bitcast.13, bf16[192,768]{1,0:T(8,128)(2,1)S(1)} %collective-permute-done.1.far_ref), custom_call_target="tpu_custom_call" | custom-call | tf_op jit(solution)/shard_map/project/pallas_call | solution.py:197
  97.2 0.0 copy-start.1
  97.2 16.5 %all_to_all.27.pieces_ref = bf16[8,240,128]{2,1,0:T(8,128)(2,1)S(1)} all-to-all(bf16[8,240,128]{2,1,0:T(8,128)(2,1)S(1)} %get-tuple-element.19), channel_id=1, replica_groups=mesh['span'=4,'zh'=2,'y2'=2,'y1'=2,'y0'=2,'core'=2,'head'=4] {'head','y0'}, dimensions={0} | all-to-all | bytes 983040 | tf_op jit(solution)/shard_map/sum_heads/all_to_all | solution.py:209
  113.8 0.0 copy-done.1
  113.8 0.9 finish.1
  (1 shorter events, 0.0 us)
Async XLA Ops:
  19.4 20.2 %collective-permute-start = (bf16[2,320,128]{2,1,0:T(8,128)(2,1)S(1)}, bf16[2,320,128]{2,1,0:T(8,128)(2,1)S(1)}, u32[]{:S(2)}, u32[]{:S(2)}) collective-permute-start(bf16[2,320,128]{2,1,0:T(8,128)(2,1)S(1)} %bitcast.14), channel_id=1, source_target_pairs={{0,64},{64,0},{1,65},{65,1},{2,66},{66,2},{3,67},{67,3},{4,68},{68... | collective-permute-start | bytes 491528 | tf_op jit(solution)/shard_map/gather_kv/ppermute | solution.py:178
  30.8 10.9 %all-to-all-start.1 = ((bf16[4,320,128]{2,1,0:T(8,128)(2,1)}), bf16[4,320,128]{2,1,0:T(8,128)(2,1)S(1)}, u32[]{:S(2)}, u32[]{:S(2)}) async-start(bf16[4,320,128]{2,1,0:T(8,128)(2,1)} %bitcast.3), calls=%async_computation.1 | async-start | bytes 655360 | tf_op jit(solution)/shard_map/gather_q/all_to_all | solution.py:175
  39.5 2.2 %copy-start.3 = (s32[4]{0:T(128)S(1)}, s32[4]{0:T(128)}, u32[]{:S(2)}) copy-start(s32[4]{0:T(128)} %order_ref.1) | copy-start | bytes 52
  39.5 2.2 %copy-start.4 = (s32[4]{0:T(128)S(1)}, s32[4]{0:T(128)}, u32[]{:S(2)}) copy-start(s32[4]{0:T(128)} %valid_ref.1) | copy-start | bytes 52
  45.9 4.7 %copy-start = (bf16[768,192]{0,1:T(8,128)(2,1)S(1)}, bf16[768,192]{0,1:T(8,128)(2,1)}, u32[]{:S(2)}) copy-start(bf16[768,192]{0,1:T(8,128)(2,1)} %param.16) | copy-start | bytes 884740
  45.9 13.1 %all-to-all-start.2 = ((bf16[4,320,256]{2,1,0:T(8,128)(2,1)}), bf16[4,320,256]{2,1,0:T(8,128)(2,1)S(1)}, u32[]{:S(2)}, u32[]{:S(2)}) async-start(bf16[4,320,256]{2,1,0:T(8,128)(2,1)} %attend.1), calls=%async_computation.2 | async-start | bytes 1310720 | tf_op jit(solution)/shard_map/return_parts/all_to_all | solution.py:188
  50.6 8.2 %collective-permute-start.1 = (bf16[192,768]{1,0:T(8,128)(2,1)S(1)}, bf16[192,768]{1,0:T(8,128)(2,1)S(1)}, u32[]{:S(2)}, u32[]{:S(2)}) collective-permute-start(bf16[192,768]{1,0:T(8,128)(2,1)S(1)} %bitcast.12), channel_id=1, source_target_pairs={{0,8},{8,0},{1,9},{9,1},{2,10},{10,2},{3,11},{11,3},{4,12},{12,4},... | collective-permute-start | bytes 884744 | tf_op jit(solution)/shard_map/fetch_weight/ppermute | solution.py:183
  59.6 10.1 %collective-permute-start.2 = (bf16[2,160,128]{2,1,0:T(8,128)(2,1)S(1)}, bf16[2,160,128]{2,1,0:T(8,128)(2,1)S(1)}, u32[]{:S(2)}, u32[]{:S(2)}) collective-permute-start(bf16[2,160,128]{2,1,0:T(8,128)(2,1)S(1)} %combine.1.near_ref), channel_id=1, source_target_pairs={{0,64},{64,0},{1,65},{65,1},{2,66},{66,2},{3,67},{67,3},{4,68},{68... | collective-permute-start | bytes 245768 | tf_op jit(solution)/shard_map/gather_attended/ppermute | solution.py:192
  88.6 7.1 %copy-start.2 = (f32[4,192]{1,0:T(4,128)S(1)}, f32[4,192]{1,0:T(4,128)}, u32[]{:S(2)}) copy-start(f32[4,192]{1,0:T(4,128)} %gates_ref.1) | copy-start | bytes 9220
  88.6 7.1 %copy-start.5 = (s32[4]{0:T(128)S(1)}, s32[4]{0:T(128)}, u32[]{:S(2)}) copy-start(s32[4]{0:T(128)} %steps_ref.1) | copy-start | bytes 52
  97.2 16.5 %copy-start.1 = (bf16[1,320,192]{1,2,0:T(8,128)(2,1)S(1)}, bf16[1,320,192]{1,2,0:T(8,128)(2,1)}, u32[]{:S(2)}) copy-start(bf16[1,320,192]{1,2,0:T(8,128)(2,1)} %param.17) | copy-start | bytes 368644

commit v12 on v10

--- a/solution.py
+++ b/solution.py
@@ -18,14 +18,20 @@
 FRAMES = 8
 
 
-def pack_kernel(q_ref, k_ref, v_ref, out_ref):
+def pack_kernel(q_ref, k_ref, v_ref, out_ref, sems):
     heads = q_ref.shape[1] // HD
-    for h in range(out_ref.shape[0]):
+    copies = []
+    for h in range(heads):
         for i, ref in enumerate((q_ref, k_ref, v_ref)):
-            if h < heads:
-                out_ref[h, i] = ref[:, h * HD : (h + 1) * HD]
-            else:
-                out_ref[h, i] = jnp.zeros(out_ref.shape[2:], out_ref.dtype)
+            copies.append(
+                pltpu.make_async_copy(ref.at[:, h * HD : (h + 1) * HD], out_ref.at[h, i], sems.at[3 * h + i])
+            )
+    for copy in copies:
+        copy.start()
+    for h in range(heads, out_ref.shape[0]):
+        out_ref[h] = jnp.zeros(out_ref.shape[1:], out_ref.dtype)
+    for copy in copies:
+        copy.wait()
 
 
 def keep_kv_kernel(packed_ref, kv_ref):
@@ -114,7 +120,8 @@
         out_ref[y, 1] = far_ref[y % 2]
 
 
-def project_kernel(rows_ref, near_ref, far_ref, out_ref):
+def project_kernel(steps_ref, gates_ref, rows_ref, near_ref, far_ref, out_ref, gate_ref):
+    gate_ref[...] = gates_ref[pl.ds(steps_ref[lax.axis_index("span")], 1), :]
     zh = lax.axis_index("zh")
     y0 = lax.axis_index("y0")
     heads = near_ref.shape[1] // HD
@@ -138,9 +145,8 @@
                 out_ref[slot, rows:, :] = tail.astype(jnp.bfloat16)
 
 
-def finish_kernel(steps_ref, pieces_ref, gate_ref, residual_ref, out_ref):
-    step = steps_ref[lax.axis_index("span")]
-    gate = gate_ref[pl.ds(step, 1), :]
+def finish_kernel(pieces_ref, gate_ref, residual_ref, out_ref):
+    gate = gate_ref[...]
     rows = residual_ref.shape[1] // 2
     half = rows // 2
     sums = []
@@ -181,7 +187,15 @@
             name=name,
         )
 
-    packed = call(pack_kernel, [(ny, 3, tokens, HD)], [vmem] * 3, "pack")(q[0], k[0], v[0])
+    packed = pl.pallas_call(
+        pack_kernel,
+        out_shape=jax.ShapeDtypeStruct((ny, 3, tokens, HD), bf16),
+        in_specs=[pl.BlockSpec(memory_space=pltpu.HBM)] * 3,
+        out_specs=vmem,
+        scratch_shapes=[pltpu.SemaphoreType.DMA((3 * width // HD,))],
+        compiler_params=pltpu.CompilerParams(vmem_limit_bytes=60 * 1024 * 1024),
+        name="pack",
+    )(q[0], k[0], v[0])
     with jax.named_scope("exchange_heads"):
         packed = lax.all_to_all(packed, ROW, 0, 0, tiled=True)
     with jax.named_scope("gather_kv"):
@@ -202,27 +216,35 @@
     )
     with jax.named_scope("return_parts"):
         parts = lax.all_to_all(parts, "span", 0, 0, tiled=True)
-        parts, weight_far = lax.optimization_barrier((parts, weight_far))
     near = call(combine_kernel, [(2, rows // 2, HD)], [vmem], "combine")(parts)
     with jax.named_scope("gather_attended"):
+        near, weight_far = lax.optimization_barrier((near, weight_far))
         far = lax.ppermute(near, "zh", swap)
         both = call(spread_kernel, [(ny, 2, rows // 2, HD)], [vmem, vmem], "spread")(near, far)
         both = lax.all_to_all(both, ROW, 0, 0, tiled=True)[: width // HD]
         both = lax.all_gather(both, "core", axis=0, tiled=True)
     cols = weight.shape[0]
-    pieces = call(project_kernel, [(8, 4 * tokens * cols // HD, HD)], [vmem] * 3, "project")(
-        both, weight, weight_far
-    )
+    pieces, gate = pl.pallas_call(
+        project_kernel,
+        out_shape=(
+            jax.ShapeDtypeStruct((8, 4 * tokens * cols // HD, HD), bf16),
+            jax.ShapeDtypeStruct((1, cols), jnp.float32),
+        ),
+        in_specs=[smem] + [vmem] * 4,
+        out_specs=(vmem, vmem),
+        compiler_params=params,
+        name="project",
+    )(noise_steps, gate_table, both, weight, weight_far)
     with jax.named_scope("sum_heads"):
         pieces = lax.all_to_all(pieces, ("head", "y0"), 0, 0, tiled=True)
     mixed = pl.pallas_call(
         finish_kernel,
         out_shape=jax.ShapeDtypeStruct(residual.shape[:0:-1], bf16),
-        in_specs=[smem, vmem, vmem, vmem],
+        in_specs=[vmem, vmem, vmem],
         out_specs=vmem,
         compiler_params=params,
         name="finish",
-    )(noise_steps, pieces, gate_table, residual[0].T)
+    )(pieces, gate, residual[0].T)
     return mixed.T[None]
 
 

time: 118 us -> 116 us (0.983)
  blocking collectives: 66.5 us -> 78.2 us
  waiting for transfers between devices: 13.9 us -> 6.84 us
  starting transfers between devices: 25.4 us -> 20.7 us
  local copies, waits for them, and re-layouts: 3.19 us -> 0.06 us
    all_to_all x0 -> x1, blocking collectives: none -> 11.4 us  [shards(): parts = lax.all_to_all(parts, 'span', 0, 0, tiled=True)]
    all_to_all x1 -> x0, waiting for transfers between devices: 7.03 us -> none  [shards(): parts = lax.all_to_all(parts, 'span', 0, 0, tiled=True)]
    all_to_all x1 -> x0, starting transfers between devices: 4.52 us -> none  [shards(): parts = lax.all_to_all(parts, 'span', 0, 0, tiled=True)]
    unnamed x18 -> x12, local copies, waits for them, and re-layouts: 3.16 us -> 0.03 us
    pallas_call x2, Pallas kernels: 1.01 us -> 3.27 us  [the longest x1 1.74 us: shards(): pl.pallas_call(pack_kernel, out_shape=jax.ShapeDtypeStruct((ny, 3, tokens...]
  transfers between devices with their start and end apart: 5 -> 4, of which waited for: 2 -> 1; matrix products, arithmetic and copies ran while one was open for 0% -> 0% of each run, Pallas kernels for 4% -> 4%
where the time goes in v12:
time: 116 us; the launch traced here: 115 us
  blocking collectives  78.2 us (67%)
  starting transfers between devices  20.7 us (18%)
  Pallas kernels  9.3 us (8%)
  waiting for transfers between devices  6.84 us (6%)
    all_to_all x1, blocking collectives, shards(): both = lax.all_to_all(both, ROW, 0, 0, tiled=True)[:width // HD]  19.1 us
    all_to_all x1, blocking collectives, shards(): pieces = lax.all_to_all(pieces, ('head', 'y0'), 0, 0, tiled=True)  17 us
    all_to_all x1, blocking collectives, shards(): packed = lax.all_to_all(packed, ROW, 0, 0, tiled=True)  16.9 us
    ppermute x1, starting transfers between devices, shards(): kv_far = lax.ppermute(kv, 'zh', swap)  11.4 us
    all_to_all x1, blocking collectives, shards(): parts = lax.all_to_all(parts, 'span', 0, 0, tiled=True)  11.4 us
    ppermute x1, waiting for transfers between devices, shards(): far = lax.ppermute(near, 'zh', swap)  6.83 us
    all_gather x1, blocking collectives, shards(): both = lax.all_gather(both, 'core', axis=0, tiled=True)  6.67 us
    all_gather x1, blocking collectives, shards(): near = lax.all_gather(kv, 'core', axis=0, tiled=True)  4.84 us
  transfers between devices with their start and end apart: 4, of which 1 were waited for; matrix products, arithmetic and copies ran while one was open for 0% of the time, Pallas kernels for 4%

profile of v12, /device:TPU:1, one launch (start us, length us, event | category | flops | bytes accessed | tf_op | source)
XLA Modules:
  0.0 115.2 jit_solution(3650257805190955388)
XLA Ops:
  0.0 1.7 %pack.1 = bf16[8,3,40,128]{3,2,1,0:T(8,128)(2,1)} custom-call(bf16[40,768]{1,0:T(8,128)(2,1)} %bitcast.17, bf16[40,768]{1,0:T(8,128)(2,1)} %bitcast.18, bf16[40,768]{1,0:T(8,128)(2,1)} %bitcast.19), custom_call_target="tpu_custom_call" | custom-call | tf_op jit(solution)/shard_map/pack/pallas_call | solution.py:190
  1.7 16.9 %all_to_all.25.packed_ref = bf16[8,3,40,128]{3,2,1,0:T(8,128)(2,1)S(1)} all-to-all(bf16[8,3,40,128]{3,2,1,0:T(8,128)(2,1)} %pack.1), channel_id=1, replica_groups=mesh['span'=4,'zh'=2,'y2'=2,'y1'=2,'y0'=2,'core'=2,'head'=4] {'y2','y1',..., dimensions={0} | all-to-all | bytes 491520 | tf_op jit(solution)/shard_map/exchange_heads/all_to_all | solution.py:200
  18.6 11.4 %collective-permute-start = (bf16[2,320,128]{2,1,0:T(8,128)(2,1)S(1)}, bf16[2,320,128]{2,1,0:T(8,128)(2,1)S(1)}, u32[]{:S(2)}, u32[]{:S(2)}) collective-permute-start(bf16[2,320,128]{2,1,0:T(8,128)(2,1)S(1)} %bitcast.12), channel_id=1, source_target_pairs={{0,64},{64,0},{1,65},{65,1},{2,66},{66,2},{3,67},{67,3},{4,68},{68... | collective-permute-start | bytes 491528 | tf_op jit(solution)/shard_map/gather_kv/ppermute | solution.py:203
  30.1 0.8 repeat_q.1
  30.8 4.0 %all-to-all-start.1 = ((bf16[4,320,128]{2,1,0:T(8,128)(2,1)}), bf16[4,320,128]{2,1,0:T(8,128)(2,1)S(1)}, u32[]{:S(2)}, u32[]{:S(2)}) async-start(bf16[4,320,128]{2,1,0:T(8,128)(2,1)} %bitcast.4), calls=%async_computation.1 | async-start | bytes 655360 | tf_op jit(solution)/shard_map/gather_q/all_to_all | solution.py:207
  34.8 0.0 copy-start
  34.8 4.8 %all_gather.9.near_ref = bf16[4,320,128]{2,1,0:T(8,128)(2,1)S(1)} all-gather(bf16[2,320,128]{2,1,0:T(8,128)(2,1)S(1)} %bitcast.13), channel_id=1, replica_groups=mesh['span'=4,'zh'=2,'y2'=2,'y1'=2,'y0'=2,'core'=2,'head'=4] {'core'}, dimensions={0}, use_global_device_ids=true | all-gather | bytes 491520 | tf_op jit(solution)/shard_map/gather_kv/all_gather | solution.py:209
  39.7 0.0 copy-done
  39.7 0.0 copy-start.3
  39.7 0.0 copy-start.4
  39.7 2.3 %collective-permute-start.1 = (bf16[192,768]{1,0:T(8,128)(2,1)S(1)}, bf16[192,768]{1,0:T(8,128)(2,1)S(1)}, u32[]{:S(2)}, u32[]{:S(2)}) collective-permute-start(bf16[192,768]{1,0:T(8,128)(2,1)S(1)} %bitcast.14), channel_id=1, source_target_pairs={{0,8},{8,0},{1,9},{9,1},{2,10},{10,2},{3,11},{11,3},{4,12},{12,4},... | collective-permute-start | bytes 884744 | tf_op jit(solution)/shard_map/fetch_weight/ppermute | solution.py:213
  42.0 0.0 collective-permute-done
  42.0 2.3 %all_gather.10.far_ref = bf16[4,320,128]{2,1,0:T(8,128)(2,1)S(1)} all-gather(bf16[2,320,128]{2,1,0:T(8,128)(2,1)S(1)} %collective-permute-done), channel_id=1, replica_groups=mesh['span'=4,'zh'=2,'y2'=2,'y1'=2,'y0'=2,'core'=2,'head'=4] {'core'}, dimensions={0}, use_global_device_ids=true | all-gather | bytes 491520 | tf_op jit(solution)/shard_map/gather_kv/all_gather | solution.py:210
  44.3 0.0 all-to-all-done.1.q_ref
  44.3 0.0 copy-done.3
  44.4 0.0 copy-done.4
  44.4 3.4 %attend.1 = bf16[4,368,128]{2,1,0:T(8,128)(2,1)S(1)} custom-call(s32[4]{0:T(128)S(1)} %copy-done.3, s32[4]{0:T(128)S(1)} %copy-done.4, bf16[4,320,128]{2,1,0:T(8,128)(2,1)S(1)} %all-to-all-done.1.q_ref, bf16[4,320,128]{2,1,0:T(8,128)(2,1)S(1)} %all_gather.9.near_ref, bf16[4,320,128]{2,1,0:T(8,128)(2,1)S(1)} %all_gather.10.far_ref), custom_call_target="tpu_custom_call" | custom-call | tf_op jit(solution)/shard_map/attend/pallas_call | solution.py:214
  47.7 11.4 %all_to_all.26.parts_ref = bf16[4,368,128]{2,1,0:T(8,128)(2,1)S(1)} all-to-all(bf16[4,368,128]{2,1,0:T(8,128)(2,1)S(1)} %attend.1), channel_id=1, replica_groups=mesh['span'=4,'zh'=2,'y2'=2,'y1'=2,'y0'=2,'core'=2,'head'=4] {'span'}, dimensions={0} | all-to-all | bytes 753664 | tf_op jit(solution)/shard_map/return_parts/all_to_all | solution.py:218
  59.1 0.9 combine.1.near_ref
  60.0 0.0 collective-permute-done.1.far_ref
  60.0 3.0 %collective-permute-start.2 = (bf16[2,160,128]{2,1,0:T(8,128)(2,1)S(1)}, bf16[2,160,128]{2,1,0:T(8,128)(2,1)S(1)}, u32[]{:S(2)}, u32[]{:S(2)}) collective-permute-start(bf16[2,160,128]{2,1,0:T(8,128)(2,1)S(1)} %combine.1.near_ref), channel_id=1, source_target_pairs={{0,64},{64,0},{1,65},{65,1},{2,66},{66,2},{3,67},{67,3},{4,68},{68... | collective-permute-start | bytes 245768 | tf_op jit(solution)/shard_map/gather_attended/ppermute | solution.py:222
  63.0 6.8 %collective-permute-done.2.far_ref = bf16[2,160,128]{2,1,0:T(8,128)(2,1)S(1)} collective-permute-done((bf16[2,160,128]{2,1,0:T(8,128)(2,1)S(1)}, bf16[2,160,128]{2,1,0:T(8,128)(2,1)S(1)}, u32[]{:S(2)}, u32[]{:S(2)}) %collective-permute-start.2) | collective-permute-done | bytes 81952 | tf_op jit(solution)/shard_map/gather_attended/ppermute | solution.py:222
  69.9 0.1 spread.1
  69.9 19.1 %all_to_all.27 = bf16[8,2,160,128]{3,2,1,0:T(8,128)(2,1)S(1)} all-to-all(bf16[8,2,160,128]{3,2,1,0:T(8,128)(2,1)S(1)} %spread.1), channel_id=1, replica_groups=mesh['span'=4,'zh'=2,'y2'=2,'y1'=2,'y0'=2,'core'=2,'head'=4] {'y2','y1',..., dimensions={0} | all-to-all | bytes 1310720 | tf_op jit(solution)/shard_map/gather_attended/all_to_all | solution.py:224
  89.1 0.0 copy-start.2
  89.1 0.0 copy-start.5
  89.1 6.7 %all_gather.11.rows_ref = bf16[12,2,160,128]{3,2,1,0:T(8,128)(2,1)S(1)} all-gather(bf16[6,2,160,128]{3,2,1,0:T(8,128)(2,1)S(1)} %slice.4), channel_id=1, replica_groups=mesh['span'=4,'zh'=2,'y2'=2,'y1'=2,'y0'=2,'core'=2,'head'=4] {'core'}, dimensions={0}, use_global_device_ids=true | all-gather | bytes 1474560 | tf_op jit(solution)/shard_map/gather_attended/all_gather | solution.py:225
  95.8 0.0 copy-done.2
  95.8 0.0 copy-done.5
  95.8 1.5 %project.1 = (bf16[8,240,128]{2,1,0:T(8,128)(2,1)S(1)}, f32[1,192]{1,0:T(1,128)S(1)}) custom-call(s32[4]{0:T(128)S(1)} %copy-done.5, f32[4,192]{1,0:T(4,128)S(1)} %copy-done.2, bf16[12,2,160,128]{3,2,1,0:T(8,128)(2,1)S(1)} %all_gather.11.rows_ref, bf16[192,768]{1,0:T(8,128)(2,1)S(1)} %bitcast.15, bf16[192,768]{1,0:T(8,128)(2,1)S(1)} %collective-permute-done.1.far_ref), custom_call_target="tpu_custom_call" | custom-call | tf_op jit(solution)/shard_map/project/pallas_call | solution.py:227
  97.4 0.0 copy-start.1
  97.4 17.0 %all_to_all.28.pieces_ref = bf16[8,240,128]{2,1,0:T(8,128)(2,1)S(1)} all-to-all(bf16[8,240,128]{2,1,0:T(8,128)(2,1)S(1)} %get-tuple-element.19), channel_id=1, replica_groups=mesh['span'=4,'zh'=2,'y2'=2,'y1'=2,'y0'=2,'core'=2,'head'=4] {'head','y0'}, dimensions={0} | all-to-all | bytes 983040 | tf_op jit(solution)/shard_map/sum_heads/all_to_all | solution.py:239
  114.4 0.0 copy-done.1
  114.4 0.9 finish.1
  (2 shorter events, 0.0 us)
Async XLA Ops:
  18.6 23.4 %collective-permute-start = (bf16[2,320,128]{2,1,0:T(8,128)(2,1)S(1)}, bf16[2,320,128]{2,1,0:T(8,128)(2,1)S(1)}, u32[]{:S(2)}, u32[]{:S(2)}) collective-permute-start(bf16[2,320,128]{2,1,0:T(8,128)(2,1)S(1)} %bitcast.12), channel_id=1, source_target_pairs={{0,64},{64,0},{1,65},{65,1},{2,66},{66,2},{3,67},{67,3},{4,68},{68... | collective-permute-start | bytes 491528 | tf_op jit(solution)/shard_map/gather_kv/ppermute | solution.py:203
  30.8 13.5 %all-to-all-start.1 = ((bf16[4,320,128]{2,1,0:T(8,128)(2,1)}), bf16[4,320,128]{2,1,0:T(8,128)(2,1)S(1)}, u32[]{:S(2)}, u32[]{:S(2)}) async-start(bf16[4,320,128]{2,1,0:T(8,128)(2,1)} %bitcast.4), calls=%async_computation.1 | async-start | bytes 655360 | tf_op jit(solution)/shard_map/gather_q/all_to_all | solution.py:207
  34.8 4.8 %copy-start = (bf16[768,192]{0,1:T(8,128)(2,1)S(1)}, bf16[768,192]{0,1:T(8,128)(2,1)}, u32[]{:S(2)}) copy-start(bf16[768,192]{0,1:T(8,128)(2,1)} %param.16) | copy-start | bytes 884740
  39.7 4.7 %copy-start.3 = (s32[4]{0:T(128)S(1)}, s32[4]{0:T(128)}, u32[]{:S(2)}) copy-start(s32[4]{0:T(128)} %order_ref.1) | copy-start | bytes 52
  39.7 4.7 %copy-start.4 = (s32[4]{0:T(128)S(1)}, s32[4]{0:T(128)}, u32[]{:S(2)}) copy-start(s32[4]{0:T(128)} %valid_ref.1) | copy-start | bytes 52
  39.7 20.3 %collective-permute-start.1 = (bf16[192,768]{1,0:T(8,128)(2,1)S(1)}, bf16[192,768]{1,0:T(8,128)(2,1)S(1)}, u32[]{:S(2)}, u32[]{:S(2)}) collective-permute-start(bf16[192,768]{1,0:T(8,128)(2,1)S(1)} %bitcast.14), channel_id=1, source_target_pairs={{0,8},{8,0},{1,9},{9,1},{2,10},{10,2},{3,11},{11,3},{4,12},{12,4},... | collective-permute-start | bytes 884744 | tf_op jit(solution)/shard_map/fetch_weight/ppermute | solution.py:213
  60.0 9.8 %collective-permute-start.2 = (bf16[2,160,128]{2,1,0:T(8,128)(2,1)S(1)}, bf16[2,160,128]{2,1,0:T(8,128)(2,1)S(1)}, u32[]{:S(2)}, u32[]{:S(2)}) collective-permute-start(bf16[2,160,128]{2,1,0:T(8,128)(2,1)S(1)} %combine.1.near_ref), channel_id=1, source_target_pairs={{0,64},{64,0},{1,65},{65,1},{2,66},{66,2},{3,67},{67,3},{4,68},{68... | collective-permute-start | bytes 245768 | tf_op jit(solution)/shard_map/gather_attended/ppermute | solution.py:222
  89.1 6.7 %copy-start.2 = (f32[4,192]{1,0:T(4,128)S(1)}, f32[4,192]{1,0:T(4,128)}, u32[]{:S(2)}) copy-start(f32[4,192]{1,0:T(4,128)} %gates_ref.1) | copy-start | bytes 9220
  89.1 6.7 %copy-start.5 = (s32[4]{0:T(128)S(1)}, s32[4]{0:T(128)}, u32[]{:S(2)}) copy-start(s32[4]{0:T(128)} %steps_ref.1) | copy-start | bytes 52
  97.4 17.0 %copy-start.1 = (bf16[1,320,192]{1,2,0:T(8,128)(2,1)S(1)}, bf16[1,320,192]{1,2,0:T(8,128)(2,1)}, u32[]{:S(2)}) copy-start(bf16[1,320,192]{1,2,0:T(8,128)(2,1)} %param.17) | copy-start | bytes 368644

commit v13 on v11

--- a/solution.py
+++ b/solution.py
@@ -16,20 +16,19 @@
 FRAMES = 8
 
 
-def pack_kernel(q_ref, k_ref, v_ref, out_ref, sems):
+def pack_kernel(q_ref, k_ref, v_ref, out_ref, held_ref, sems):
     heads = q_ref.shape[1] // HD
-    copies = []
-    for h in range(heads):
-        for i, ref in enumerate((q_ref, k_ref, v_ref)):
-            copies.append(
-                pltpu.make_async_copy(ref.at[:, h * HD : (h + 1) * HD], out_ref.at[h, i], sems.at[3 * h + i])
-            )
+    copies = [
+        pltpu.make_async_copy(ref, held_ref.at[i], sems.at[i]) for i, ref in enumerate((q_ref, k_ref, v_ref))
+    ]
     for copy in copies:
         copy.start()
     for h in range(heads, out_ref.shape[0]):
         out_ref[h] = jnp.zeros(out_ref.shape[1:], out_ref.dtype)
-    for copy in copies:
+    for i, copy in enumerate(copies):
         copy.wait()
+        for h in range(heads):
+            out_ref[h, i] = held_ref[i, :, h * HD : (h + 1) * HD]
 
 
 def unpack_kernel(packed_ref, queries_ref, kv_ref):
@@ -164,7 +163,7 @@
         out_shape=jax.ShapeDtypeStruct((ny, 3, tokens, HD), bf16),
         in_specs=[pl.BlockSpec(memory_space=pltpu.HBM)] * 3,
         out_specs=vmem,
-        scratch_shapes=[pltpu.SemaphoreType.DMA((3 * width // HD,))],
+        scratch_shapes=[pltpu.VMEM((3, tokens, width), bf16), pltpu.SemaphoreType.DMA((3,))],
         compiler_params=pltpu.CompilerParams(vmem_limit_bytes=60 * 1024 * 1024),
         name="pack",
     )(q[0], k[0], v[0])

time: 116 us -> 116 us (level)
  no operation moved by 1% of the time
where the time goes in v13:
time: 116 us; the launch traced here: 115 us
  blocking collectives  66.1 us (57%)
  starting transfers between devices  30.4 us (26%)
  Pallas kernels  9.64 us (8%)
  waiting for transfers between devices  8.22 us (7%)
    all_to_all x1, blocking collectives, shards(): both = lax.all_to_all(both, ROW, 0, 0, tiled=True)[:width // HD]  18.7 us
    all_to_all x1, blocking collectives, shards(): packed = lax.all_to_all(packed, ROW, 0, 0, tiled=True)  16.9 us
    all_to_all x1, blocking collectives, shards(): pieces = lax.all_to_all(pieces, ('head', 'y0'), 0, 0, tiled=True)  16.5 us
    ppermute x1, starting transfers between devices, shards(): kv_far = lax.ppermute(kv, 'zh', swap)  11.4 us
    ppermute x1, starting transfers between devices, shards(): far = lax.ppermute(near, 'zh', swap)  8.18 us
    all_gather x1, blocking collectives, shards(): both = lax.all_gather(both, 'core', axis=0, tiled=True)  7.04 us
    ppermute x1, waiting for transfers between devices, shards(): weight_far = lax.ppermute(weight, 'y0', swap)  6.01 us
    all_gather x1, blocking collectives, shards(): near = lax.all_gather(kv, 'core', axis=0, tiled=True)  4.7 us
  transfers between devices with their start and end apart: 5, of which 3 were waited for; matrix products, arithmetic and copies ran while one was open for 0% of the time, Pallas kernels for 0%

profile of v13, /device:TPU:1, one launch (start us, length us, event | category | flops | bytes accessed | tf_op | source)
XLA Modules:
  0.0 114.5 jit_solution(14478591281096429089)
XLA Ops:
  0.0 1.6 %pack.1 = bf16[8,3,40,128]{3,2,1,0:T(8,128)(2,1)} custom-call(bf16[40,768]{1,0:T(8,128)(2,1)} %bitcast.17, bf16[40,768]{1,0:T(8,128)(2,1)} %bitcast.18, bf16[40,768]{1,0:T(8,128)(2,1)} %bitcast.19), custom_call_target="tpu_custom_call" | custom-call | tf_op jit(solution)/shard_map/pack/pallas_call | solution.py:161
  1.6 16.9 %all_to_all.25.packed_ref = bf16[8,3,40,128]{3,2,1,0:T(8,128)(2,1)S(1)} all-to-all(bf16[8,3,40,128]{3,2,1,0:T(8,128)(2,1)} %pack.1), channel_id=1, replica_groups=mesh['span'=4,'zh'=2,'y2'=2,'y1'=2,'y0'=2,'core'=2,'head'=4] {'y2','y1',..., dimensions={0} | all-to-all | bytes 491520 | tf_op jit(solution)/shard_map/exchange_heads/all_to_all | solution.py:171
  18.5 0.8 unpack.1
  19.3 11.4 %collective-permute-start = (bf16[2,320,128]{2,1,0:T(8,128)(2,1)S(1)}, bf16[2,320,128]{2,1,0:T(8,128)(2,1)S(1)}, u32[]{:S(2)}, u32[]{:S(2)}) collective-permute-start(bf16[2,320,128]{2,1,0:T(8,128)(2,1)S(1)} %bitcast.14), channel_id=1, source_target_pairs={{0,64},{64,0},{1,65},{65,1},{2,66},{66,2},{3,67},{67,3},{4,68},{68... | collective-permute-start | bytes 491528 | tf_op jit(solution)/shard_map/gather_kv/ppermute | solution.py:177
  30.7 4.0 %all-to-all-start.1 = ((bf16[4,320,128]{2,1,0:T(8,128)(2,1)}), bf16[4,320,128]{2,1,0:T(8,128)(2,1)S(1)}, u32[]{:S(2)}, u32[]{:S(2)}) async-start(bf16[4,320,128]{2,1,0:T(8,128)(2,1)} %bitcast.3), calls=%async_computation.1 | async-start | bytes 655360 | tf_op jit(solution)/shard_map/gather_q/all_to_all | solution.py:174
  34.7 4.7 %all_gather.9.near_ref = bf16[4,320,128]{2,1,0:T(8,128)(2,1)S(1)} all-gather(bf16[2,320,128]{2,1,0:T(8,128)(2,1)S(1)} %bitcast.15), channel_id=1, replica_groups=mesh['span'=4,'zh'=2,'y2'=2,'y1'=2,'y0'=2,'core'=2,'head'=4] {'core'}, dimensions={0}, use_global_device_ids=true | all-gather | bytes 491520 | tf_op jit(solution)/shard_map/gather_kv/all_gather | solution.py:178
  39.4 0.0 copy-start.3
  39.4 0.0 copy-start.4
  39.4 0.0 collective-permute-done
  39.4 2.2 %all_gather.10.far_ref = bf16[4,320,128]{2,1,0:T(8,128)(2,1)S(1)} all-gather(bf16[2,320,128]{2,1,0:T(8,128)(2,1)S(1)} %collective-permute-done), channel_id=1, replica_groups=mesh['span'=4,'zh'=2,'y2'=2,'y1'=2,'y0'=2,'core'=2,'head'=4] {'core'}, dimensions={0}, use_global_device_ids=true | all-gather | bytes 491520 | tf_op jit(solution)/shard_map/gather_kv/all_gather | solution.py:179
  41.6 0.0 all-to-all-done.1.q_ref
  41.6 0.0 copy-done.3
  41.6 0.0 copy-done.4
  41.6 4.2 %attend.1 = bf16[4,320,256]{2,1,0:T(8,128)(2,1)} custom-call(s32[4]{0:T(128)S(1)} %copy-done.3, s32[4]{0:T(128)S(1)} %copy-done.4, bf16[4,320,128]{2,1,0:T(8,128)(2,1)S(1)} %all-to-all-done.1.q_ref, bf16[4,320,128]{2,1,0:T(8,128)(2,1)S(1)} %all_gather.9.near_ref, bf16[4,320,128]{2,1,0:T(8,128)(2,1)S(1)} %all_gather.10.far_ref), custom_call_target="tpu_custom_call" | custom-call | tf_op jit(solution)/shard_map/attend/pallas_call | solution.py:183
  45.8 0.0 copy-start
  45.8 4.6 %all-to-all-start.2 = ((bf16[4,320,256]{2,1,0:T(8,128)(2,1)}), bf16[4,320,256]{2,1,0:T(8,128)(2,1)S(1)}, u32[]{:S(2)}, u32[]{:S(2)}) async-start(bf16[4,320,256]{2,1,0:T(8,128)(2,1)} %attend.1), calls=%async_computation.2 | async-start | bytes 1310720 | tf_op jit(solution)/shard_map/return_parts/all_to_all | solution.py:187
  50.5 0.0 copy-done
  50.5 2.2 %collective-permute-start.1 = (bf16[192,768]{1,0:T(8,128)(2,1)S(1)}, bf16[192,768]{1,0:T(8,128)(2,1)S(1)}, u32[]{:S(2)}, u32[]{:S(2)}) collective-permute-start(bf16[192,768]{1,0:T(8,128)(2,1)S(1)} %bitcast.12), channel_id=1, source_target_pairs={{0,8},{8,0},{1,9},{9,1},{2,10},{10,2},{3,11},{11,3},{4,12},{12,4},... | collective-permute-start | bytes 884744 | tf_op jit(solution)/shard_map/fetch_weight/ppermute | solution.py:182
  52.7 6.0 %collective-permute-done.1.far_ref = bf16[192,768]{1,0:T(8,128)(2,1)S(1)} collective-permute-done((bf16[192,768]{1,0:T(8,128)(2,1)S(1)}, bf16[192,768]{1,0:T(8,128)(2,1)S(1)}, u32[]{:S(2)}, u32[]{:S(2)}) %collective-permute-start.1) | collective-permute-done | bytes 294944 | tf_op jit(solution)/shard_map/fetch_weight/ppermute | solution.py:182
  58.7 0.3 all-to-all-done.2.parts_ref
  59.0 0.6 combine.1.near_ref
  59.5 8.2 %collective-permute-start.2 = (bf16[2,160,128]{2,1,0:T(8,128)(2,1)S(1)}, bf16[2,160,128]{2,1,0:T(8,128)(2,1)S(1)}, u32[]{:S(2)}, u32[]{:S(2)}) collective-permute-start(bf16[2,160,128]{2,1,0:T(8,128)(2,1)S(1)} %combine.1.near_ref), channel_id=1, source_target_pairs={{0,64},{64,0},{1,65},{65,1},{2,66},{66,2},{3,67},{67,3},{4,68},{68... | collective-permute-start | bytes 245768 | tf_op jit(solution)/shard_map/gather_attended/ppermute | solution.py:191
  67.7 1.9 %collective-permute-done.2.far_ref = bf16[2,160,128]{2,1,0:T(8,128)(2,1)S(1)} collective-permute-done((bf16[2,160,128]{2,1,0:T(8,128)(2,1)S(1)}, bf16[2,160,128]{2,1,0:T(8,128)(2,1)S(1)}, u32[]{:S(2)}, u32[]{:S(2)}) %collective-permute-start.2) | collective-permute-done | bytes 81952 | tf_op jit(solution)/shard_map/gather_attended/ppermute | solution.py:191
  69.6 0.1 spread.1
  69.7 18.7 %all_to_all.26 = bf16[8,2,160,128]{3,2,1,0:T(8,128)(2,1)S(1)} all-to-all(bf16[8,2,160,128]{3,2,1,0:T(8,128)(2,1)S(1)} %spread.1), channel_id=1, replica_groups=mesh['span'=4,'zh'=2,'y2'=2,'y1'=2,'y0'=2,'core'=2,'head'=4] {'y2','y1',..., dimensions={0} | all-to-all | bytes 1310720 | tf_op jit(solution)/shard_map/gather_attended/all_to_all | solution.py:193
  88.5 0.0 copy-start.2
  88.5 0.0 copy-start.5
  88.5 7.0 %all_gather.11.rows_ref = bf16[12,2,160,128]{3,2,1,0:T(8,128)(2,1)S(1)} all-gather(bf16[6,2,160,128]{3,2,1,0:T(8,128)(2,1)S(1)} %slice.4), channel_id=1, replica_groups=mesh['span'=4,'zh'=2,'y2'=2,'y1'=2,'y0'=2,'core'=2,'head'=4] {'core'}, dimensions={0}, use_global_device_ids=true | all-gather | bytes 1474560 | tf_op jit(solution)/shard_map/gather_attended/all_gather | solution.py:194
  95.6 0.0 copy-done.2
  95.6 0.0 copy-done.5
  95.6 1.5 %project.1 = (bf16[8,240,128]{2,1,0:T(8,128)(2,1)S(1)}, f32[1,192]{1,0:T(1,128)S(1)}) custom-call(s32[4]{0:T(128)S(1)} %copy-done.5, f32[4,192]{1,0:T(4,128)S(1)} %copy-done.2, bf16[12,2,160,128]{3,2,1,0:T(8,128)(2,1)S(1)} %all_gather.11.rows_ref, bf16[192,768]{1,0:T(8,128)(2,1)S(1)} %bitcast.13, bf16[192,768]{1,0:T(8,128)(2,1)S(1)} %collective-permute-done.1.far_ref), custom_call_target="tpu_custom_call" | custom-call | tf_op jit(solution)/shard_map/project/pallas_call | solution.py:196
  97.1 0.0 copy-start.1
  97.1 16.5 %all_to_all.27.pieces_ref = bf16[8,240,128]{2,1,0:T(8,128)(2,1)S(1)} all-to-all(bf16[8,240,128]{2,1,0:T(8,128)(2,1)S(1)} %get-tuple-element.19), channel_id=1, replica_groups=mesh['span'=4,'zh'=2,'y2'=2,'y1'=2,'y0'=2,'core'=2,'head'=4] {'head','y0'}, dimensions={0} | all-to-all | bytes 983040 | tf_op jit(solution)/shard_map/sum_heads/all_to_all | solution.py:208
  113.6 0.0 copy-done.1
  113.7 0.9 finish.1
  (1 shorter events, 0.0 us)
Async XLA Ops:
  19.3 20.2 %collective-permute-start = (bf16[2,320,128]{2,1,0:T(8,128)(2,1)S(1)}, bf16[2,320,128]{2,1,0:T(8,128)(2,1)S(1)}, u32[]{:S(2)}, u32[]{:S(2)}) collective-permute-start(bf16[2,320,128]{2,1,0:T(8,128)(2,1)S(1)} %bitcast.14), channel_id=1, source_target_pairs={{0,64},{64,0},{1,65},{65,1},{2,66},{66,2},{3,67},{67,3},{4,68},{68... | collective-permute-start | bytes 491528 | tf_op jit(solution)/shard_map/gather_kv/ppermute | solution.py:177
  30.7 10.9 %all-to-all-start.1 = ((bf16[4,320,128]{2,1,0:T(8,128)(2,1)}), bf16[4,320,128]{2,1,0:T(8,128)(2,1)S(1)}, u32[]{:S(2)}, u32[]{:S(2)}) async-start(bf16[4,320,128]{2,1,0:T(8,128)(2,1)} %bitcast.3), calls=%async_computation.1 | async-start | bytes 655360 | tf_op jit(solution)/shard_map/gather_q/all_to_all | solution.py:174
  39.4 2.2 %copy-start.3 = (s32[4]{0:T(128)S(1)}, s32[4]{0:T(128)}, u32[]{:S(2)}) copy-start(s32[4]{0:T(128)} %order_ref.1) | copy-start | bytes 52
  39.4 2.2 %copy-start.4 = (s32[4]{0:T(128)S(1)}, s32[4]{0:T(128)}, u32[]{:S(2)}) copy-start(s32[4]{0:T(128)} %valid_ref.1) | copy-start | bytes 52
  45.8 4.7 %copy-start = (bf16[768,192]{0,1:T(8,128)(2,1)S(1)}, bf16[768,192]{0,1:T(8,128)(2,1)}, u32[]{:S(2)}) copy-start(bf16[768,192]{0,1:T(8,128)(2,1)} %param.16) | copy-start | bytes 884740
  45.8 13.1 %all-to-all-start.2 = ((bf16[4,320,256]{2,1,0:T(8,128)(2,1)}), bf16[4,320,256]{2,1,0:T(8,128)(2,1)S(1)}, u32[]{:S(2)}, u32[]{:S(2)}) async-start(bf16[4,320,256]{2,1,0:T(8,128)(2,1)} %attend.1), calls=%async_computation.2 | async-start | bytes 1310720 | tf_op jit(solution)/shard_map/return_parts/all_to_all | solution.py:187
  50.5 8.2 %collective-permute-start.1 = (bf16[192,768]{1,0:T(8,128)(2,1)S(1)}, bf16[192,768]{1,0:T(8,128)(2,1)S(1)}, u32[]{:S(2)}, u32[]{:S(2)}) collective-permute-start(bf16[192,768]{1,0:T(8,128)(2,1)S(1)} %bitcast.12), channel_id=1, source_target_pairs={{0,8},{8,0},{1,9},{9,1},{2,10},{10,2},{3,11},{11,3},{4,12},{12,4},... | collective-permute-start | bytes 884744 | tf_op jit(solution)/shard_map/fetch_weight/ppermute | solution.py:182
  59.5 10.1 %collective-permute-start.2 = (bf16[2,160,128]{2,1,0:T(8,128)(2,1)S(1)}, bf16[2,160,128]{2,1,0:T(8,128)(2,1)S(1)}, u32[]{:S(2)}, u32[]{:S(2)}) collective-permute-start(bf16[2,160,128]{2,1,0:T(8,128)(2,1)S(1)} %combine.1.near_ref), channel_id=1, source_target_pairs={{0,64},{64,0},{1,65},{65,1},{2,66},{66,2},{3,67},{67,3},{4,68},{68... | collective-permute-start | bytes 245768 | tf_op jit(solution)/shard_map/gather_attended/ppermute | solution.py:191
  88.5 7.1 %copy-start.2 = (f32[4,192]{1,0:T(4,128)S(1)}, f32[4,192]{1,0:T(4,128)}, u32[]{:S(2)}) copy-start(f32[4,192]{1,0:T(4,128)} %gates_ref.1) | copy-start | bytes 9220
  88.5 7.1 %copy-start.5 = (s32[4]{0:T(128)S(1)}, s32[4]{0:T(128)}, u32[]{:S(2)}) copy-start(s32[4]{0:T(128)} %steps_ref.1) | copy-start | bytes 52
  97.1 16.5 %copy-start.1 = (bf16[1,320,192]{1,2,0:T(8,128)(2,1)S(1)}, bf16[1,320,192]{1,2,0:T(8,128)(2,1)}, u32[]{:S(2)}) copy-start(bf16[1,320,192]{1,2,0:T(8,128)(2,1)} %param.17) | copy-start | bytes 368644

commit v14 on v13

--- a/solution.py
+++ b/solution.py
@@ -39,7 +39,7 @@
             kv_ref[i, y] = packed_ref[y, 1 + i]
 
 
-def attend_kernel(order_ref, valid_ref, q_ref, near_ref, far_ref, out_ref):
+def attend_kernel(order_ref, valid_ref, q_ref, near_ref, far_ref, out_ref, held_ref, sems):
     blocks, rows = q_ref.shape[:2]
     zh = lax.axis_index("zh")
     span = lax.axis_index("span")
@@ -57,6 +57,7 @@
     bias = jnp.where(inner < limit, 0.0, CLOSED)
     lane = lax.broadcasted_iota(jnp.int32, (rows, HD), 1)
     scale = math.log2(math.e) / HD**0.5
+    copies = []
     for block in range(blocks):
         closed = jnp.where(order_ref[span] <= order_ref[block], 0.0, CLOSED)
         s = lax.dot_general(q_ref[block], keys, (((1,), (1,)), ((), ())), preferred_element_type=jnp.float32)
@@ -68,8 +69,13 @@
         acc = jnp.dot(w.astype(jnp.bfloat16), values, preferred_element_type=jnp.float32)
         coarse = total.astype(jnp.bfloat16).astype(jnp.float32)
         stats = jnp.where(lane == 0, top, jnp.where(lane == 1, coarse, total - coarse))
-        out_ref[block, :, :HD] = acc.astype(jnp.bfloat16)
-        out_ref[block, :, HD:] = stats.astype(jnp.bfloat16)
+        held_ref[block, :, :HD] = acc.astype(jnp.bfloat16)
+        held_ref[block, :, HD:] = stats.astype(jnp.bfloat16)
+        copy = pltpu.make_async_copy(held_ref.at[block], out_ref.at[block], sems.at[block])
+        copy.start()
+        copies.append(copy)
+    for copy in copies:
+        copy.wait()
 
 
 def combine_kernel(parts_ref, out_ref):
@@ -180,9 +186,15 @@
     with jax.named_scope("fetch_weight"):
         weight, near = lax.optimization_barrier((out_weight.T, near))
         weight_far = lax.ppermute(weight, "y0", swap)
-    parts = call(attend_kernel, [(nx, rows, 2 * HD)], [smem, smem, vmem, vmem, vmem], "attend")(
-        block_order, valid_frames, queries, near, far
-    )
+    parts = pl.pallas_call(
+        attend_kernel,
+        out_shape=jax.ShapeDtypeStruct((nx, rows, 2 * HD), bf16),
+        in_specs=[smem, smem, vmem, vmem, vmem],
+        out_specs=pl.BlockSpec(memory_space=pltpu.HBM),
+        scratch_shapes=[pltpu.VMEM((nx, rows, 2 * HD), bf16), pltpu.SemaphoreType.DMA((nx,))],
+        compiler_params=params,
+        name="attend",
+    )(block_order, valid_frames, queries, near, far)
     with jax.named_scope("return_parts"):
         parts = lax.all_to_all(parts, "span", 0, 0, tiled=True)
         parts, weight_far = lax.optimization_barrier((parts, weight_far))

time: 116 us -> 116 us (level)
  no operation moved by 1% of the time
where the time goes in v14:
time: 116 us; the launch traced here: 114 us
  blocking collectives  66.1 us (57%)
  starting transfers between devices  30.5 us (26%)
  Pallas kernels  9.52 us (8%)
  waiting for transfers between devices  8.22 us (7%)
    all_to_all x1, blocking collectives, shards(): both = lax.all_to_all(both, ROW, 0, 0, tiled=True)[:width // HD]  18.8 us
    all_to_all x1, blocking collectives, shards(): packed = lax.all_to_all(packed, ROW, 0, 0, tiled=True)  16.9 us
    all_to_all x1, blocking collectives, shards(): pieces = lax.all_to_all(pieces, ('head', 'y0'), 0, 0, tiled=True)  16.5 us
    ppermute x1, starting transfers between devices, shards(): kv_far = lax.ppermute(kv, 'zh', swap)  11.4 us
    ppermute x1, starting transfers between devices, shards(): far = lax.ppermute(near, 'zh', swap)  8.18 us
    all_gather x1, blocking collectives, shards(): both = lax.all_gather(both, 'core', axis=0, tiled=True)  7.02 us
    ppermute x1, waiting for transfers between devices, shards(): weight_far = lax.ppermute(weight, 'y0', swap)  6.01 us
    all_gather x1, blocking collectives, shards(): near = lax.all_gather(kv, 'core', axis=0, tiled=True)  4.7 us
  transfers between devices with their start and end apart: 5, of which 3 were waited for; matrix products, arithmetic and copies ran while one was open for 0% of the time, Pallas kernels for 0%

profile of v14, /device:TPU:1, one launch (start us, length us, event | category | flops | bytes accessed | tf_op | source)
XLA Modules:
  0.0 114.4 jit_solution(17525559509890431844)
XLA Ops:
  0.0 1.6 %pack.1 = bf16[8,3,40,128]{3,2,1,0:T(8,128)(2,1)} custom-call(bf16[40,768]{1,0:T(8,128)(2,1)} %bitcast.17, bf16[40,768]{1,0:T(8,128)(2,1)} %bitcast.18, bf16[40,768]{1,0:T(8,128)(2,1)} %bitcast.19), custom_call_target="tpu_custom_call" | custom-call | tf_op jit(solution)/shard_map/pack/pallas_call | solution.py:167
  1.6 16.9 %all_to_all.25.packed_ref = bf16[8,3,40,128]{3,2,1,0:T(8,128)(2,1)S(1)} all-to-all(bf16[8,3,40,128]{3,2,1,0:T(8,128)(2,1)} %pack.1), channel_id=1, replica_groups=mesh['span'=4,'zh'=2,'y2'=2,'y1'=2,'y0'=2,'core'=2,'head'=4] {'y2','y1',..., dimensions={0} | all-to-all | bytes 491520 | tf_op jit(solution)/shard_map/exchange_heads/all_to_all | solution.py:177
  18.5 0.8 unpack.1
  19.3 11.4 %collective-permute-start = (bf16[2,320,128]{2,1,0:T(8,128)(2,1)S(1)}, bf16[2,320,128]{2,1,0:T(8,128)(2,1)S(1)}, u32[]{:S(2)}, u32[]{:S(2)}) collective-permute-start(bf16[2,320,128]{2,1,0:T(8,128)(2,1)S(1)} %bitcast.14), channel_id=1, source_target_pairs={{0,64},{64,0},{1,65},{65,1},{2,66},{66,2},{3,67},{67,3},{4,68},{68... | collective-permute-start | bytes 491528 | tf_op jit(solution)/shard_map/gather_kv/ppermute | solution.py:183
  30.7 4.0 %all-to-all-start.1 = ((bf16[4,320,128]{2,1,0:T(8,128)(2,1)}), bf16[4,320,128]{2,1,0:T(8,128)(2,1)S(1)}, u32[]{:S(2)}, u32[]{:S(2)}) async-start(bf16[4,320,128]{2,1,0:T(8,128)(2,1)} %bitcast.3), calls=%async_computation.1 | async-start | bytes 655360 | tf_op jit(solution)/shard_map/gather_q/all_to_all | solution.py:180
  34.7 4.7 %all_gather.9.near_ref = bf16[4,320,128]{2,1,0:T(8,128)(2,1)S(1)} all-gather(bf16[2,320,128]{2,1,0:T(8,128)(2,1)S(1)} %bitcast.15), channel_id=1, replica_groups=mesh['span'=4,'zh'=2,'y2'=2,'y1'=2,'y0'=2,'core'=2,'head'=4] {'core'}, dimensions={0}, use_global_device_ids=true | all-gather | bytes 491520 | tf_op jit(solution)/shard_map/gather_kv/all_gather | solution.py:184
  39.4 0.0 copy-start.3
  39.4 0.0 copy-start.4
  39.4 0.0 collective-permute-done
  39.4 2.2 %all_gather.10.far_ref = bf16[4,320,128]{2,1,0:T(8,128)(2,1)S(1)} all-gather(bf16[2,320,128]{2,1,0:T(8,128)(2,1)S(1)} %collective-permute-done), channel_id=1, replica_groups=mesh['span'=4,'zh'=2,'y2'=2,'y1'=2,'y0'=2,'core'=2,'head'=4] {'core'}, dimensions={0}, use_global_device_ids=true | all-gather | bytes 491520 | tf_op jit(solution)/shard_map/gather_kv/all_gather | solution.py:185
  41.6 0.0 all-to-all-done.1.q_ref
  41.6 0.0 copy-done.3
  41.6 0.0 copy-done.4
  41.6 4.1 %attend.1 = bf16[4,320,256]{2,1,0:T(8,128)(2,1)} custom-call(s32[4]{0:T(128)S(1)} %copy-done.3, s32[4]{0:T(128)S(1)} %copy-done.4, bf16[4,320,128]{2,1,0:T(8,128)(2,1)S(1)} %all-to-all-done.1.q_ref, bf16[4,320,128]{2,1,0:T(8,128)(2,1)S(1)} %all_gather.9.near_ref, bf16[4,320,128]{2,1,0:T(8,128)(2,1)S(1)} %all_gather.10.far_ref), custom_call_target="tpu_custom_call" | custom-call | tf_op jit(solution)/shard_map/attend/pallas_call | solution.py:189
  45.7 0.0 copy-start
  45.7 4.7 %all-to-all-start.2 = ((bf16[4,320,256]{2,1,0:T(8,128)(2,1)}), bf16[4,320,256]{2,1,0:T(8,128)(2,1)S(1)}, u32[]{:S(2)}, u32[]{:S(2)}) async-start(bf16[4,320,256]{2,1,0:T(8,128)(2,1)} %attend.1), calls=%async_computation.2 | async-start | bytes 1310720 | tf_op jit(solution)/shard_map/return_parts/all_to_all | solution.py:199
  50.4 0.0 copy-done
  50.4 2.2 %collective-permute-start.1 = (bf16[192,768]{1,0:T(8,128)(2,1)S(1)}, bf16[192,768]{1,0:T(8,128)(2,1)S(1)}, u32[]{:S(2)}, u32[]{:S(2)}) collective-permute-start(bf16[192,768]{1,0:T(8,128)(2,1)S(1)} %bitcast.12), channel_id=1, source_target_pairs={{0,8},{8,0},{1,9},{9,1},{2,10},{10,2},{3,11},{11,3},{4,12},{12,4},... | collective-permute-start | bytes 884744 | tf_op jit(solution)/shard_map/fetch_weight/ppermute | solution.py:188
  52.6 6.0 %collective-permute-done.1.far_ref = bf16[192,768]{1,0:T(8,128)(2,1)S(1)} collective-permute-done((bf16[192,768]{1,0:T(8,128)(2,1)S(1)}, bf16[192,768]{1,0:T(8,128)(2,1)S(1)}, u32[]{:S(2)}, u32[]{:S(2)}) %collective-permute-start.1) | collective-permute-done | bytes 294944 | tf_op jit(solution)/shard_map/fetch_weight/ppermute | solution.py:188
  58.6 0.3 all-to-all-done.2.parts_ref
  58.9 0.6 combine.1.near_ref
  59.4 8.2 %collective-permute-start.2 = (bf16[2,160,128]{2,1,0:T(8,128)(2,1)S(1)}, bf16[2,160,128]{2,1,0:T(8,128)(2,1)S(1)}, u32[]{:S(2)}, u32[]{:S(2)}) collective-permute-start(bf16[2,160,128]{2,1,0:T(8,128)(2,1)S(1)} %combine.1.near_ref), channel_id=1, source_target_pairs={{0,64},{64,0},{1,65},{65,1},{2,66},{66,2},{3,67},{67,3},{4,68},{68... | collective-permute-start | bytes 245768 | tf_op jit(solution)/shard_map/gather_attended/ppermute | solution.py:203
  67.6 1.9 %collective-permute-done.2.far_ref = bf16[2,160,128]{2,1,0:T(8,128)(2,1)S(1)} collective-permute-done((bf16[2,160,128]{2,1,0:T(8,128)(2,1)S(1)}, bf16[2,160,128]{2,1,0:T(8,128)(2,1)S(1)}, u32[]{:S(2)}, u32[]{:S(2)}) %collective-permute-start.2) | collective-permute-done | bytes 81952 | tf_op jit(solution)/shard_map/gather_attended/ppermute | solution.py:203
  69.5 0.1 spread.1
  69.6 18.8 %all_to_all.26 = bf16[8,2,160,128]{3,2,1,0:T(8,128)(2,1)S(1)} all-to-all(bf16[8,2,160,128]{3,2,1,0:T(8,128)(2,1)S(1)} %spread.1), channel_id=1, replica_groups=mesh['span'=4,'zh'=2,'y2'=2,'y1'=2,'y0'=2,'core'=2,'head'=4] {'y2','y1',..., dimensions={0} | all-to-all | bytes 1310720 | tf_op jit(solution)/shard_map/gather_attended/all_to_all | solution.py:205
  88.4 0.0 copy-start.2
  88.4 0.0 copy-start.5
  88.4 7.0 %all_gather.11.rows_ref = bf16[12,2,160,128]{3,2,1,0:T(8,128)(2,1)S(1)} all-gather(bf16[6,2,160,128]{3,2,1,0:T(8,128)(2,1)S(1)} %slice.4), channel_id=1, replica_groups=mesh['span'=4,'zh'=2,'y2'=2,'y1'=2,'y0'=2,'core'=2,'head'=4] {'core'}, dimensions={0}, use_global_device_ids=true | all-gather | bytes 1474560 | tf_op jit(solution)/shard_map/gather_attended/all_gather | solution.py:206
  95.5 0.0 copy-done.2
  95.5 0.0 copy-done.5
  95.5 1.5 %project.1 = (bf16[8,240,128]{2,1,0:T(8,128)(2,1)S(1)}, f32[1,192]{1,0:T(1,128)S(1)}) custom-call(s32[4]{0:T(128)S(1)} %copy-done.5, f32[4,192]{1,0:T(4,128)S(1)} %copy-done.2, bf16[12,2,160,128]{3,2,1,0:T(8,128)(2,1)S(1)} %all_gather.11.rows_ref, bf16[192,768]{1,0:T(8,128)(2,1)S(1)} %bitcast.13, bf16[192,768]{1,0:T(8,128)(2,1)S(1)} %collective-permute-done.1.far_ref), custom_call_target="tpu_custom_call" | custom-call | tf_op jit(solution)/shard_map/project/pallas_call | solution.py:208
  97.0 0.0 copy-start.1
  97.0 16.5 %all_to_all.27.pieces_ref = bf16[8,240,128]{2,1,0:T(8,128)(2,1)S(1)} all-to-all(bf16[8,240,128]{2,1,0:T(8,128)(2,1)S(1)} %get-tuple-element.19), channel_id=1, replica_groups=mesh['span'=4,'zh'=2,'y2'=2,'y1'=2,'y0'=2,'core'=2,'head'=4] {'head','y0'}, dimensions={0} | all-to-all | bytes 983040 | tf_op jit(solution)/shard_map/sum_heads/all_to_all | solution.py:220
  113.6 0.0 copy-done.1
  113.6 0.9 finish.1
  (1 shorter events, 0.0 us)
Async XLA Ops:
  19.3 20.2 %collective-permute-start = (bf16[2,320,128]{2,1,0:T(8,128)(2,1)S(1)}, bf16[2,320,128]{2,1,0:T(8,128)(2,1)S(1)}, u32[]{:S(2)}, u32[]{:S(2)}) collective-permute-start(bf16[2,320,128]{2,1,0:T(8,128)(2,1)S(1)} %bitcast.14), channel_id=1, source_target_pairs={{0,64},{64,0},{1,65},{65,1},{2,66},{66,2},{3,67},{67,3},{4,68},{68... | collective-permute-start | bytes 491528 | tf_op jit(solution)/shard_map/gather_kv/ppermute | solution.py:183
  30.7 10.9 %all-to-all-start.1 = ((bf16[4,320,128]{2,1,0:T(8,128)(2,1)}), bf16[4,320,128]{2,1,0:T(8,128)(2,1)S(1)}, u32[]{:S(2)}, u32[]{:S(2)}) async-start(bf16[4,320,128]{2,1,0:T(8,128)(2,1)} %bitcast.3), calls=%async_computation.1 | async-start | bytes 655360 | tf_op jit(solution)/shard_map/gather_q/all_to_all | solution.py:180
  39.4 2.2 %copy-start.3 = (s32[4]{0:T(128)S(1)}, s32[4]{0:T(128)}, u32[]{:S(2)}) copy-start(s32[4]{0:T(128)} %order_ref.1) | copy-start | bytes 52
  39.4 2.2 %copy-start.4 = (s32[4]{0:T(128)S(1)}, s32[4]{0:T(128)}, u32[]{:S(2)}) copy-start(s32[4]{0:T(128)} %valid_ref.1) | copy-start | bytes 52
  45.7 4.7 %copy-start = (bf16[768,192]{0,1:T(8,128)(2,1)S(1)}, bf16[768,192]{0,1:T(8,128)(2,1)}, u32[]{:S(2)}) copy-start(bf16[768,192]{0,1:T(8,128)(2,1)} %param.16) | copy-start | bytes 884740
  45.7 13.2 %all-to-all-start.2 = ((bf16[4,320,256]{2,1,0:T(8,128)(2,1)}), bf16[4,320,256]{2,1,0:T(8,128)(2,1)S(1)}, u32[]{:S(2)}, u32[]{:S(2)}) async-start(bf16[4,320,256]{2,1,0:T(8,128)(2,1)} %attend.1), calls=%async_computation.2 | async-start | bytes 1310720 | tf_op jit(solution)/shard_map/return_parts/all_to_all | solution.py:199
  50.4 8.2 %collective-permute-start.1 = (bf16[192,768]{1,0:T(8,128)(2,1)S(1)}, bf16[192,768]{1,0:T(8,128)(2,1)S(1)}, u32[]{:S(2)}, u32[]{:S(2)}) collective-permute-start(bf16[192,768]{1,0:T(8,128)(2,1)S(1)} %bitcast.12), channel_id=1, source_target_pairs={{0,8},{8,0},{1,9},{9,1},{2,10},{10,2},{3,11},{11,3},{4,12},{12,4},... | collective-permute-start | bytes 884744 | tf_op jit(solution)/shard_map/fetch_weight/ppermute | solution.py:188
  59.4 10.1 %collective-permute-start.2 = (bf16[2,160,128]{2,1,0:T(8,128)(2,1)S(1)}, bf16[2,160,128]{2,1,0:T(8,128)(2,1)S(1)}, u32[]{:S(2)}, u32[]{:S(2)}) collective-permute-start(bf16[2,160,128]{2,1,0:T(8,128)(2,1)S(1)} %combine.1.near_ref), channel_id=1, source_target_pairs={{0,64},{64,0},{1,65},{65,1},{2,66},{66,2},{3,67},{67,3},{4,68},{68... | collective-permute-start | bytes 245768 | tf_op jit(solution)/shard_map/gather_attended/ppermute | solution.py:203
  88.4 7.1 %copy-start.2 = (f32[4,192]{1,0:T(4,128)S(1)}, f32[4,192]{1,0:T(4,128)}, u32[]{:S(2)}) copy-start(f32[4,192]{1,0:T(4,128)} %gates_ref.1) | copy-start | bytes 9220
  88.4 7.0 %copy-start.5 = (s32[4]{0:T(128)S(1)}, s32[4]{0:T(128)}, u32[]{:S(2)}) copy-start(s32[4]{0:T(128)} %steps_ref.1) | copy-start | bytes 52
  97.0 16.6 %copy-start.1 = (bf16[1,320,192]{1,2,0:T(8,128)(2,1)S(1)}, bf16[1,320,192]{1,2,0:T(8,128)(2,1)}, u32[]{:S(2)}) copy-start(bf16[1,320,192]{1,2,0:T(8,128)(2,1)} %param.17) | copy-start | bytes 368644

commit v15 on v14

--- a/solution.py
+++ b/solution.py
@@ -31,12 +31,16 @@
             out_ref[h, i] = held_ref[i, :, h * HD : (h + 1) * HD]
 
 
-def unpack_kernel(packed_ref, queries_ref, kv_ref):
+def keep_kv_kernel(packed_ref, kv_ref):
+    for y in range(packed_ref.shape[0]):
+        for i in range(2):
+            kv_ref[i, y] = packed_ref[y, 1 + i]
+
+
+def repeat_q_kernel(packed_ref, queries_ref):
     for y in range(packed_ref.shape[0]):
         for i in range(queries_ref.shape[0]):
             queries_ref[i, y] = packed_ref[y, 0]
-        for i in range(2):
-            kv_ref[i, y] = packed_ref[y, 1 + i]
 
 
 def attend_kernel(order_ref, valid_ref, q_ref, near_ref, far_ref, out_ref, held_ref, sems):
@@ -175,12 +179,14 @@
     )(q[0], k[0], v[0])
     with jax.named_scope("exchange_heads"):
         packed = lax.all_to_all(packed, ROW, 0, 0, tiled=True)
-    queries, kv = call(unpack_kernel, [(nx, ny, tokens, HD), (2, ny, tokens, HD)], [vmem], "unpack")(packed)
+    with jax.named_scope("gather_kv"):
+        kv = call(keep_kv_kernel, [(2, ny, tokens, HD)], [vmem], "keep_kv")(packed).reshape(2, rows, HD)
+        kv_far = lax.ppermute(kv, "zh", swap)
     with jax.named_scope("gather_q"):
+        packed, kv = lax.optimization_barrier((packed, kv))
+        queries = call(repeat_q_kernel, [(nx, ny, tokens, HD)], [vmem], "repeat_q")(packed)
         queries = lax.all_to_all(queries.reshape(nx, rows, HD), "span", 0, 0, tiled=True)
     with jax.named_scope("gather_kv"):
-        kv = kv.reshape(2, rows, HD)
-        kv_far = lax.ppermute(kv, "zh", swap)
         near = lax.all_gather(kv, "core", axis=0, tiled=True)
         far = lax.all_gather(kv_far, "core", axis=0, tiled=True)
     with jax.named_scope("fetch_weight"):

time: 116 us -> 115 us (level)
  transfers between devices with their start and end apart: 5 -> 5, of which waited for: 3 -> 3; matrix products, arithmetic and copies ran while one was open for 0% -> 0% of each run, Pallas kernels for 0% -> 1%
where the time goes in v15:
time: 115 us; the launch traced here: 114 us
  blocking collectives  66.2 us (58%)
  starting transfers between devices  29.7 us (26%)
  Pallas kernels  9.5 us (8%)
  waiting for transfers between devices  8.23 us (7%)
    all_to_all x1, blocking collectives, shards(): both = lax.all_to_all(both, ROW, 0, 0, tiled=True)[:width // HD]  18.2 us
    all_to_all x1, blocking collectives, shards(): packed = lax.all_to_all(packed, ROW, 0, 0, tiled=True)  16.9 us
    all_to_all x1, blocking collectives, shards(): pieces = lax.all_to_all(pieces, ('head', 'y0'), 0, 0, tiled=True)  16.6 us
    ppermute x1, starting transfers between devices, shards(): kv_far = lax.ppermute(kv, 'zh', swap)  11.4 us
    all_gather x1, blocking collectives, shards(): both = lax.all_gather(both, 'core', axis=0, tiled=True)  7.61 us
    ppermute x1, starting transfers between devices, shards(): far = lax.ppermute(near, 'zh', swap)  7.42 us
    ppermute x1, waiting for transfers between devices, shards(): weight_far = lax.ppermute(weight, 'y0', swap)  6.02 us
    all_gather x1, blocking collectives, shards(): near = lax.all_gather(kv, 'core', axis=0, tiled=True)  4.7 us
  transfers between devices with their start and end apart: 5, of which 3 were waited for; matrix products, arithmetic and copies ran while one was open for 0% of the time, Pallas kernels for 1%

profile of v15, /device:TPU:1, one launch (start us, length us, event | category | flops | bytes accessed | tf_op | source)
XLA Modules:
  0.0 113.8 jit_solution(3536660489734779576)
XLA Ops:
  0.0 1.6 %pack.1 = bf16[8,3,40,128]{3,2,1,0:T(8,128)(2,1)} custom-call(bf16[40,768]{1,0:T(8,128)(2,1)} %bitcast.17, bf16[40,768]{1,0:T(8,128)(2,1)} %bitcast.18, bf16[40,768]{1,0:T(8,128)(2,1)} %bitcast.19), custom_call_target="tpu_custom_call" | custom-call | tf_op jit(solution)/shard_map/pack/pallas_call | solution.py:171
  1.6 16.9 %all_to_all.25.packed_ref = bf16[8,3,40,128]{3,2,1,0:T(8,128)(2,1)S(1)} all-to-all(bf16[8,3,40,128]{3,2,1,0:T(8,128)(2,1)} %pack.1), channel_id=1, replica_groups=mesh['span'=4,'zh'=2,'y2'=2,'y1'=2,'y0'=2,'core'=2,'head'=4] {'y2','y1',..., dimensions={0} | all-to-all | bytes 491520 | tf_op jit(solution)/shard_map/exchange_heads/all_to_all | solution.py:181
  18.5 11.4 %collective-permute-start = (bf16[2,320,128]{2,1,0:T(8,128)(2,1)S(1)}, bf16[2,320,128]{2,1,0:T(8,128)(2,1)S(1)}, u32[]{:S(2)}, u32[]{:S(2)}) collective-permute-start(bf16[2,320,128]{2,1,0:T(8,128)(2,1)S(1)} %bitcast.12), channel_id=1, source_target_pairs={{0,64},{64,0},{1,65},{65,1},{2,66},{66,2},{3,67},{67,3},{4,68},{68... | collective-permute-start | bytes 491528 | tf_op jit(solution)/shard_map/gather_kv/ppermute | solution.py:184
  29.9 0.8 repeat_q.1
  30.7 4.0 %all-to-all-start.1 = ((bf16[4,320,128]{2,1,0:T(8,128)(2,1)}), bf16[4,320,128]{2,1,0:T(8,128)(2,1)S(1)}, u32[]{:S(2)}, u32[]{:S(2)}) async-start(bf16[4,320,128]{2,1,0:T(8,128)(2,1)} %bitcast.4), calls=%async_computation.1 | async-start | bytes 655360 | tf_op jit(solution)/shard_map/gather_q/all_to_all | solution.py:188
  34.7 4.7 %all_gather.9.near_ref = bf16[4,320,128]{2,1,0:T(8,128)(2,1)S(1)} all-gather(bf16[2,320,128]{2,1,0:T(8,128)(2,1)S(1)} %bitcast.13), channel_id=1, replica_groups=mesh['span'=4,'zh'=2,'y2'=2,'y1'=2,'y0'=2,'core'=2,'head'=4] {'core'}, dimensions={0}, use_global_device_ids=true | all-gather | bytes 491520 | tf_op jit(solution)/shard_map/gather_kv/all_gather | solution.py:190
  39.4 0.0 copy-start.3
  39.4 0.0 copy-start.4
  39.4 0.0 collective-permute-done
  39.4 2.2 %all_gather.10.far_ref = bf16[4,320,128]{2,1,0:T(8,128)(2,1)S(1)} all-gather(bf16[2,320,128]{2,1,0:T(8,128)(2,1)S(1)} %collective-permute-done), channel_id=1, replica_groups=mesh['span'=4,'zh'=2,'y2'=2,'y1'=2,'y0'=2,'core'=2,'head'=4] {'core'}, dimensions={0}, use_global_device_ids=true | all-gather | bytes 491520 | tf_op jit(solution)/shard_map/gather_kv/all_gather | solution.py:191
  41.6 0.0 all-to-all-done.1.q_ref
  41.6 0.0 copy-done.3
  41.6 0.0 copy-done.4
  41.6 4.1 %attend.1 = bf16[4,320,256]{2,1,0:T(8,128)(2,1)} custom-call(s32[4]{0:T(128)S(1)} %copy-done.3, s32[4]{0:T(128)S(1)} %copy-done.4, bf16[4,320,128]{2,1,0:T(8,128)(2,1)S(1)} %all-to-all-done.1.q_ref, bf16[4,320,128]{2,1,0:T(8,128)(2,1)S(1)} %all_gather.9.near_ref, bf16[4,320,128]{2,1,0:T(8,128)(2,1)S(1)} %all_gather.10.far_ref), custom_call_target="tpu_custom_call" | custom-call | tf_op jit(solution)/shard_map/attend/pallas_call | solution.py:195
  45.7 0.0 copy-start
  45.7 4.7 %all-to-all-start.2 = ((bf16[4,320,256]{2,1,0:T(8,128)(2,1)}), bf16[4,320,256]{2,1,0:T(8,128)(2,1)S(1)}, u32[]{:S(2)}, u32[]{:S(2)}) async-start(bf16[4,320,256]{2,1,0:T(8,128)(2,1)} %attend.1), calls=%async_computation.2 | async-start | bytes 1310720 | tf_op jit(solution)/shard_map/return_parts/all_to_all | solution.py:205
  50.4 0.0 copy-done
  50.4 2.2 %collective-permute-start.1 = (bf16[192,768]{1,0:T(8,128)(2,1)S(1)}, bf16[192,768]{1,0:T(8,128)(2,1)S(1)}, u32[]{:S(2)}, u32[]{:S(2)}) collective-permute-start(bf16[192,768]{1,0:T(8,128)(2,1)S(1)} %bitcast.14), channel_id=1, source_target_pairs={{0,8},{8,0},{1,9},{9,1},{2,10},{10,2},{3,11},{11,3},{4,12},{12,4},... | collective-permute-start | bytes 884744 | tf_op jit(solution)/shard_map/fetch_weight/ppermute | solution.py:194
  52.6 6.0 %collective-permute-done.1.far_ref = bf16[192,768]{1,0:T(8,128)(2,1)S(1)} collective-permute-done((bf16[192,768]{1,0:T(8,128)(2,1)S(1)}, bf16[192,768]{1,0:T(8,128)(2,1)S(1)}, u32[]{:S(2)}, u32[]{:S(2)}) %collective-permute-start.1) | collective-permute-done | bytes 294944 | tf_op jit(solution)/shard_map/fetch_weight/ppermute | solution.py:194
  58.6 0.3 all-to-all-done.2.parts_ref
  58.9 0.6 combine.1.near_ref
  59.4 7.4 %collective-permute-start.2 = (bf16[2,160,128]{2,1,0:T(8,128)(2,1)S(1)}, bf16[2,160,128]{2,1,0:T(8,128)(2,1)S(1)}, u32[]{:S(2)}, u32[]{:S(2)}) collective-permute-start(bf16[2,160,128]{2,1,0:T(8,128)(2,1)S(1)} %combine.1.near_ref), channel_id=1, source_target_pairs={{0,64},{64,0},{1,65},{65,1},{2,66},{66,2},{3,67},{67,3},{4,68},{68... | collective-permute-start | bytes 245768 | tf_op jit(solution)/shard_map/gather_attended/ppermute | solution.py:209
  66.9 1.9 %collective-permute-done.2.far_ref = bf16[2,160,128]{2,1,0:T(8,128)(2,1)S(1)} collective-permute-done((bf16[2,160,128]{2,1,0:T(8,128)(2,1)S(1)}, bf16[2,160,128]{2,1,0:T(8,128)(2,1)S(1)}, u32[]{:S(2)}, u32[]{:S(2)}) %collective-permute-start.2) | collective-permute-done | bytes 81952 | tf_op jit(solution)/shard_map/gather_attended/ppermute | solution.py:209
  68.8 0.1 spread.1
  68.9 18.2 %all_to_all.26 = bf16[8,2,160,128]{3,2,1,0:T(8,128)(2,1)S(1)} all-to-all(bf16[8,2,160,128]{3,2,1,0:T(8,128)(2,1)S(1)} %spread.1), channel_id=1, replica_groups=mesh['span'=4,'zh'=2,'y2'=2,'y1'=2,'y0'=2,'core'=2,'head'=4] {'y2','y1',..., dimensions={0} | all-to-all | bytes 1310720 | tf_op jit(solution)/shard_map/gather_attended/all_to_all | solution.py:211
  87.1 0.0 copy-start.2
  87.1 0.0 copy-start.5
  87.1 7.6 %all_gather.11.rows_ref = bf16[12,2,160,128]{3,2,1,0:T(8,128)(2,1)S(1)} all-gather(bf16[6,2,160,128]{3,2,1,0:T(8,128)(2,1)S(1)} %slice.4), channel_id=1, replica_groups=mesh['span'=4,'zh'=2,'y2'=2,'y1'=2,'y0'=2,'core'=2,'head'=4] {'core'}, dimensions={0}, use_global_device_ids=true | all-gather | bytes 1474560 | tf_op jit(solution)/shard_map/gather_attended/all_gather | solution.py:212
  94.7 0.0 copy-done.2
  94.7 0.0 copy-done.5
  94.7 1.5 %project.1 = (bf16[8,240,128]{2,1,0:T(8,128)(2,1)S(1)}, f32[1,192]{1,0:T(1,128)S(1)}) custom-call(s32[4]{0:T(128)S(1)} %copy-done.5, f32[4,192]{1,0:T(4,128)S(1)} %copy-done.2, bf16[12,2,160,128]{3,2,1,0:T(8,128)(2,1)S(1)} %all_gather.11.rows_ref, bf16[192,768]{1,0:T(8,128)(2,1)S(1)} %bitcast.15, bf16[192,768]{1,0:T(8,128)(2,1)S(1)} %collective-permute-done.1.far_ref), custom_call_target="tpu_custom_call" | custom-call | tf_op jit(solution)/shard_map/project/pallas_call | solution.py:214
  96.2 0.0 copy-start.1
  96.3 16.6 %all_to_all.27.pieces_ref = bf16[8,240,128]{2,1,0:T(8,128)(2,1)S(1)} all-to-all(bf16[8,240,128]{2,1,0:T(8,128)(2,1)S(1)} %get-tuple-element.19), channel_id=1, replica_groups=mesh['span'=4,'zh'=2,'y2'=2,'y1'=2,'y0'=2,'core'=2,'head'=4] {'head','y0'}, dimensions={0} | all-to-all | bytes 983040 | tf_op jit(solution)/shard_map/sum_heads/all_to_all | solution.py:226
  112.9 0.0 copy-done.1
  112.9 0.9 finish.1
  (2 shorter events, 0.0 us)
Async XLA Ops:
  18.5 20.9 %collective-permute-start = (bf16[2,320,128]{2,1,0:T(8,128)(2,1)S(1)}, bf16[2,320,128]{2,1,0:T(8,128)(2,1)S(1)}, u32[]{:S(2)}, u32[]{:S(2)}) collective-permute-start(bf16[2,320,128]{2,1,0:T(8,128)(2,1)S(1)} %bitcast.12), channel_id=1, source_target_pairs={{0,64},{64,0},{1,65},{65,1},{2,66},{66,2},{3,67},{67,3},{4,68},{68... | collective-permute-start | bytes 491528 | tf_op jit(solution)/shard_map/gather_kv/ppermute | solution.py:184
  30.7 10.9 %all-to-all-start.1 = ((bf16[4,320,128]{2,1,0:T(8,128)(2,1)}), bf16[4,320,128]{2,1,0:T(8,128)(2,1)S(1)}, u32[]{:S(2)}, u32[]{:S(2)}) async-start(bf16[4,320,128]{2,1,0:T(8,128)(2,1)} %bitcast.4), calls=%async_computation.1 | async-start | bytes 655360 | tf_op jit(solution)/shard_map/gather_q/all_to_all | solution.py:188
  39.4 2.2 %copy-start.3 = (s32[4]{0:T(128)S(1)}, s32[4]{0:T(128)}, u32[]{:S(2)}) copy-start(s32[4]{0:T(128)} %order_ref.1) | copy-start | bytes 52
  39.4 2.2 %copy-start.4 = (s32[4]{0:T(128)S(1)}, s32[4]{0:T(128)}, u32[]{:S(2)}) copy-start(s32[4]{0:T(128)} %valid_ref.1) | copy-start | bytes 52
  45.7 4.7 %copy-start = (bf16[768,192]{0,1:T(8,128)(2,1)S(1)}, bf16[768,192]{0,1:T(8,128)(2,1)}, u32[]{:S(2)}) copy-start(bf16[768,192]{0,1:T(8,128)(2,1)} %param.16) | copy-start | bytes 884740
  45.7 13.2 %all-to-all-start.2 = ((bf16[4,320,256]{2,1,0:T(8,128)(2,1)}), bf16[4,320,256]{2,1,0:T(8,128)(2,1)S(1)}, u32[]{:S(2)}, u32[]{:S(2)}) async-start(bf16[4,320,256]{2,1,0:T(8,128)(2,1)} %attend.1), calls=%async_computation.2 | async-start | bytes 1310720 | tf_op jit(solution)/shard_map/return_parts/all_to_all | solution.py:205
  50.4 8.2 %collective-permute-start.1 = (bf16[192,768]{1,0:T(8,128)(2,1)S(1)}, bf16[192,768]{1,0:T(8,128)(2,1)S(1)}, u32[]{:S(2)}, u32[]{:S(2)}) collective-permute-start(bf16[192,768]{1,0:T(8,128)(2,1)S(1)} %bitcast.14), channel_id=1, source_target_pairs={{0,8},{8,0},{1,9},{9,1},{2,10},{10,2},{3,11},{11,3},{4,12},{12,4},... | collective-permute-start | bytes 884744 | tf_op jit(solution)/shard_map/fetch_weight/ppermute | solution.py:194
  59.4 9.3 %collective-permute-start.2 = (bf16[2,160,128]{2,1,0:T(8,128)(2,1)S(1)}, bf16[2,160,128]{2,1,0:T(8,128)(2,1)S(1)}, u32[]{:S(2)}, u32[]{:S(2)}) collective-permute-start(bf16[2,160,128]{2,1,0:T(8,128)(2,1)S(1)} %combine.1.near_ref), channel_id=1, source_target_pairs={{0,64},{64,0},{1,65},{65,1},{2,66},{66,2},{3,67},{67,3},{4,68},{68... | collective-permute-start | bytes 245768 | tf_op jit(solution)/shard_map/gather_attended/ppermute | solution.py:209
  87.1 7.6 %copy-start.2 = (f32[4,192]{1,0:T(4,128)S(1)}, f32[4,192]{1,0:T(4,128)}, u32[]{:S(2)}) copy-start(f32[4,192]{1,0:T(4,128)} %gates_ref.1) | copy-start | bytes 9220
  87.1 7.6 %copy-start.5 = (s32[4]{0:T(128)S(1)}, s32[4]{0:T(128)}, u32[]{:S(2)}) copy-start(s32[4]{0:T(128)} %steps_ref.1) | copy-start | bytes 52
  96.2 16.6 %copy-start.1 = (bf16[1,320,192]{1,2,0:T(8,128)(2,1)S(1)}, bf16[1,320,192]{1,2,0:T(8,128)(2,1)}, u32[]{:S(2)}) copy-start(bf16[1,320,192]{1,2,0:T(8,128)(2,1)} %param.17) | copy-start | bytes 368644
